TPU v7x, 32 devices: a whole 2x2x4 slice. The times are simulated.
32 devices in a mesh: groups: 2 (over y), ctx: 4 (over z), mp: 4 (over x, core).
Axes of the slice: x: 2, y: 2, z: 4, core: 2. Of those that a mesh axis runs over, the one named last changes fastest.
Arguments:
- streams: bfloat16 [3, 2048, 4096], P(None, ('groups', 'ctx'), 'mp'), parts along dimension 1, may hold values from -6 to 6
- short_filter: float32 [3, 3, 4096], P(None, None, 'mp'), may hold values from -3 to 3
- mode_params: float32 [2, 4096, 8], P(None, 'mp'), may hold values from -2 to 2, as said below
- out_weight: bfloat16 [4096, 4096], P('mp', 'ctx'), may hold values from -0.09375 to 0.09375
- norm_gain: float32 [4096], P('mp'), may hold values from 0.5 to 1.5
- unembed: bfloat16 [4096, 512], P('mp'), may hold values from -40 to 40
- native: int32 [2048], P(('groups', 'ctx')), parts along dimension 0, may hold values from 0 to 511
- mut_pos: int32 [512], P('groups'), parts along dimension 0, may hold values from 0 to 1023
- mut_ids: int32 [512], P('groups'), parts along dimension 0, may hold values from 0 to 511
Outputs:
- loglik: float32 [2048], P(('groups', 'ctx')), parts along dimension 0
- scores: float32 [512], P('groups'), parts along dimension 0
There are 2 independent parts, one for each index of `groups`. A program takes and returns all parts, laid end to end along the dimension named above; an argument that names none is the same for every part. Nothing has to cross between parts.
Inputs may be any that keep to these rules, and one draw needn't show every extreme that they name: mode_params[0] holds positive decay rates, mode_params[1] residues.
All inputs are finite; a program needn't handle non-finite values.
Results may differ from a plain program's by a relative error of at most 0.0065.
Values may be sent and summed in bfloat16 or wider, within the bound.
No kernel may reach another device: no remote copies, remote signals or barrier semaphores. Data moves between devices by JAX's collectives and lax.ppermute only.
A program may use at most 192 MiB of HBM per device.

v0:
```python
import jax
import jax.numpy as jnp
from jax import lax
from jax.sharding import PartitionSpec as P

D = 4096


PRECISE = lax.Precision.HIGHEST


def from_behind(value, axis, steps):
    count = lax.axis_size(axis)
    initial, last = (max(0, -steps), min(count, count - steps))
    return lax.ppermute(value, axis, [(source, source + steps) for source in range(initial, last)])


def prefix(value, axis, join, neutral):
    count, mine = (lax.axis_size(axis), lax.axis_index(axis))
    pieces = jax.tree.map(lambda part: lax.all_gather(part, axis), value)
    so_far = jax.tree.map(
        lambda part, zero: jnp.full_like(part, 0) + jnp.asarray(zero, part.dtype), value, neutral
    )

    def hop(position, so_far):
        longer = join(so_far, jax.tree.map(lambda part: part[position], pieces))
        return jax.tree.map(lambda new, old: jnp.where(position < mine, new, old), longer, so_far)

    return lax.fori_loop(0, count - 1, hop, so_far)


def short_mix(padded, short_filter, seq_rows):
    return (
        short_filter[:, 0, None, :] * padded[:, 2:, :]
        + short_filter[:, 1, None, :] * padded[:, 1 : seq_rows + 1, :]
        + short_filter[:, 2, None, :] * padded[:, 0:seq_rows, :]
    )


def carry_terms(starts, decays, residue, span_len):
    lag_steps = jnp.arange(span_len, dtype=jnp.float32)
    weights = residue[None] * jnp.exp(-decays[None] * (lag_steps + 1.0)[:, None, None])
    return jnp.einsum("ncm,tcm->ntc", starts, weights, precision=PRECISE)


def span_conv(values, decays, residue, span_len):
    seq_all, channels = values.shape
    spans = seq_all // span_len
    lag_steps = jnp.arange(span_len, dtype=jnp.float32)
    powers = jnp.exp(-decays[None] * lag_steps[:, None, None])
    kernel = jnp.sum(residue[None] * powers, axis=2)
    offsets = jnp.arange(span_len, dtype=jnp.int32)
    spread = offsets[:, None] - offsets[None, :]
    toeplitz = jnp.where((spread >= 0)[:, :, None], kernel[jnp.clip(spread, 0, span_len - 1)], 0.0)
    blocked = values.reshape(spans, span_len, channels)
    inside = jnp.einsum("tsc,nsc->ntc", toeplitz, blocked, precision=PRECISE)
    tail_pows = jnp.exp(-decays[None] * (span_len - 1.0 - lag_steps)[:, None, None])
    own_states = jnp.einsum("nsc,scm->ncm", blocked, tail_pows, precision=PRECISE)
    factor = jnp.exp(-decays * span_len)

    def advance(carried, own_part):
        return (factor * carried + own_part, carried)

    end_state, starts = lax.scan(advance, jnp.zeros_like(factor), own_states)
    result = inside + carry_terms(starts, decays, residue, span_len)
    return (result.reshape(seq_all, channels), end_state)


def enter_terms(entering, decays, residue, spans, span_len):
    span_index = jnp.arange(spans, dtype=jnp.float32)
    starts = jnp.exp(-decays[None] * (span_index * span_len)[:, None, None]) * entering[None]
    added = carry_terms(starts, decays, residue, span_len)
    return added.reshape(spans * span_len, decays.shape[0])


def chain_pair(earlier, following):
    return (earlier[0] * following[0], following[0] * earlier[1] + following[1])


def body(
    streams, short_filter, mode_params, out_weight, norm_gain, unembed, native, mut_pos, mut_ids
):
    seq_rows = streams.shape[1]
    prior = from_behind(streams[:, seq_rows - 2 :, :], "ctx", 1)
    padded = jnp.concatenate([prior, streams], axis=1).astype(jnp.float32)
    mixed = short_mix(padded, short_filter, seq_rows)
    gate_bf = lax.optimization_barrier(mixed[0].astype(jnp.bfloat16))
    product = (mixed[1] * mixed[2]).astype(jnp.bfloat16)
    decays = mode_params[0]
    residue = mode_params[1]
    span_len = min(64, seq_rows)
    spans = seq_rows // span_len
    inside, own_end = span_conv(product.astype(jnp.float32), decays, residue, span_len)
    factor = jnp.exp(-decays * seq_rows)
    unused, entering = prefix(
        (factor, own_end), "ctx", chain_pair, (jnp.ones_like(factor), jnp.zeros_like(own_end))
    )
    conv_sum = inside + enter_terms(entering, decays, residue, spans, span_len)
    conv_bf = conv_sum.astype(jnp.bfloat16)
    conv_bf = lax.optimization_barrier(conv_bf)
    gated = (gate_bf.astype(jnp.float32) * conv_bf.astype(jnp.float32)).astype(jnp.bfloat16)
    terms = jnp.dot(
        gated,
        lax.all_gather(out_weight, "ctx", axis=1, tiled=True),
        preferred_element_type=jnp.float32,
    )
    output = lax.psum_scatter(terms, "mp", scatter_dimension=1, tiled=True)
    squares = lax.psum(jnp.sum(output * output, axis=1), "mp")
    normed = (output * lax.rsqrt(squares[:, None] / D + 1e-05) * norm_gain).astype(jnp.bfloat16)
    logit_terms = jnp.dot(normed, unembed, preferred_element_type=jnp.float32)
    local_pos = mut_pos - lax.axis_index("ctx") * seq_rows
    owned_mut = (local_pos >= 0) & (local_pos < seq_rows)
    slot_rows = jnp.clip(local_pos, 0, seq_rows - 1)
    logits = lax.psum(logit_terms, "mp")
    vocab_ids = jnp.arange(logits.shape[1], dtype=jnp.int32)
    totals = jax.nn.logsumexp(logits, axis=1)
    picked = jnp.sum(jnp.where(vocab_ids[None, :] == native[:, None], logits, 0.0), axis=1)
    chosen = jnp.sum(
        jnp.where(vocab_ids[None, :] == mut_ids[:, None], logits[slot_rows], 0.0), axis=1
    )
    loglik = picked - totals
    mut_terms = jnp.where(owned_mut, chosen - picked[slot_rows], 0.0)
    scores = lax.psum(mut_terms, "ctx")
    return (loglik, scores)


def solution(mesh):
    in_specs = (
        P(None, ("groups", "ctx"), "mp"),
        P(None, None, "mp"),
        P(None, "mp", None),
        P("mp", "ctx"),
        P("mp"),
        P("mp", None),
        P(("groups", "ctx")),
        P("groups"),
        P("groups"),
    )
    out_specs = (P(("groups", "ctx")), P("groups"))
    return jax.shard_map(body, mesh=mesh, in_specs=in_specs, out_specs=out_specs, check_vma=False)
```

profile of v0, /device:TPU:0, one launch (start us, length us, event | category | flops | bytes accessed | tf_op | source)
XLA Modules:
  0.0 301.2 jit_solution(9533523569857050880)
XLA Ops:
  8.0 0.8 slice.38
  8.8 5.0 %collective-permute-start = (bf16[3,2,1024]{2,1,0:T(2,128)(2,1)S(1)}, bf16[3,2,1024]{2,1,0:T(2,128)(2,1)S(1)}, u32[]{:S(2)}, u32[]{:S(2)}) collective-permute-start(bf16[3,2,1024]{2,1,0:T(2,128)(2,1)S(1)} %slice.38), channel_id=1, source_target_pairs={{0,4},{4,8},{8,12},{1,5},{5,9},{9,13},{2,6},{6,10},{10,14},{3,7},{... | collective-permute-start | bytes 36872 | tf_op jit(solution)/shard_map/ppermute | solution.py:15
  13.8 0.8 exponential_bitcast_fusion
  15.2 5.8 %multiply_reduce_fusion = f32[64,1024]{0,1:T(8,128)S(1)} fusion(f32[1024,8]{1,0:T(8,128)S(1)} %copy.32, f32[1024,8]{1,0:T(8,128)S(1)} %copy.31), kind=kLoop, calls=%fused_computation.18 | loop fusion | flops 1507328 | bytes 327680 | tf_op jit(solution)/shard_map/reduce_sum | solution.py:51
  21.0 20.9 %all_gather.13 = f32[4,1024,8]{1,2,0:T(8,128)S(1)} all-gather(f32[1,1024,8]{1,2,0:T(8,128)S(1)} %get-tuple-element.201), channel_id=1, replica_groups=mesh['groups'=2,'ctx'=4,'mp'=4] {'ctx'}, dimensions={0}, use_global_device_ids=true | all-gather | bytes 163840 | tf_op jit(solution)/shard_map/all_gather | solution.py:20
  42.1 18.4 %gather_fusion = f32[4096,1024]{1,0:T(8,128)} fusion(f32[64,1024]{1,0:T(8,128)S(1)} %copy.33, s32[4096]{0:T(1024)S(1)} %broadcast_clamp_fusion), kind=kCustom, calls=%fused_computation | custom fusion | bytes 33570816 | tf_op jit(solution)/shard_map/gather | solution.py:54
  60.6 30.5 %copy.34 = f32[64,64,1024]{1,0,2:T(8,128)} copy(f32[64,64,1024]{2,1,0:T(8,128)} %bitcast.58) | data formatting | bytes 33554432 | tf_op jit(solution)/shard_map/gather | solution.py:54
  91.1 1.9 maximum_convert_fusion
  93.0 0.9 fusion.10
  93.9 1.6 copy-done.2
  95.7 0.7 copy.35
  96.4 6.0 %fusion.26 = f32[4,1024,8]{2,0,1:T(4,128)} fusion(bf16[4,64,1024]{1,0,2:T(4,128)(2,1)S(1)} %copy.35, f32[64]{0:T(128)S(1)} %iota_subtract_fusion, f32[1024,8]{1,0:T(8,128)S(1)} %copy.32), kind=kOutput, calls=%fused_computation.38 | convolution fusion | flops 25690112 | bytes 688384 | tf_op jit(solution)/shard_map/nsc,scm->ncm/dot_general | solution.py:58
  102.4 1.9 copy.37
  104.3 2.5 while.27
  106.9 15.5 %all-gather = f32[4096,8]{0,1:T(8,128)S(1)} all-gather(f32[1024,8]{0,1:T(8,128)S(1)} %get-tuple-element.125), channel_id=2, replica_groups=mesh['groups'=2,'ctx'=4,'mp'=4] {'ctx'}, dimensions={0}, use_global_device_ids=true | all-gather | bytes 163840 | tf_op jit(solution)/shard_map/all_gather | solution.py:20
  122.5 1.0 copy.40
  123.5 2.5 copy.38
  126.0 10.4 %fusion.8 = f32[1024,64,4]{1,2,0:T(4,128)S(1)} fusion(f32[64]{0:T(128)S(1)} %iota_add_fusion, f32[1024,8]{1,0:T(8,128)S(1)} %copy.32, f32[1024,8]{1,0:T(8,128)S(1)} %copy-done.4, f32[1024,8]{1,0:T(8,128)} %copy.40, f32[4]{0:T(128)S(1)} %iota_multiply_fusion), kind=kOutput, calls=%fused_computation.16 | convolution fusion | flops 26279936 | bytes 1147152 | tf_op jit(solution)/shard_map/ncm,tcm->ntc/dot_general | solution.py:43
  136.5 9.8 %fusion.9 = f32[1024,64,4]{1,2,0:T(4,128)S(1)} fusion(f32[4,1024,8]{2,0,1:T(4,128)S(1)} %copy-done.5, f32[64]{0:T(128)S(1)} %iota_add_fusion, f32[1024,8]{1,0:T(8,128)S(1)} %copy.32, f32[1024,8]{1,0:T(8,128)S(1)} %copy-done.4), kind=kOutput, calls=%fused_computation.17 | convolution fusion | flops 26214400 | bytes 1245440 | tf_op jit(solution)/shard_map/ncm,tcm->ntc/dot_general | solution.py:43
  146.2 29.9 %fusion.12 = bf16[4,64,1024]{1,0,2:T(4,128)(2,1)S(1)} fusion(f32[1024,64,4]{1,2,0:T(4,128)S(1)} %fusion.8, f32[1024,64,4]{1,2,0:T(4,128)S(1)} %fusion.9, bf16[4,64,1024]{1,0,2:T(4,128)(2,1)S(1)} %copy.35, f32[64,64,1024]{1,0,2:T(8,128)} %copy.34, pred[64,64]{1,0:T(8,128)(4,1)S(1)} %subtract_compare_fusion), kind=kOutput, calls=%fused_computation.25 | convolution fusion | flops 206307328 | bytes 19927040 | tf_op jit(solution)/shard_map/tsc,nsc->ntc/dot_general | solution.py:56
  176.8 1.3 fusion.35
  178.1 7.6 %fusion.33 = f32[256,4096]{1,0:T(8,128)} fusion(bf16[1024,4096]{1,0:T(8,128)(2,1)} %all-gather.3.cloned.1.call-done, bf16[256,1024]{1,0:T(8,128)(2,1)S(1)} %bitcast.59, bf16[256,1024]{1,0:T(8,128)(2,1)S(1)} %fusion.35), kind=kOutput, calls=%fused_computation.49 | convolution fusion | flops 2148532224 | bytes 13631488 | tf_op jit(solution)/shard_map/dot_general | solution.py:102
  185.8 46.4 %reduce-scatter.2.cloned.1.call-done = f32[256,1024]{1,0:T(8,128)} async-done(((f32[256,4096]{1,0:T(8,128)}), f32[256,1024]{1,0:T(8,128)}) %reduce-scatter.2.cloned.1.call-update) | async-done | bytes 1048592 | tf_op jit(solution)/shard_map/reduce_scatter | solution.py:107
  232.2 1.4 multiply_reduce_fusion.1
  233.6 5.8 %psum.21 = f32[256]{0:T(256)S(1)} all-reduce(f32[256]{0:T(256)S(1)} %multiply_reduce_fusion.1), channel_id=1, replica_groups=mesh['groups'=2,'ctx'=4,'mp'=4] {'mp'}, use_global_device_ids=true, to_apply=%region_7.8 | all-reduce | flops 256 | bytes 2048 | tf_op jit(solution)/shard_map/psum | solution.py:108
  239.4 2.5 fusion.34
  242.0 34.1 %all-reduce.2.cloned.1.call-done = f32[256,512]{1,0:T(8,128)} async-done(((f32[256,512]{1,0:T(8,128)}), f32[256,512]{1,0:T(8,128)}) %all-reduce.2.cloned.1.call-update) | async-done | bytes 524304 | tf_op jit(solution)/shard_map/psum | solution.py:114
  276.1 1.2 reduce_max.9
  277.4 1.3 exponential_reduce_fusion
  278.7 1.9 gather_fusion.2
  280.7 1.0 gather_fusion.1
  281.9 12.2 %psum.23 = f32[256]{0:T(256)} all-reduce(f32[256]{0:T(256)S(1)} %and_select_fusion), channel_id=1, replica_groups=mesh['groups'=2,'ctx'=4,'mp'=4] {'ctx'}, use_global_device_ids=true, to_apply=%region_13.14 | all-reduce | flops 256 | bytes 2048 | tf_op jit(solution)/shard_map/psum | solution.py:123
  (66 shorter events, 5.8 us)
Async XLA Ops:
  7.2 232.2 %copy-start = (bf16[1024,512]{1,0:T(8,128)(2,1)S(1)}, bf16[1024,512]{1,0:T(8,128)(2,1)}, u32[]{:S(2)}) copy-start(bf16[1024,512]{1,0:T(8,128)(2,1)} %param.18) | copy-start | bytes 3145732
  7.2 7.9 %copy-start.6 = (f32[3,3,1024]{2,1,0:T(4,128)S(1)}, f32[3,3,1024]{2,1,0:T(4,128)}, u32[]{:S(2)}) copy-start(f32[3,3,1024]{2,1,0:T(4,128)} %param.14) | copy-start | bytes 110596
  7.2 170.9 %all-gather.3.cloned.1.call-start = ((), (), s32[]{:S(2)}) async-start(), calls=%async_computation.1 | async-start | bytes 10485760 | tf_op jit(solution)/shard_map/all_gather | solution.py:104
  7.9 224.3 %reduce-scatter.2.cloned.1.call-start = ((), (), s32[]{:S(2)}) async-start(), calls=%async_computation.2 | async-start | bytes 5242880 | tf_op jit(solution)/shard_map/reduce_scatter | solution.py:107
  8.8 82.3 %collective-permute-start = (bf16[3,2,1024]{2,1,0:T(2,128)(2,1)S(1)}, bf16[3,2,1024]{2,1,0:T(2,128)(2,1)S(1)}, u32[]{:S(2)}, u32[]{:S(2)}) collective-permute-start(bf16[3,2,1024]{2,1,0:T(2,128)(2,1)S(1)} %slice.38), channel_id=1, source_target_pairs={{0,4},{4,8},{8,12},{1,5},{5,9},{9,13},{2,6},{6,10},{10,14},{3,7},{... | collective-permute-start | bytes 36872 | tf_op jit(solution)/shard_map/ppermute | solution.py:15
  15.0 27.0 %copy-start.3 = (f32[1024,8]{1,0:T(8,128)}, f32[1024,8]{1,0:T(8,128)S(1)}, u32[]{:S(2)}) copy-start(f32[1024,8]{1,0:T(8,128)S(1)} %copy.31) | copy-start | bytes 98308
  93.9 1.6 copy-start.2
  102.4 23.6 %copy-start.4 = (f32[1024,8]{1,0:T(8,128)S(1)}, f32[1024,8]{1,0:T(8,128)}, u32[]{:S(2)}) copy-start(f32[1024,8]{1,0:T(8,128)} %copy-done.3) | copy-start | bytes 98308
  126.0 10.4 %copy-start.5 = (f32[4,1024,8]{2,0,1:T(4,128)S(1)}, f32[4,1024,8]{2,0,1:T(4,128)}, u32[]{:S(2)}) copy-start(f32[4,1024,8]{2,0,1:T(4,128)} %copy.38) | copy-start | bytes 393220
  185.7 53.7 %copy-start.7 = (f32[1024]{0:T(1024)S(1)}, f32[1024]{0:T(1024)}, u32[]{:S(2)}) copy-start(f32[1024]{0:T(1024)} %param.17) | copy-start | bytes 12292
  185.7 56.2 %copy-start.8 = (s32[256]{0:T(256)S(1)}, s32[256]{0:T(256)}, u32[]{:S(2)}) copy-start(s32[256]{0:T(256)} %param.20) | copy-start | bytes 3076
  185.8 91.6 %copy-start.9 = (s32[256]{0:T(256)S(1)}, s32[256]{0:T(256)}, u32[]{:S(2)}) copy-start(s32[256]{0:T(256)} %param.19) | copy-start | bytes 3076
  185.8 90.3 %all-reduce.2.cloned.1.call-start = ((), (), s32[]{:S(2)}) async-start(), calls=%async_computation.3 | async-start | bytes 1048576 | tf_op jit(solution)/shard_map/psum | solution.py:114
  276.1 4.6 %copy-start.1 = (f32[256,512]{1,0:T(8,128)S(1)}, f32[256,512]{1,0:T(8,128)}, u32[]{:S(2)}) copy-start(f32[256,512]{1,0:T(8,128)} %all-reduce.2.cloned.1.call-done) | copy-start | bytes 1572868
  277.4 4.3 %copy-start.10 = (s32[256]{0:T(256)S(1)}, s32[256]{0:T(256)}, u32[]{:S(2)}) copy-start(s32[256]{0:T(256)} %param.21) | copy-start | bytes 3076
Sparse Core Ops, SparseCore 0:
  9.6 156.0 all-gather.2
  185.9 46.3 reduce-scatter.1
  242.0 34.0 all-reduce.1
where the time goes:
time: 303 us; the launch traced here: 301 us
  waiting for transfers between devices  81.3 us (27%)
  matrix products  66.2 us (22%)
  local copies, waits for them, and re-layouts  63.1 us (21%)
  blocking collectives  54.4 us (18%)
  other arithmetic  16.9 us (6%)
  between operations  14.1 us (5%)
  starting transfers between devices  5.07 us (2%)
    gather x2, local copies, waits for them, and re-layouts, span_conv(): kernel[jnp.clip(spread, 0, span_len - 1)]  48.9 us
    reduce_scatter x1, waiting for transfers between devices, body(): output = lax.psum_scatter(terms, 'mp', scatter_dimension=1, tiled=True)  46.4 us
    all_gather x2, blocking collectives, prefix(): pieces = jax.tree.map(lambda part: lax.all_gather(part, axis), value)  36.4 us
    psum x1, waiting for transfers between devices, body(): logits = lax.psum(logit_terms, 'mp')  34.1 us
    dot_general x1, matrix products, span_conv(): inside = jnp.einsum('tsc,nsc->ntc', toeplitz, blocked, precision=PRECISE)  29.9 us
    dot_general x2, matrix products, carry_terms(): return jnp.einsum('ncm,tcm->ntc', starts, weights, precision=PRECISE)  20.2 us
    psum x1, blocking collectives, body(): scores = lax.psum(mut_terms, 'ctx')  12.2 us
    dot_general x1, matrix products, body(): jnp.dot(gated, lax.all_gather(out_weight, 'ctx', axis=1, tiled=True), pre...  7.64 us
  transfers between devices with their start and end apart: 4, of which 2 were waited for; matrix products, arithmetic and copies ran while one was open for 42% of the time, Pallas kernels for 0%

commit v1 on v0

v1 whole, which is shorter than its diff:
```python
import functools

import jax
import jax.numpy as jnp
from jax import lax
from jax.experimental import pallas as pl
from jax.experimental.pallas import tpu as pltpu
from jax.sharding import PartitionSpec as P

F32 = jnp.float32
BF16 = jnp.bfloat16
LANES = 128
SUBS = 8
EPS = 1e-05


def swap(value, axis, bit):
    count = lax.axis_size(axis)
    return lax.ppermute(value, axis, [(i, i ^ bit) for i in range(count)])


def rows_of(ref, start, size):
    return ref[pl.ds(pl.multiple_of(start, size), size), :]


def mix(taps, now, back1, back2):
    return taps[0] * now + taps[1] * back1 + taps[2] * back2


def rounded(value):
    return value.astype(BF16).astype(F32)


def taps_of(filt_ref, stream, cols):
    return [filt_ref[stream, j : j + 1, cols] for j in range(3)]


def local_kernel(steps, modes, x_ref, filt_ref, mode_ref, nat_ref, y_ref, gate_ref, start_ref, msg_ref, xs, gs):
    rows = steps * SUBS
    for tile in range(x_ref.shape[2] // LANES):
        cols = slice(tile * LANES, (tile + 1) * LANES)
        sub = lax.broadcasted_iota(jnp.int32, (SUBS, LANES), 0)
        for i in range(3):
            xs[i] = x_ref[i, :, cols].astype(F32)
        decay = [jnp.broadcast_to(mode_ref[0, m : m + 1, cols], (SUBS, LANES)) for m in range(modes)]
        res = [jnp.broadcast_to(mode_ref[1, m : m + 1, cols], (SUBS, LANES)) for m in range(modes)]
        fall = [jnp.exp(-d) for d in decay]
        taps = [taps_of(filt_ref, i, cols) for i in range(3)]

        def at(i, t):
            return xs[i, pl.ds(t, SUBS, stride=steps), :]

        def behind(value):
            return jnp.where(sub == 0, 0.0, pltpu.roll(value, 1, 0))

        back2 = [behind(at(i, steps - 2)) for i in range(3)]
        back1 = [behind(at(i, steps - 1)) for i in range(3)]
        state = [jnp.zeros((SUBS, LANES), F32) for _ in range(modes)]
        for t in range(steps):
            now = [at(i, t) for i in range(3)]
            mixed = [mix(taps[i], now[i], back1[i], back2[i]) for i in range(3)]
            back2, back1 = back1, now
            gs[pl.ds(t, SUBS, stride=steps), :] = mixed[0]
            prod = rounded(mixed[1] * mixed[2])
            if t < 2:
                prod = jnp.where(sub == 0, 0.0, prod)
            state = [f * s + prod for f, s in zip(fall, state)]
            y_ref[t * SUBS : (t + 1) * SUBS, cols] = functools.reduce(
                lambda p, q: p + q, [r * s for r, s in zip(res, state)]
            )
        gate_ref[:, cols] = gs[...].astype(BF16)
        ends = []
        for m in range(modes):
            total = state[m]
            for reach in (1, 2, 4):
                power = jnp.exp(-decay[m] * float(steps * reach))
                total = total + jnp.where(sub < reach, 0.0, power * pltpu.roll(total, reach, 0))
            start_ref[m * SUBS : (m + 1) * SUBS, cols] = behind(total)
            ends.append(total[SUBS - 1 : SUBS, :])
        end = jnp.concatenate(ends, axis=0)
        high = rounded(end)
        first = [xs[i, 0:2, :] for i in range(3)]
        last = [xs[i, rows - 2 : rows, :] for i in range(3)]
        edge = jnp.concatenate([first[1], first[2], last[1], last[2]], axis=0)
        other = jnp.concatenate(
            [last[0], first[0], nat_ref[0:1, cols], jnp.zeros((3, LANES), F32)], axis=0
        )
        msg_ref[:, cols] = jnp.concatenate([high, end - high, edge, other], axis=0).astype(BF16)


def local_part(streams, filt, modes_t, nat_row):
    rows, width = streams.shape[1:]
    modes = modes_t.shape[1]
    steps = rows // SUBS
    block = 2 * LANES
    msg_rows = 2 * modes + 16
    return pl.pallas_call(
        functools.partial(local_kernel, steps, modes),
        grid=(width // block,),
        in_specs=[
            pl.BlockSpec((3, rows, block), lambda c: (0, 0, c)),
            pl.BlockSpec((3, 3, block), lambda c: (0, 0, c)),
            pl.BlockSpec((2, modes, block), lambda c: (0, 0, c)),
            pl.BlockSpec((1, block), lambda c: (0, c)),
        ],
        out_specs=[
            pl.BlockSpec((rows, block), lambda c: (0, c)),
            pl.BlockSpec((rows, block), lambda c: (0, c)),
            pl.BlockSpec((modes * SUBS, block), lambda c: (0, c)),
            pl.BlockSpec((msg_rows, block), lambda c: (0, c)),
        ],
        out_shape=[
            jax.ShapeDtypeStruct((rows, width), F32),
            jax.ShapeDtypeStruct((rows, width), BF16),
            jax.ShapeDtypeStruct((modes * SUBS, width), F32),
            jax.ShapeDtypeStruct((msg_rows, width), BF16),
        ],
        scratch_shapes=[pltpu.VMEM((3, rows, LANES), F32), pltpu.VMEM((rows, LANES), F32)],
        compiler_params=pltpu.CompilerParams(vmem_limit_bytes=24 * 2**20),
        cost_estimate=pl.CostEstimate(flops=rows * width * 64, bytes_accessed=rows * width * 12, transcendentals=0),
        name="local_part",
    )(streams, filt, modes_t, nat_row)


def carry_kernel(steps, modes, stacked, count, where_ref, filt_ref, mode_ref, y_ref, gate_ref, start_ref, *rest):
    msg_refs, (out_ref, held, conv) = rest[:-3], rest[-3:]
    me = where_ref[0]
    rows = steps * SUBS
    base = 2 * modes
    for tile in range(y_ref.shape[1] // LANES):
        cols = slice(tile * LANES, (tile + 1) * LANES)
        sub = lax.broadcasted_iota(jnp.int32, (SUBS, LANES), 0)
        for k in range(count):
            if stacked:
                held[k] = msg_refs[0][k, :, cols].astype(F32)
            else:
                held[me ^ k] = msg_refs[k][:, cols].astype(F32)
        decay = mode_ref[0, :, cols]
        taps = [taps_of(filt_ref, i, cols) for i in range(3)]

        def firsts(own, prior, keep):
            pair = []
            for i, lane in ((1, 0), (2, 2)):
                f0 = own[base + lane : base + lane + 1, :]
                f1 = own[base + lane + 1 : base + lane + 2, :]
                l2 = jnp.where(keep, prior[base + lane + 4 : base + lane + 5, :], 0.0)
                l1 = jnp.where(keep, prior[base + lane + 5 : base + lane + 6, :], 0.0)
                pair.append((mix(taps[i], f0, l1, l2), mix(taps[i], f1, f0, l1)))
            return rounded(pair[0][0] * pair[1][0]), rounded(pair[0][1] * pair[1][1])

        full = jnp.exp(-decay * float(rows))
        near0 = jnp.exp(-decay * float(rows - 1))
        near1 = jnp.exp(-decay * float(rows - 2))

        def advance(b, entering):
            own = held[b]
            p0, p1 = firsts(own, held[jnp.maximum(b - 1, 0)], b > 0)
            end = own[0:modes, :] + own[modes : 2 * modes, :] + near0 * p0 + near1 * p1
            return jnp.where(b < me, full * entering + end, entering)

        entering = jnp.zeros((modes, LANES), F32)
        if count <= 8:
            for b in range(count - 1):
                entering = advance(b, entering)
        else:
            entering = lax.fori_loop(0, count - 1, advance, entering)
        own = held[me]
        prior = held[jnp.maximum(me - 1, 0)]
        p0, p1 = firsts(own, prior, me > 0)
        later = (
            jnp.exp(-decay * float(steps)) * entering
            + jnp.exp(-decay * float(steps - 1)) * p0
            + jnp.exp(-decay * float(steps - 2)) * p1
        )
        shift = float(steps) * jnp.maximum(sub - 1, 0).astype(F32)
        fall, res, flow = [], [], []
        for m in range(modes):
            d = jnp.broadcast_to(decay[m : m + 1, :], (SUBS, LANES))
            r = jnp.broadcast_to(mode_ref[1, m : m + 1, cols], (SUBS, LANES))
            fall.append(jnp.exp(-d))
            res.append(r)
            begin = jnp.where(sub == 0, entering[m : m + 1, :], jnp.exp(-d * shift) * later[m : m + 1, :])
            flow.append(r * (start_ref[m * SUBS : (m + 1) * SUBS, cols] + begin))
        inject = (p0, p1)
        for t in range(steps):
            flow = [f * v for f, v in zip(fall, flow)]
            if t < 2:
                extra = jnp.where(sub == 0, inject[t], 0.0)
                flow = [v + r * extra for v, r in zip(flow, res)]
            conv[pl.ds(t, SUBS, stride=steps), :] = functools.reduce(
                lambda p, q: p + q, flow, y_ref[t * SUBS : (t + 1) * SUBS, cols]
            )
        g0 = own[base + 10 : base + 11, :]
        g1 = own[base + 11 : base + 12, :]
        l2 = jnp.where(me > 0, prior[base + 8 : base + 9, :], 0.0)
        l1 = jnp.where(me > 0, prior[base + 9 : base + 10, :], 0.0)
        head0 = mix(taps[0], g0, l1, l2)
        head1 = mix(taps[0], g1, g0, l1)
        gate = gate_ref[:, cols].astype(F32)
        line = lax.broadcasted_iota(jnp.int32, (16, LANES), 0)
        head = jnp.where(line == 0, rounded(head0), jnp.where(line == 1, rounded(head1), gate[0:16, :]))
        out_ref[0:16, cols] = (head * rounded(conv[0:16, :])).astype(BF16)
        out_ref[16:rows, cols] = (gate[16:rows, :] * rounded(conv[16:rows, :])).astype(BF16)


def carry_part(me, filt, modes_t, y, gate, start, msgs, stacked):
    rows, width = y.shape
    modes = modes_t.shape[1]
    steps = rows // SUBS
    block = 2 * LANES
    count = msgs[0].shape[0] if stacked else len(msgs)
    msg_rows = msgs[0].shape[-2]
    if stacked:
        msg_specs = [pl.BlockSpec((count, msg_rows, block), lambda c, w: (0, 0, c))]
    else:
        msg_specs = [pl.BlockSpec((msg_rows, block), lambda c, w: (0, c))] * count
    return pl.pallas_call(
        functools.partial(carry_kernel, steps, modes, stacked, count),
        grid_spec=pltpu.PrefetchScalarGridSpec(
            num_scalar_prefetch=1,
            grid=(width // block,),
            in_specs=[
                pl.BlockSpec((3, 3, block), lambda c, w: (0, 0, c)),
                pl.BlockSpec((2, modes, block), lambda c, w: (0, 0, c)),
                pl.BlockSpec((rows, block), lambda c, w: (0, c)),
                pl.BlockSpec((rows, block), lambda c, w: (0, c)),
                pl.BlockSpec((modes * SUBS, block), lambda c, w: (0, c)),
            ]
            + msg_specs,
            out_specs=pl.BlockSpec((rows, block), lambda c, w: (0, c)),
            scratch_shapes=[pltpu.VMEM((count, msg_rows, LANES), F32), pltpu.VMEM((rows, LANES), F32)],
        ),
        out_shape=jax.ShapeDtypeStruct((rows, width), BF16),
        compiler_params=pltpu.CompilerParams(vmem_limit_bytes=24 * 2**20),
        cost_estimate=pl.CostEstimate(flops=rows * width * 32, bytes_accessed=rows * width * 8, transcendentals=0),
        name="carry_part",
    )(me, filt, modes_t, y, gate, start, *msgs)


def as_row(col, width):
    rows = col.shape[0]
    r = lax.broadcasted_iota(jnp.int32, (rows, width), 0)
    c = lax.broadcasted_iota(jnp.int32, (rows, width), 1)
    return jnp.sum(jnp.where(r == c, col, 0.0), axis=0, keepdims=True)


def exact_dot(onehot, values):
    high = values.astype(BF16)
    low = (values - high.astype(F32)).astype(BF16)
    return jnp.dot(onehot, high, preferred_element_type=F32) + jnp.dot(onehot, low, preferred_element_type=F32)


def logit_kernel(share, where_ref, un_ref, row_ref, id_ref, nat_ref, *rest):
    slots = where_ref.shape[0]
    slot_refs, (part_ref, square_ref, score_ref, acc) = rest[:slots], rest[slots:]
    for k in range(slots):
        acc[pl.ds(pl.multiple_of(where_ref[k] * share, share), share), :] = slot_refs[k][...]
    values = acc[...]
    total = values.shape[0]
    square_ref[...] = as_row(jnp.sum(values * values, axis=1, keepdims=True), total)
    part = jnp.dot(values.astype(BF16), un_ref[...], preferred_element_type=F32)
    part_ref[...] = part
    muts = row_ref.shape[0]
    vocab = part.shape[1]
    spots = lax.broadcasted_iota(jnp.int32, (muts, total), 1)
    picked = exact_dot((spots == row_ref[...]).astype(BF16), part)
    words = lax.broadcasted_iota(jnp.int32, (muts, vocab), 1)
    gain = jnp.where(words == id_ref[...], picked, 0.0) - jnp.where(words == nat_ref[...], picked, 0.0)
    score_ref[...] = as_row(jnp.sum(gain, axis=1, keepdims=True), muts)


def logit_part(where, slots, un, mut_row, mut_id, mut_nat):
    share, wide = slots[0].shape
    total = share * len(slots)
    vocab = un.shape[1]
    muts = mut_row.shape[0]
    whole = pl.BlockSpec(memory_space=pltpu.VMEM)
    return pl.pallas_call(
        functools.partial(logit_kernel, share),
        in_specs=[pl.BlockSpec(memory_space=pltpu.SMEM)] + [whole] * (4 + len(slots)),
        out_specs=[whole] * 3,
        out_shape=[
            jax.ShapeDtypeStruct((total, vocab), F32),
            jax.ShapeDtypeStruct((1, total), F32),
            jax.ShapeDtypeStruct((1, muts), F32),
        ],
        scratch_shapes=[pltpu.VMEM((total, wide), F32)],
        compiler_params=pltpu.CompilerParams(vmem_limit_bytes=40 * 2**20),
        name="logit_part",
    )(where, un, mut_row, mut_id, mut_nat, *slots)


def final_kernel(feats, where_ref, log_ref, square_ref, score_ref, nat_ref, row_ref, out_ref):
    me, piece = where_ref[0], where_ref[1]
    share, vocab = log_ref.shape
    total = square_ref.shape[1]
    muts = score_ref.shape[1]
    width = out_ref.shape[1]
    scale_row = lax.rsqrt(square_ref[...] / feats + EPS)
    r = lax.broadcasted_iota(jnp.int32, (share, total), 0)
    c = lax.broadcasted_iota(jnp.int32, (share, total), 1)
    scale = jnp.sum(jnp.where(c == r + me * share, scale_row, 0.0), axis=1, keepdims=True)
    logits = log_ref[...] * scale
    top = jnp.max(logits, axis=1, keepdims=True)
    norm = top + jnp.log(jnp.sum(jnp.exp(logits - top), axis=1, keepdims=True))
    words = lax.broadcasted_iota(jnp.int32, (share, vocab), 1)
    like = jnp.sum(jnp.where(words == nat_ref[...], logits, 0.0), axis=1, keepdims=True) - norm
    r = lax.broadcasted_iota(jnp.int32, (share, width), 0)
    c = lax.broadcasted_iota(jnp.int32, (share, width), 1)
    out_ref[0:1, :] = jnp.sum(jnp.where(c == r + piece * share, like, 0.0), axis=0, keepdims=True)
    r = lax.broadcasted_iota(jnp.int32, (muts, total), 0)
    c = lax.broadcasted_iota(jnp.int32, (muts, total), 1)
    at_mut = jnp.sum(jnp.where(c == row_ref[...], scale_row, 0.0), axis=1, keepdims=True)
    out_ref[1:2, 0:muts] = score_ref[...] * as_row(at_mut, muts)


def final_part(feats, where, logits, squares, scores, nat, mut_row, width):
    whole = pl.BlockSpec(memory_space=pltpu.VMEM)
    return pl.pallas_call(
        functools.partial(final_kernel, float(feats)),
        in_specs=[pl.BlockSpec(memory_space=pltpu.SMEM)] + [whole] * 5,
        out_specs=whole,
        out_shape=jax.ShapeDtypeStruct((2, width), F32),
        name="final_part",
    )(where, logits, squares, scores, nat, mut_row)


def spread_unembed(unembed, norm_gain, rows_wanted):
    count, shards = lax.axis_size("ctx"), lax.axis_size("mp")
    scaled = (unembed.astype(F32) * norm_gain[:, None]).astype(BF16)
    held = unembed.shape[0]
    z, m = lax.axis_index("ctx"), lax.axis_index("mp")
    if held % rows_wanted != 0:
        every = lax.all_gather(scaled, "mp", axis=0, tiled=True)
        return lax.dynamic_slice_in_dim(every, z * rows_wanted, rows_wanted, 0)
    ratio = held // rows_wanted
    owner = [i // ratio for i in range(count)]
    piece = lax.dynamic_slice_in_dim(scaled, (z % ratio) * rows_wanted, rows_wanted, 0)
    value = jnp.where(m == z // ratio, piece, jnp.zeros_like(piece))
    bit, holders = shards // 2, [0]
    while bit:
        pairs = [
            (i * shards + (owner[i] ^ h), i * shards + (owner[i] ^ h ^ bit)) for i in range(count) for h in holders
        ]
        value = value + lax.ppermute(value, ("ctx", "mp"), pairs)
        holders = holders + [h ^ bit for h in holders]
        bit //= 2
    return value


def split_half(value, upper):
    half = value.shape[0] // 2
    keep = lax.dynamic_slice_in_dim(value, upper * half, half, 0)
    send = lax.dynamic_slice_in_dim(value, (1 - upper) * half, half, 0)
    return keep, send


def project(gated, weight):
    shards = lax.axis_size("mp")
    m = lax.axis_index("mp")
    bit = 1
    value = None
    while bit < shards:
        upper = (m // bit) % 2
        keep, send = split_half(gated if value is None else value, upper)
        if value is None:
            sent = jnp.dot(send, weight, preferred_element_type=F32).astype(BF16)
            keep = jnp.dot(keep, weight, preferred_element_type=F32)
        else:
            sent = send.astype(BF16)
        value = keep + swap(sent, "mp", bit).astype(F32)
        bit *= 2
    return jnp.dot(gated, weight, preferred_element_type=F32) if value is None else value


def row_piece():
    shards = lax.axis_size("mp")
    m = lax.axis_index("mp")
    piece, bit = 0, 1
    while bit < shards:
        piece = piece * 2 + (m // bit) % 2
        bit *= 2
    return piece


def body(streams, short_filter, mode_params, out_weight, norm_gain, unembed, native, mut_pos, mut_ids):
    rows, width = streams.shape[1:]
    count, shards = lax.axis_size("ctx"), lax.axis_size("mp")
    z = lax.axis_index("ctx")
    quick = count == 4
    modes_t = jnp.swapaxes(mode_params, 1, 2)
    me = z.astype(jnp.int32)[None]
    high = native // 256
    nat_row = jnp.concatenate([high, native - high * 256]).astype(F32)
    nat_row = jnp.pad(nat_row, (0, width - 2 * rows))[None, :]
    y, gate, start, msg = local_part(streams, short_filter, modes_t, nat_row)
    nat_at = 2 * mode_params.shape[2] + 12
    if quick:
        msgs = [msg] + [swap(msg, "ctx", k) for k in range(1, count)]
        gated = carry_part(me, short_filter, modes_t, y, gate, start, msgs, False)
        nat_rows = jnp.stack([msgs[k][nat_at, : 2 * rows] for k in range(count)])
        nat_rows = nat_rows[z ^ jnp.arange(count)]
    else:
        every = lax.all_gather(msg, "ctx")
        gated = carry_part(me, short_filter, modes_t, y, gate, start, [every], True)
        nat_rows = every[:, nat_at, : 2 * rows]
    nat_rows = nat_rows.astype(jnp.int32)
    nat_all = (nat_rows[:, :rows] * 256 + nat_rows[:, rows:]).reshape(-1)

    un = spread_unembed(unembed, norm_gain, out_weight.shape[1])
    piece = row_piece()
    share = rows // shards
    block, inner = mut_pos // rows, mut_pos % rows
    mut_row = jnp.where(inner // share == piece, block * share + inner % share, -1)[:, None]
    mut_nat = nat_all[mut_pos][:, None]

    if quick:
        middle = [(1, 2), (2, 1)]
        beside = swap(gated, "ctx", 1)
        mid_a = lax.ppermute(gated, "ctx", middle)
        mid_b = lax.ppermute(beside, "ctx", middle)
        far_a = swap(mid_a, "ctx", 1)
        far_b = swap(mid_b, "ctx", 1)
        blocks = [gated, beside, mid_a + far_a, mid_b + far_b]
        low = z < 2
        where = jnp.stack([z, z ^ 1, jnp.where(low, 2, 1), jnp.where(low, 3, 0)]).astype(jnp.int32)
    else:
        every = lax.all_gather(gated, "ctx")
        blocks = [every[b] for b in range(count)]
        where = jnp.arange(count, dtype=jnp.int32)
    slots = [project(part, out_weight) for part in blocks]
    part, squares, scores = logit_part(where, slots, un, mut_row, mut_ids[:, None], mut_nat)

    if quick:
        vocab = part.shape[1]
        own = lax.dynamic_slice_in_dim(part, z * share, share, 0)

        def wide(value):
            first = value.astype(BF16)
            second = (value - first.astype(F32)).astype(BF16)
            both = jnp.concatenate([first, second], axis=0)
            return jnp.pad(both, ((0, 0), (0, vocab - both.shape[1])))

        extra = jnp.concatenate([wide(squares), wide(scores)], axis=0)
        logits = own
        for k in range(1, count):
            theirs = lax.dynamic_slice_in_dim(part, (z ^ k) * share, share, 0).astype(BF16)
            got = swap(jnp.concatenate([theirs, extra], axis=0), "ctx", k).astype(F32)
            logits = logits + got[:share]
            squares = squares + (got[share : share + 1] + got[share + 1 : share + 2])[:, : squares.shape[1]]
            scores = scores + (got[share + 2 : share + 3] + got[share + 3 : share + 4])[:, : scores.shape[1]]
    else:
        logits = lax.psum_scatter(part, "ctx", scatter_dimension=0, tiled=True)
        squares = lax.psum(squares, "ctx")
        scores = lax.psum(scores, "ctx")

    own_nat = lax.dynamic_slice_in_dim(native, piece * share, share, 0)[:, None]
    spot = jnp.stack([z, piece]).astype(jnp.int32)
    feats = norm_gain.shape[0] * shards
    span = max(rows, mut_pos.shape[0])
    result = final_part(feats, spot, logits, squares, scores, own_nat, mut_row, span)
    total = result
    for k in range(1, shards):
        total = total + swap(result, "mp", k)
    return total[0, :rows], total[1, : mut_pos.shape[0]]


def solution(mesh):
    in_specs = (
        P(None, ("groups", "ctx"), "mp"),
        P(None, None, "mp"),
        P(None, "mp", None),
        P("mp", "ctx"),
        P("mp"),
        P("mp", None),
        P(("groups", "ctx")),
        P("groups"),
        P("groups"),
    )
    out_specs = (P(("groups", "ctx")), P("groups"))
    return jax.shard_map(body, mesh=mesh, in_specs=in_specs, out_specs=out_specs, check_vma=False)
```

time: 303 us -> 111 us (0.37)
  matrix products: 66.2 us -> 6.18 us
  blocking collectives: 54.4 us -> 0 us
  waiting for transfers between devices: 81.3 us -> 30.7 us
  local copies, waits for them, and re-layouts: 63.1 us -> 15.3 us
  starting transfers between devices: 5.07 us -> 37.4 us
  between operations: 14.1 us -> 1.29 us
  Pallas kernels: 0 us -> 9.12 us
  other arithmetic: 16.9 us -> 10.2 us
    dot_general x6 -> x8, matrix products: 66.2 us -> 6.18 us  [the longest x4 3.43 us: project(): sent = jnp.dot(send, weight, preferred_element_type=F32).astype(BF16)]
    gather x4 -> x2, local copies, waits for them, and re-layouts: 51.9 us -> 1.93 us  [the longest x1 1.37 us: body(): mut_nat = nat_all[mut_pos][:, None]]
    reduce_scatter x1 -> x0, waiting for transfers between devices: 46.4 us -> none  [body(): output = lax.psum_scatter(terms, 'mp', scatter_dimension=1, tiled=True)]
    all_gather x2 -> x0, blocking collectives: 36.4 us -> none  [prefix(): pieces = jax.tree.map(lambda part: lax.all_gather(part, axis), value)]
    psum x1 -> x0, waiting for transfers between devices: 34.1 us -> none  [body(): logits = lax.psum(logit_terms, 'mp')]
    ppermute x1 -> x24, starting transfers between devices: 4.96 us -> 37.4 us  [the longest x20 29.1 us: swap(): return lax.ppermute(value, axis, [(i, i ^ bit) for i in range(count)])]
    ppermute x1 -> x24, waiting for transfers between devices: 0.01 us -> 30.7 us  [the longest x20 30.7 us: swap(): return lax.ppermute(value, axis, [(i, i ^ bit) for i in range(count)])]
    psum x2 -> x0, blocking collectives: 18 us -> none  [the longest x1 12.2 us: body(): scores = lax.psum(mut_terms, 'ctx')]
  transfers between devices with their start and end apart: 4 -> 24, of which waited for: 2 -> 9; matrix products, arithmetic and copies ran while one was open for 42% -> 14% of each run, Pallas kernels for 0% -> 2%
where the time goes in v1:
time: 111 us; the launch traced here: 110 us
  starting transfers between devices  37.4 us (34%)
  waiting for transfers between devices  30.7 us (28%)
  local copies, waits for them, and re-layouts  15.3 us (14%)
  other arithmetic  10.2 us (9%)
  Pallas kernels  9.12 us (8%)
  matrix products  6.18 us (6%)
  between operations  1.29 us (1%)
    ppermute x20, waiting for transfers between devices, swap(): return lax.ppermute(value, axis, [(i, i ^ bit) for i in range(count)])  30.7 us
    ppermute x20, starting transfers between devices, swap(): return lax.ppermute(value, axis, [(i, i ^ bit) for i in range(count)])  29.1 us
    unnamed x47, local copies, waits for them, and re-layouts  11.4 us
    ppermute x2, starting transfers between devices, spread_unembed(): value = value + lax.ppermute(value, ('ctx', 'mp'), pairs)  5.94 us
    pallas_call x1, Pallas kernels, local_part(): pl.pallas_call(functools.partial(local_kernel, steps, modes), grid=(width...  4.01 us
    dot_general x4, matrix products, project(): sent = jnp.dot(send, weight, preferred_element_type=F32).astype(BF16)  3.43 us
    dot_general x4, matrix products, project(): keep = jnp.dot(keep, weight, preferred_element_type=F32)  2.75 us
    select_n x1, other arithmetic, spread_unembed(): value = jnp.where(m == z // ratio, piece, jnp.zeros_like(piece))  2.55 us
  transfers between devices with their start and end apart: 24, of which 9 were waited for; matrix products, arithmetic and copies ran while one was open for 14% of the time, Pallas kernels for 2%

profile of v1, /device:TPU:0, one launch (start us, length us, event | category | flops | bytes accessed | tf_op | source)
XLA Modules:
  0.0 110.2 jit_solution(3803341511327634766)
XLA Ops:
  1.6 1.4 %copy-done.1 = bf16[3,256,1024]{2,1,0:T(8,128)(2,1)S(1)} copy-done((bf16[3,256,1024]{2,1,0:T(8,128)(2,1)S(1)}, bf16[3,256,1024]{2,1,0:T(8,128)(2,1)}, u32[]{:S(2)}) %copy-start.1) | copy-done | bytes 1572888
  4.6 4.0 %local_part.1 = (f32[256,1024]{1,0:T(8,128)S(1)}, bf16[256,1024]{1,0:T(8,128)(2,1)S(1)}, f32[64,1024]{1,0:T(8,128)S(1)}, bf16[32,1024]{1,0:T(8,128)(2,1)S(1)}) custom-call(bf16[3,256,1024]{2,1,0:T(8,128)(2,1)S(1)} %copy-done.1, f32[3,3,1024]{2,1,0:T(4,128)S(1)} %copy-done.9, f32[2,8,1024]{2,1,0:T(8,128)S(1)} %bitcast.27, f32[1,1024]{1,0:T(1,128)S(1)} %bitcast.29), custom_call_target="tpu_custom_call" | custom-call | flops 16777216 | bytes 3145728 | tf_op jit(solution)/shard_map/local_part/pallas_call | solution.py:97
  9.6 3.1 %collective-permute-start.2 = (bf16[32,1024]{1,0:T(8,128)(2,1)S(1)}, bf16[32,1024]{1,0:T(8,128)(2,1)S(1)}, u32[]{:S(2)}, u32[]{:S(2)}) collective-permute-start(bf16[32,1024]{1,0:T(8,128)(2,1)S(1)} %get-tuple-element.9.rest_0_), channel_id=1, source_target_pairs={{0,4},{4,0},{8,12},{12,8},{1,5},{5,1},{9,13},{13,9},{2,6},{6,2},{1... | collective-permute-start | bytes 196616 | tf_op jit(solution)/shard_map/ppermute | solution.py:19
  12.7 2.6 %collective-permute-start.3 = (bf16[32,1024]{1,0:T(8,128)(2,1)S(1)}, bf16[32,1024]{1,0:T(8,128)(2,1)S(1)}, u32[]{:S(2)}, u32[]{:S(2)}) collective-permute-start(bf16[32,1024]{1,0:T(8,128)(2,1)S(1)} %get-tuple-element.9.rest_0_), channel_id=1, source_target_pairs={{0,8},{4,12},{8,0},{12,4},{1,9},{5,13},{9,1},{13,5},{2,10},{6,14},... | collective-permute-start | bytes 196616 | tf_op jit(solution)/shard_map/ppermute | solution.py:19
  15.3 2.5 %fusion = bf16[1024,512]{1,0:T(8,128)(2,1)} fusion(bf16[1024,512]{1,0:T(8,128)(2,1)} %param.14, f32[1024]{0:T(1024)} %param.13, pred[]{:T(512)S(6)} %eq.24), kind=kLoop, calls=%fused_computation.11 | loop fusion | flops 2097152 | bytes 2101249 | tf_op jit(solution)/shard_map/jit(_where)/select_n | solution.py:339
  17.8 4.6 %collective-permute-start = (bf16[1024,512]{1,0:T(8,128)(2,1)}, bf16[1024,512]{1,0:T(8,128)(2,1)}, u32[]{:S(2)}, u32[]{:S(2)}) collective-permute-start(bf16[1024,512]{1,0:T(8,128)(2,1)} %fusion), channel_id=1, source_target_pairs={{0,2},{5,7},{10,8},{15,13},{16,18},{21,23},{26,24},{31,29}} | collective-permute-start | bytes 3145736 | tf_op jit(solution)/shard_map/ppermute | solution.py:345
  25.6 1.2 %copy-done.4 = f32[256,1024]{1,0:T(8,128)S(1)} copy-done((f32[256,1024]{1,0:T(8,128)S(1)}, f32[256,1024]{1,0:T(8,128)}, u32[]{:S(2)}) %copy-start.4) | copy-done | bytes 1048600
  31.1 1.7 %carry_part.1 = bf16[256,1024]{1,0:T(8,128)(2,1)S(1)} custom-call(s32[1]{0:T(128)} %bitcast.where_ref, f32[3,3,1024]{2,1,0:T(4,128)S(1)} %copy-done.10, f32[2,8,1024]{2,1,0:T(8,128)S(1)} %bitcast.28, f32[256,1024]{1,0:T(8,128)S(1)} %copy-done.4, bf16[256,1024]{1,0:T(8,128)(2,1)S(1)} %get-tuple-element.11.gate_ref, f32[64,1024]{1,0:T(8,128)S(1)} %copy-done.6, ...), custom_call_target="tpu_custom_call" | custom-call | flops 8388608 | bytes 2097152 | tf_op jit(solution)/shard_map/carry_part/pallas_call | solution.py:217
  32.9 1.5 %collective-permute-start.10 = (bf16[256,1024]{1,0:T(8,128)(2,1)S(1)}, bf16[256,1024]{1,0:T(8,128)(2,1)}, u32[]{:S(2)}, u32[]{:S(2)}) collective-permute-start(bf16[256,1024]{1,0:T(8,128)(2,1)S(1)} %carry_part.1), channel_id=1, source_target_pairs={{4,8},{8,4},{5,9},{9,5},{6,10},{10,6},{7,11},{11,7},{20,24},{24,20... | collective-permute-start | bytes 1572872 | tf_op jit(solution)/shard_map/ppermute | solution.py:420
  34.4 1.1 %convolution_convert_fusion.3 = bf16[128,1024]{1,0:T(8,128)(2,1)} fusion(bf16[1024,1024]{1,0:T(8,128)(2,1)S(1)} %copy-done, bf16[256,1024]{1,0:T(8,128)(2,1)S(1)} %carry_part.1, s32[]{:T(128)S(6)} %select_n.155), kind=kOutput, calls=%fused_computation.10 | convolution fusion | flops 268566528 | bytes 2621444 | tf_op jit(solution)/shard_map/dot_general | solution.py:367
  36.2 1.4 %gather_fusion.1 = s32[256]{0:T(256)S(1)} fusion(s32[1024]{0:T(1024)S(1)} %bitcast.30, s32[1024]{0:T(1024)S(1)} %pad_clamp_fusion), kind=kCustom, calls=%fused_computation.1 | custom fusion | bytes 3072 | tf_op jit(solution)/shard_map/gather | solution.py:415
  37.7 6.8 %collective-permute-done.7 = bf16[256,1024]{1,0:T(8,128)(2,1)} collective-permute-done((bf16[256,1024]{1,0:T(8,128)(2,1)S(1)}, bf16[256,1024]{1,0:T(8,128)(2,1)}, u32[]{:S(2)}, u32[]{:S(2)}) %collective-permute-start.7) | collective-permute-done | bytes 524320 | tf_op jit(solution)/shard_map/ppermute | solution.py:19
  44.5 1.4 %convolution_convert_fusion.2 = bf16[128,1024]{1,0:T(8,128)(2,1)S(1)} fusion(bf16[1024,1024]{1,0:T(8,128)(2,1)S(1)} %copy-done, bf16[256,1024]{1,0:T(8,128)(2,1)} %collective-permute-done.7, s32[]{:T(128)S(6)} %select_n.155), kind=kOutput, calls=%fused_computation.9 | convolution fusion | flops 268566528 | bytes 2621444 | tf_op jit(solution)/shard_map/dot_general | solution.py:367
  47.6 1.4 %convolution_add_fusion.2 = f32[128,1024]{1,0:T(8,128)S(1)} fusion(bf16[1024,1024]{1,0:T(8,128)(2,1)S(1)} %copy-done, bf16[128,1024]{1,0:T(8,128)(2,1)S(1)} %collective-permute-done.8, bf16[256,1024]{1,0:T(8,128)(2,1)} %collective-permute-done.7, s32[]{:T(128)S(6)} %select_n.154), kind=kOutput, calls=%fused_computation.5 | convolution fusion | flops 268697600 | bytes 3145732 | tf_op jit(solution)/shard_map/dot_general | solution.py:368
  49.0 1.8 %collective-permute-start.9 = (bf16[64,1024]{1,0:T(8,128)(2,1)S(1)}, bf16[64,1024]{1,0:T(8,128)(2,1)S(1)}, u32[]{:S(2)}, u32[]{:S(2)}) collective-permute-start(bf16[64,1024]{1,0:T(8,128)(2,1)S(1)} %dynamic-slice_convert_fusion.2), channel_id=1, source_target_pairs={{0,2},{1,3},{2,0},{3,1},{4,6},{5,7},{6,4},{7,5},{8,10},{9,11},{10,... | collective-permute-start | bytes 393224 | tf_op jit(solution)/shard_map/ppermute | solution.py:19
  50.8 2.1 %collective-permute-done.6 = bf16[64,1024]{1,0:T(8,128)(2,1)S(1)} collective-permute-done((bf16[64,1024]{1,0:T(8,128)(2,1)S(1)}, bf16[64,1024]{1,0:T(8,128)(2,1)S(1)}, u32[]{:S(2)}, u32[]{:S(2)}) %collective-permute-start.6) | collective-permute-done | bytes 131104 | tf_op jit(solution)/shard_map/ppermute | solution.py:19
  52.9 1.9 %collective-permute-start.11 = (bf16[256,1024]{1,0:T(8,128)(2,1)}, bf16[256,1024]{1,0:T(8,128)(2,1)S(1)}, u32[]{:S(2)}, u32[]{:S(2)}) collective-permute-start(bf16[256,1024]{1,0:T(8,128)(2,1)} %collective-permute-done.10), channel_id=1, source_target_pairs={{0,4},{4,0},{8,12},{12,8},{1,5},{5,1},{9,13},{13,9},{2,6},{6,2},{1... | collective-permute-start | bytes 1572872 | tf_op jit(solution)/shard_map/ppermute | solution.py:19
  55.3 10.3 %collective-permute-start.15 = (bf16[256,1024]{1,0:T(8,128)(2,1)S(1)}, bf16[256,1024]{1,0:T(8,128)(2,1)S(1)}, u32[]{:S(2)}, u32[]{:S(2)}) collective-permute-start(bf16[256,1024]{1,0:T(8,128)(2,1)S(1)} %collective-permute-done.14), channel_id=1, source_target_pairs={{0,4},{4,0},{8,12},{12,8},{1,5},{5,1},{9,13},{13,9},{2,6},{6,2},{1... | collective-permute-start | bytes 1572872 | tf_op jit(solution)/shard_map/ppermute | solution.py:19
  65.6 1.7 %fusion.46 = bf16[1024,512]{1,0:T(8,128)(2,1)S(1)} fusion(bf16[1024,512]{1,0:T(8,128)(2,1)} %collective-permute-done, f32[1024]{0:T(1024)S(1)} %copy-done.20, bf16[1024,512]{1,0:T(8,128)(2,1)S(1)} %copy-done.19, pred[]{:T(512)S(6)} %eq.24), kind=kLoop, calls=%fused_computation.106 | loop fusion | flops 2621440 | bytes 3149825 | tf_op jit(solution)/shard_map/add | solution.py:345
  67.2 1.4 %collective-permute-start.1 = (bf16[1024,512]{1,0:T(8,128)(2,1)S(1)}, bf16[1024,512]{1,0:T(8,128)(2,1)S(1)}, u32[]{:S(2)}, u32[]{:S(2)}) collective-permute-start(bf16[1024,512]{1,0:T(8,128)(2,1)S(1)} %fusion.46), channel_id=1, source_target_pairs={{0,1},{2,3},{5,4},{7,6},{10,11},{8,9},{15,14},{13,12},{16,17},{18,... | collective-permute-start | bytes 3145736 | tf_op jit(solution)/shard_map/ppermute | solution.py:345
  68.6 1.2 %add.213 = bf16[256,1024]{1,0:T(8,128)(2,1)S(1)} add(bf16[256,1024]{1,0:T(8,128)(2,1)} %collective-permute-done.10, bf16[256,1024]{1,0:T(8,128)(2,1)S(1)} %collective-permute-done.11) | non-fusion elementwise | flops 262144 | bytes 1572864 | tf_op jit(solution)/shard_map/add | solution.py:424
  70.4 8.0 %collective-permute-done.15 = bf16[256,1024]{1,0:T(8,128)(2,1)S(1)} collective-permute-done((bf16[256,1024]{1,0:T(8,128)(2,1)S(1)}, bf16[256,1024]{1,0:T(8,128)(2,1)S(1)}, u32[]{:S(2)}, u32[]{:S(2)}) %collective-permute-start.15) | collective-permute-done | bytes 524320 | tf_op jit(solution)/shard_map/ppermute | solution.py:19
  79.6 1.7 %collective-permute-start.13 = (bf16[64,1024]{1,0:T(8,128)(2,1)S(1)}, bf16[64,1024]{1,0:T(8,128)(2,1)S(1)}, u32[]{:S(2)}, u32[]{:S(2)}) collective-permute-start(bf16[64,1024]{1,0:T(8,128)(2,1)S(1)} %dynamic-slice_convert_fusion.1), channel_id=1, source_target_pairs={{0,2},{1,3},{2,0},{3,1},{4,6},{5,7},{6,4},{7,5},{8,10},{9,11},{10,... | collective-permute-start | bytes 393224 | tf_op jit(solution)/shard_map/ppermute | solution.py:19
  82.8 3.3 %collective-permute-done.13 = bf16[64,1024]{1,0:T(8,128)(2,1)S(1)} collective-permute-done((bf16[64,1024]{1,0:T(8,128)(2,1)S(1)}, bf16[64,1024]{1,0:T(8,128)(2,1)S(1)}, u32[]{:S(2)}, u32[]{:S(2)}) %collective-permute-start.13) | collective-permute-done | bytes 131104 | tf_op jit(solution)/shard_map/ppermute | solution.py:19
  86.0 2.3 %collective-permute-done.17 = bf16[64,1024]{1,0:T(8,128)(2,1)S(1)} collective-permute-done((bf16[64,1024]{1,0:T(8,128)(2,1)S(1)}, bf16[64,1024]{1,0:T(8,128)(2,1)S(1)}, u32[]{:S(2)}, u32[]{:S(2)}) %collective-permute-start.17) | collective-permute-done | bytes 131104 | tf_op jit(solution)/shard_map/ppermute | solution.py:19
  88.7 1.5 %logit_part.1 = (f32[256,512]{1,0:T(8,128)S(1)}, f32[1,256]{1,0:T(1,128)S(1)}, f32[1,256]{1,0:T(1,128)S(1)}) custom-call(s32[4]{0:T(128)S(1)} %pad_add_fusion.1.where_ref, bf16[1024,512]{1,0:T(8,128)(2,1)S(1)} %add.197.un_ref, s32[256,1]{1,0:T(8,128)S(1)} %copy.12.row_ref, s32[256,1]{1,0:T(8,128)S(1)} %copy.13.id_ref, s32[256,1]{1,0:T(8,128)S(1)} %copy.14.nat_ref, ...), custom_call_target="tpu_custom_call" | custom-call | tf_op jit(solution)/shard_map/logit_part/pallas_call | solution.py:278
  90.3 1.8 %collective-permute-start.18 = (bf16[68,512]{1,0:T(8,128)(2,1)S(1)}, bf16[68,512]{1,0:T(8,128)(2,1)S(1)}, u32[]{:S(2)}, u32[]{:S(2)}) collective-permute-start(bf16[68,512]{1,0:T(8,128)(2,1)S(1)} %get-tuple-element.33), channel_id=1, source_target_pairs={{0,4},{4,0},{8,12},{12,8},{1,5},{5,1},{9,13},{13,9},{2,6},{6,2},{1... | collective-permute-start | bytes 208904 | tf_op jit(solution)/shard_map/ppermute | solution.py:19
  92.1 1.7 %collective-permute-start.19 = (bf16[68,512]{1,0:T(8,128)(2,1)S(1)}, bf16[68,512]{1,0:T(8,128)(2,1)S(1)}, u32[]{:S(2)}, u32[]{:S(2)}) collective-permute-start(bf16[68,512]{1,0:T(8,128)(2,1)S(1)} %get-tuple-element.34), channel_id=1, source_target_pairs={{0,8},{4,12},{8,0},{12,4},{1,9},{5,13},{9,1},{13,5},{2,10},{6,14},... | collective-permute-start | bytes 208904 | tf_op jit(solution)/shard_map/ppermute | solution.py:19
  95.4 4.9 %collective-permute-done.19 = bf16[68,512]{1,0:T(8,128)(2,1)S(1)} collective-permute-done((bf16[68,512]{1,0:T(8,128)(2,1)S(1)}, bf16[68,512]{1,0:T(8,128)(2,1)S(1)}, u32[]{:S(2)}, u32[]{:S(2)}) %collective-permute-start.19) | collective-permute-done | bytes 69664 | tf_op jit(solution)/shard_map/ppermute | solution.py:19
  102.2 1.9 %final_part.1 = f32[2,256]{1,0:T(2,128)} custom-call(s32[2]{0:T(128)} %pad_add_fusion.where_ref, f32[64,512]{1,0:T(8,128)} %slice_add_fusion.log_ref, f32[1,256]{1,0:T(1,128)} %fusion.28.square_ref, f32[1,256]{1,0:T(1,128)} %fusion.25.score_ref, s32[64,1]{1,0:T(8,128)} %copy.15.nat_ref, s32[256,1]{1,0:T(8,128)} %copy-done.2), custom_call_target="tpu_custom_call" | custom-call | tf_op jit(solution)/shard_map/final_part/pallas_call | solution.py:319
  104.1 1.6 %collective-permute-start.22 = (f32[2,256]{1,0:T(2,128)}, f32[2,256]{1,0:T(2,128)S(1)}, u32[]{:S(2)}, u32[]{:S(2)}) collective-permute-start(f32[2,256]{1,0:T(2,128)} %final_part.1), channel_id=1, source_target_pairs={{0,2},{1,3},{2,0},{3,1},{4,6},{5,7},{6,4},{7,5},{8,10},{9,11},{10,... | collective-permute-start | bytes 6152 | tf_op jit(solution)/shard_map/ppermute | solution.py:19
  106.0 1.9 %collective-permute-done.22 = f32[2,256]{1,0:T(2,128)S(1)} collective-permute-done((f32[2,256]{1,0:T(2,128)}, f32[2,256]{1,0:T(2,128)S(1)}, u32[]{:S(2)}, u32[]{:S(2)}) %collective-permute-start.22) | collective-permute-done | bytes 2080 | tf_op jit(solution)/shard_map/ppermute | solution.py:19
  (127 shorter events, 23.4 us)
Async XLA Ops:
  0.6 33.8 %copy-start = (bf16[1024,1024]{1,0:T(8,128)(2,1)S(1)}, bf16[1024,1024]{1,0:T(8,128)(2,1)}, u32[]{:S(2)}) copy-start(bf16[1024,1024]{1,0:T(8,128)(2,1)} %param.12) | copy-start | bytes 6291460
  0.6 22.0 %copy-start.21 = (s32[256]{0:T(256)S(1)}, s32[256]{0:T(256)}, u32[]{:S(2)}) copy-start(s32[256]{0:T(256)} %param.17) | copy-start | bytes 3076
  0.7 22.1 %copy-start.22 = (s32[256]{0:T(256)S(1)}, s32[256]{0:T(256)}, u32[]{:S(2)}) copy-start(s32[256]{0:T(256)} %param.15) | copy-start | bytes 3076
  4.6 20.9 %copy-start.8 = (f32[2,1024,8]{1,2,0:T(8,128)S(1)}, f32[2,1024,8]{1,2,0:T(8,128)}, u32[]{:S(2)}) copy-start(f32[2,1024,8]{1,2,0:T(8,128)} %param.11) | copy-start | bytes 196612
  4.6 20.9 %copy-start.10 = (f32[3,3,1024]{2,1,0:T(4,128)S(1)}, f32[3,3,1024]{2,1,0:T(4,128)}, u32[]{:S(2)}) copy-start(f32[3,3,1024]{2,1,0:T(4,128)} %filt_ref.3) | copy-start | bytes 110596
  9.6 14.0 %collective-permute-start.2 = (bf16[32,1024]{1,0:T(8,128)(2,1)S(1)}, bf16[32,1024]{1,0:T(8,128)(2,1)S(1)}, u32[]{:S(2)}, u32[]{:S(2)}) collective-permute-start(bf16[32,1024]{1,0:T(8,128)(2,1)S(1)} %get-tuple-element.9.rest_0_), channel_id=1, source_target_pairs={{0,4},{4,0},{8,12},{12,8},{1,5},{5,1},{9,13},{13,9},{2,6},{6,2},{1... | collective-permute-start | bytes 196616 | tf_op jit(solution)/shard_map/ppermute | solution.py:19
  12.7 11.6 %collective-permute-start.3 = (bf16[32,1024]{1,0:T(8,128)(2,1)S(1)}, bf16[32,1024]{1,0:T(8,128)(2,1)S(1)}, u32[]{:S(2)}, u32[]{:S(2)}) collective-permute-start(bf16[32,1024]{1,0:T(8,128)(2,1)S(1)} %get-tuple-element.9.rest_0_), channel_id=1, source_target_pairs={{0,8},{4,12},{8,0},{12,4},{1,9},{5,13},{9,1},{13,5},{2,10},{6,14},... | collective-permute-start | bytes 196616 | tf_op jit(solution)/shard_map/ppermute | solution.py:19
  15.3 9.6 %collective-permute-start.4 = (bf16[32,1024]{1,0:T(8,128)(2,1)S(1)}, bf16[32,1024]{1,0:T(8,128)(2,1)S(1)}, u32[]{:S(2)}, u32[]{:S(2)}) collective-permute-start(bf16[32,1024]{1,0:T(8,128)(2,1)S(1)} %get-tuple-element.9.rest_0_), channel_id=1, source_target_pairs={{0,12},{4,8},{8,4},{12,0},{1,13},{5,9},{9,5},{13,1},{2,14},{6,10},... | collective-permute-start | bytes 196616 | tf_op jit(solution)/shard_map/ppermute | solution.py:19
  17.8 47.7 %collective-permute-start = (bf16[1024,512]{1,0:T(8,128)(2,1)}, bf16[1024,512]{1,0:T(8,128)(2,1)}, u32[]{:S(2)}, u32[]{:S(2)}) collective-permute-start(bf16[1024,512]{1,0:T(8,128)(2,1)} %fusion), channel_id=1, source_target_pairs={{0,2},{5,7},{10,8},{15,13},{16,18},{21,23},{26,24},{31,29}} | collective-permute-start | bytes 3145736 | tf_op jit(solution)/shard_map/ppermute | solution.py:345
  22.6 66.0 %copy-start.2 = (s32[256,1]{1,0:T(8,128)}, s32[256,1]{1,0:T(8,128)S(1)}, u32[]{:S(2)}) copy-start(s32[256,1]{1,0:T(8,128)S(1)} %copy.12.row_ref) | copy-start | bytes 3076
  32.8 11.7 %collective-permute-start.7 = (bf16[256,1024]{1,0:T(8,128)(2,1)S(1)}, bf16[256,1024]{1,0:T(8,128)(2,1)}, u32[]{:S(2)}, u32[]{:S(2)}) collective-permute-start(bf16[256,1024]{1,0:T(8,128)(2,1)S(1)} %carry_part.1), channel_id=1, source_target_pairs={{0,4},{4,0},{8,12},{12,8},{1,5},{5,1},{9,13},{13,9},{2,6},{6,2},{1... | collective-permute-start | bytes 1572872 | tf_op jit(solution)/shard_map/ppermute | solution.py:19
  32.9 20.0 %collective-permute-start.10 = (bf16[256,1024]{1,0:T(8,128)(2,1)S(1)}, bf16[256,1024]{1,0:T(8,128)(2,1)}, u32[]{:S(2)}, u32[]{:S(2)}) collective-permute-start(bf16[256,1024]{1,0:T(8,128)(2,1)S(1)} %carry_part.1), channel_id=1, source_target_pairs={{4,8},{8,4},{5,9},{9,5},{6,10},{10,6},{7,11},{11,7},{20,24},{24,20... | collective-permute-start | bytes 1572872 | tf_op jit(solution)/shard_map/ppermute | solution.py:420
  35.5 10.5 %collective-permute-start.5 = (bf16[128,1024]{1,0:T(8,128)(2,1)}, bf16[128,1024]{1,0:T(8,128)(2,1)S(1)}, u32[]{:S(2)}, u32[]{:S(2)}) collective-permute-start(bf16[128,1024]{1,0:T(8,128)(2,1)} %convolution_convert_fusion.3), channel_id=1, source_target_pairs={{0,1},{1,0},{2,3},{3,2},{4,5},{5,4},{6,7},{7,6},{8,9},{9,8},{10,11... | collective-permute-start | bytes 786440 | tf_op jit(solution)/shard_map/ppermute | solution.py:19
  45.9 1.6 %collective-permute-start.8 = (bf16[128,1024]{1,0:T(8,128)(2,1)S(1)}, bf16[128,1024]{1,0:T(8,128)(2,1)S(1)}, u32[]{:S(2)}, u32[]{:S(2)}) collective-permute-start(bf16[128,1024]{1,0:T(8,128)(2,1)S(1)} %convolution_convert_fusion.2), channel_id=1, source_target_pairs={{0,1},{1,0},{2,3},{3,2},{4,5},{5,4},{6,7},{7,6},{8,9},{9,8},{10,11... | collective-permute-start | bytes 786440 | tf_op jit(solution)/shard_map/ppermute | solution.py:19
  46.5 19.1 %copy-start.19 = (bf16[1024,512]{1,0:T(8,128)(2,1)S(1)}, bf16[1024,512]{1,0:T(8,128)(2,1)}, u32[]{:S(2)}) copy-start(bf16[1024,512]{1,0:T(8,128)(2,1)} %param.14) | copy-start | bytes 3145732
  46.5 19.1 %copy-start.20 = (f32[1024]{0:T(1024)S(1)}, f32[1024]{0:T(1024)}, u32[]{:S(2)}) copy-start(f32[1024]{0:T(1024)} %param.13) | copy-start | bytes 12292
  46.5 6.4 %collective-permute-start.6 = (bf16[64,1024]{1,0:T(8,128)(2,1)S(1)}, bf16[64,1024]{1,0:T(8,128)(2,1)S(1)}, u32[]{:S(2)}, u32[]{:S(2)}) collective-permute-start(bf16[64,1024]{1,0:T(8,128)(2,1)S(1)} %dynamic-slice_convert_fusion.3), channel_id=1, source_target_pairs={{0,2},{1,3},{2,0},{3,1},{4,6},{5,7},{6,4},{7,5},{8,10},{9,11},{10,... | collective-permute-start | bytes 393224 | tf_op jit(solution)/shard_map/ppermute | solution.py:19
  46.7 8.6 %collective-permute-start.14 = (bf16[256,1024]{1,0:T(8,128)(2,1)}, bf16[256,1024]{1,0:T(8,128)(2,1)S(1)}, u32[]{:S(2)}, u32[]{:S(2)}) collective-permute-start(bf16[256,1024]{1,0:T(8,128)(2,1)} %collective-permute-done.7), channel_id=1, source_target_pairs={{4,8},{8,4},{5,9},{9,5},{6,10},{10,6},{7,11},{11,7},{20,24},{24,20... | collective-permute-start | bytes 1572872 | tf_op jit(solution)/shard_map/ppermute | solution.py:421
  49.0 6.3 %collective-permute-start.9 = (bf16[64,1024]{1,0:T(8,128)(2,1)S(1)}, bf16[64,1024]{1,0:T(8,128)(2,1)S(1)}, u32[]{:S(2)}, u32[]{:S(2)}) collective-permute-start(bf16[64,1024]{1,0:T(8,128)(2,1)S(1)} %dynamic-slice_convert_fusion.2), channel_id=1, source_target_pairs={{0,2},{1,3},{2,0},{3,1},{4,6},{5,7},{6,4},{7,5},{8,10},{9,11},{10,... | collective-permute-start | bytes 393224 | tf_op jit(solution)/shard_map/ppermute | solution.py:19
  52.9 15.7 %collective-permute-start.11 = (bf16[256,1024]{1,0:T(8,128)(2,1)}, bf16[256,1024]{1,0:T(8,128)(2,1)S(1)}, u32[]{:S(2)}, u32[]{:S(2)}) collective-permute-start(bf16[256,1024]{1,0:T(8,128)(2,1)} %collective-permute-done.10), channel_id=1, source_target_pairs={{0,4},{4,0},{8,12},{12,8},{1,5},{5,1},{9,13},{13,9},{2,6},{6,2},{1... | collective-permute-start | bytes 1572872 | tf_op jit(solution)/shard_map/ppermute | solution.py:19
  55.3 23.0 %collective-permute-start.15 = (bf16[256,1024]{1,0:T(8,128)(2,1)S(1)}, bf16[256,1024]{1,0:T(8,128)(2,1)S(1)}, u32[]{:S(2)}, u32[]{:S(2)}) collective-permute-start(bf16[256,1024]{1,0:T(8,128)(2,1)S(1)} %collective-permute-done.14), channel_id=1, source_target_pairs={{0,4},{4,0},{8,12},{12,8},{1,5},{5,1},{9,13},{13,9},{2,6},{6,2},{1... | collective-permute-start | bytes 1572872 | tf_op jit(solution)/shard_map/ppermute | solution.py:19
  67.2 21.1 %collective-permute-start.1 = (bf16[1024,512]{1,0:T(8,128)(2,1)S(1)}, bf16[1024,512]{1,0:T(8,128)(2,1)S(1)}, u32[]{:S(2)}, u32[]{:S(2)}) collective-permute-start(bf16[1024,512]{1,0:T(8,128)(2,1)S(1)} %fusion.46), channel_id=1, source_target_pairs={{0,1},{2,3},{5,4},{7,6},{10,11},{8,9},{15,14},{13,12},{16,17},{18,... | collective-permute-start | bytes 3145736 | tf_op jit(solution)/shard_map/ppermute | solution.py:345
  70.3 8.8 %collective-permute-start.12 = (bf16[128,1024]{1,0:T(8,128)(2,1)S(1)}, bf16[128,1024]{1,0:T(8,128)(2,1)S(1)}, u32[]{:S(2)}, u32[]{:S(2)}) collective-permute-start(bf16[128,1024]{1,0:T(8,128)(2,1)S(1)} %convolution_convert_fusion.1), channel_id=1, source_target_pairs={{0,1},{1,0},{2,3},{3,2},{4,5},{5,4},{6,7},{7,6},{8,9},{9,8},{10,11... | collective-permute-start | bytes 786440 | tf_op jit(solution)/shard_map/ppermute | solution.py:19
  79.0 2.2 %collective-permute-start.16 = (bf16[128,1024]{1,0:T(8,128)(2,1)S(1)}, bf16[128,1024]{1,0:T(8,128)(2,1)S(1)}, u32[]{:S(2)}, u32[]{:S(2)}) collective-permute-start(bf16[128,1024]{1,0:T(8,128)(2,1)S(1)} %convolution_convert_fusion), channel_id=1, source_target_pairs={{0,1},{1,0},{2,3},{3,2},{4,5},{5,4},{6,7},{7,6},{8,9},{9,8},{10,11... | collective-permute-start | bytes 786440 | tf_op jit(solution)/shard_map/ppermute | solution.py:19
  79.6 6.4 %collective-permute-start.13 = (bf16[64,1024]{1,0:T(8,128)(2,1)S(1)}, bf16[64,1024]{1,0:T(8,128)(2,1)S(1)}, u32[]{:S(2)}, u32[]{:S(2)}) collective-permute-start(bf16[64,1024]{1,0:T(8,128)(2,1)S(1)} %dynamic-slice_convert_fusion.1), channel_id=1, source_target_pairs={{0,2},{1,3},{2,0},{3,1},{4,6},{5,7},{6,4},{7,5},{8,10},{9,11},{10,... | collective-permute-start | bytes 393224 | tf_op jit(solution)/shard_map/ppermute | solution.py:19
  81.7 6.6 %collective-permute-start.17 = (bf16[64,1024]{1,0:T(8,128)(2,1)S(1)}, bf16[64,1024]{1,0:T(8,128)(2,1)S(1)}, u32[]{:S(2)}, u32[]{:S(2)}) collective-permute-start(bf16[64,1024]{1,0:T(8,128)(2,1)S(1)} %dynamic-slice_convert_fusion), channel_id=1, source_target_pairs={{0,2},{1,3},{2,0},{3,1},{4,6},{5,7},{6,4},{7,5},{8,10},{9,11},{10,... | collective-permute-start | bytes 393224 | tf_op jit(solution)/shard_map/ppermute | solution.py:19
  90.3 5.1 %collective-permute-start.18 = (bf16[68,512]{1,0:T(8,128)(2,1)S(1)}, bf16[68,512]{1,0:T(8,128)(2,1)S(1)}, u32[]{:S(2)}, u32[]{:S(2)}) collective-permute-start(bf16[68,512]{1,0:T(8,128)(2,1)S(1)} %get-tuple-element.33), channel_id=1, source_target_pairs={{0,4},{4,0},{8,12},{12,8},{1,5},{5,1},{9,13},{13,9},{2,6},{6,2},{1... | collective-permute-start | bytes 208904 | tf_op jit(solution)/shard_map/ppermute | solution.py:19
  92.1 8.2 %collective-permute-start.19 = (bf16[68,512]{1,0:T(8,128)(2,1)S(1)}, bf16[68,512]{1,0:T(8,128)(2,1)S(1)}, u32[]{:S(2)}, u32[]{:S(2)}) collective-permute-start(bf16[68,512]{1,0:T(8,128)(2,1)S(1)} %get-tuple-element.34), channel_id=1, source_target_pairs={{0,8},{4,12},{8,0},{12,4},{1,9},{5,13},{9,1},{13,5},{2,10},{6,14},... | collective-permute-start | bytes 208904 | tf_op jit(solution)/shard_map/ppermute | solution.py:19
  93.8 6.5 %collective-permute-start.20 = (bf16[68,512]{1,0:T(8,128)(2,1)S(1)}, bf16[68,512]{1,0:T(8,128)(2,1)S(1)}, u32[]{:S(2)}, u32[]{:S(2)}) collective-permute-start(bf16[68,512]{1,0:T(8,128)(2,1)S(1)} %get-tuple-element.35), channel_id=1, source_target_pairs={{0,12},{4,8},{8,4},{12,0},{1,13},{5,9},{9,5},{13,1},{2,14},{6,10},... | collective-permute-start | bytes 208904 | tf_op jit(solution)/shard_map/ppermute | solution.py:19
  104.1 1.9 %collective-permute-start.21 = (f32[2,256]{1,0:T(2,128)}, f32[2,256]{1,0:T(2,128)S(1)}, u32[]{:S(2)}, u32[]{:S(2)}) collective-permute-start(f32[2,256]{1,0:T(2,128)} %final_part.1), channel_id=1, source_target_pairs={{0,1},{1,0},{2,3},{3,2},{4,5},{5,4},{6,7},{7,6},{8,9},{9,8},{10,11... | collective-permute-start | bytes 6152 | tf_op jit(solution)/shard_map/ppermute | solution.py:19
  104.1 3.8 %collective-permute-start.22 = (f32[2,256]{1,0:T(2,128)}, f32[2,256]{1,0:T(2,128)S(1)}, u32[]{:S(2)}, u32[]{:S(2)}) collective-permute-start(f32[2,256]{1,0:T(2,128)} %final_part.1), channel_id=1, source_target_pairs={{0,2},{1,3},{2,0},{3,1},{4,6},{5,7},{6,4},{7,5},{8,10},{9,11},{10,... | collective-permute-start | bytes 6152 | tf_op jit(solution)/shard_map/ppermute | solution.py:19
  105.7 3.2 %collective-permute-start.23 = (f32[2,256]{1,0:T(2,128)}, f32[2,256]{1,0:T(2,128)S(1)}, u32[]{:S(2)}, u32[]{:S(2)}) collective-permute-start(f32[2,256]{1,0:T(2,128)} %final_part.1), channel_id=1, source_target_pairs={{0,3},{1,2},{2,1},{3,0},{4,7},{5,6},{6,5},{7,4},{8,11},{9,10},{10,... | collective-permute-start | bytes 6152 | tf_op jit(solution)/shard_map/ppermute | solution.py:19
  (15 other events, 43.2 us)

commit v2 on v1

--- a/solution.py
+++ b/solution.py
@@ -7,6 +7,7 @@
 from jax.experimental.pallas import tpu as pltpu
 from jax.sharding import PartitionSpec as P
 
+
 F32 = jnp.float32
 BF16 = jnp.bfloat16
 LANES = 128
@@ -19,10 +20,6 @@
     return lax.ppermute(value, axis, [(i, i ^ bit) for i in range(count)])
 
 
-def rows_of(ref, start, size):
-    return ref[pl.ds(pl.multiple_of(start, size), size), :]
-
-
 def mix(taps, now, back1, back2):
     return taps[0] * now + taps[1] * back1 + taps[2] * back2
 
@@ -35,8 +32,11 @@
     return [filt_ref[stream, j : j + 1, cols] for j in range(3)]
 
 
-def local_kernel(steps, modes, x_ref, filt_ref, mode_ref, nat_ref, y_ref, gate_ref, start_ref, msg_ref, xs, gs):
+def local_kernel(steps, modes, spread, x_ref, filt_ref, mode_ref, nat_ref, y_ref, gate_ref, start_ref, msg_ref, xs, gs):
     rows = steps * SUBS
+    turn = pl.program_id(0)
+    ids = nat_ref[...]
+    ids = jnp.where(turn < spread, ids // 256, jnp.where(turn < 2 * spread, ids % 256, 0)).astype(F32)
     for tile in range(x_ref.shape[2] // LANES):
         cols = slice(tile * LANES, (tile + 1) * LANES)
         sub = lax.broadcasted_iota(jnp.int32, (SUBS, LANES), 0)
@@ -83,25 +83,25 @@
         last = [xs[i, rows - 2 : rows, :] for i in range(3)]
         edge = jnp.concatenate([first[1], first[2], last[1], last[2]], axis=0)
         other = jnp.concatenate(
-            [last[0], first[0], nat_ref[0:1, cols], jnp.zeros((3, LANES), F32)], axis=0
+            [last[0], first[0], ids[:, cols], jnp.zeros((3, LANES), F32)], axis=0
         )
         msg_ref[:, cols] = jnp.concatenate([high, end - high, edge, other], axis=0).astype(BF16)
 
 
-def local_part(streams, filt, modes_t, nat_row):
+def local_part(streams, filt, modes_t, native):
     rows, width = streams.shape[1:]
     modes = modes_t.shape[1]
     steps = rows // SUBS
     block = 2 * LANES
     msg_rows = 2 * modes + 16
     return pl.pallas_call(
-        functools.partial(local_kernel, steps, modes),
+        functools.partial(local_kernel, steps, modes, rows // block),
         grid=(width // block,),
         in_specs=[
             pl.BlockSpec((3, rows, block), lambda c: (0, 0, c)),
             pl.BlockSpec((3, 3, block), lambda c: (0, 0, c)),
             pl.BlockSpec((2, modes, block), lambda c: (0, 0, c)),
-            pl.BlockSpec((1, block), lambda c: (0, c)),
+            pl.BlockSpec((1, block), lambda c: (0, c % (rows // block))),
         ],
         out_specs=[
             pl.BlockSpec((rows, block), lambda c: (0, c)),
@@ -116,10 +116,9 @@
             jax.ShapeDtypeStruct((msg_rows, width), BF16),
         ],
         scratch_shapes=[pltpu.VMEM((3, rows, LANES), F32), pltpu.VMEM((rows, LANES), F32)],
-        compiler_params=pltpu.CompilerParams(vmem_limit_bytes=24 * 2**20),
         cost_estimate=pl.CostEstimate(flops=rows * width * 64, bytes_accessed=rows * width * 12, transcendentals=0),
         name="local_part",
-    )(streams, filt, modes_t, nat_row)
+    )(streams, filt, modes_t, native[None, :])
 
 
 def carry_kernel(steps, modes, stacked, count, where_ref, filt_ref, mode_ref, y_ref, gate_ref, start_ref, *rest):
@@ -231,7 +230,6 @@
             scratch_shapes=[pltpu.VMEM((count, msg_rows, LANES), F32), pltpu.VMEM((rows, LANES), F32)],
         ),
         out_shape=jax.ShapeDtypeStruct((rows, width), BF16),
-        compiler_params=pltpu.CompilerParams(vmem_limit_bytes=24 * 2**20),
         cost_estimate=pl.CostEstimate(flops=rows * width * 32, bytes_accessed=rows * width * 8, transcendentals=0),
         name="carry_part",
     )(me, filt, modes_t, y, gate, start, *msgs)
@@ -250,14 +248,23 @@
     return jnp.dot(onehot, high, preferred_element_type=F32) + jnp.dot(onehot, low, preferred_element_type=F32)
 
 
-def logit_kernel(share, where_ref, un_ref, row_ref, id_ref, nat_ref, *rest):
-    slots = where_ref.shape[0]
-    slot_refs, (part_ref, square_ref, score_ref, acc) = rest[:slots], rest[slots:]
+def two_rows(row, width):
+    high = rounded(row)
+    both = jnp.concatenate([high, row - high], axis=0)
+    return jnp.concatenate([both, jnp.zeros((2, width - row.shape[1]), F32)], axis=1)
+
+
+def logit_kernel(share, peers, where_ref, un_ref, row_ref, id_ref, nat_ref, *rest):
+    slots = where_ref.shape[0] - 1
+    slot_refs, rest = rest[:slots], rest[slots:]
+    part_ref, square_ref, score_ref = rest[:3]
+    msg_refs, acc = rest[3 : 3 + peers], rest[-1]
     for k in range(slots):
         acc[pl.ds(pl.multiple_of(where_ref[k] * share, share), share), :] = slot_refs[k][...]
     values = acc[...]
     total = values.shape[0]
-    square_ref[...] = as_row(jnp.sum(values * values, axis=1, keepdims=True), total)
+    square = as_row(jnp.sum(values * values, axis=1, keepdims=True), total)
+    square_ref[...] = square
     part = jnp.dot(values.astype(BF16), un_ref[...], preferred_element_type=F32)
     part_ref[...] = part
     muts = row_ref.shape[0]
@@ -266,41 +273,63 @@
     picked = exact_dot((spots == row_ref[...]).astype(BF16), part)
     words = lax.broadcasted_iota(jnp.int32, (muts, vocab), 1)
     gain = jnp.where(words == id_ref[...], picked, 0.0) - jnp.where(words == nat_ref[...], picked, 0.0)
-    score_ref[...] = as_row(jnp.sum(gain, axis=1, keepdims=True), muts)
-
-
-def logit_part(where, slots, un, mut_row, mut_id, mut_nat):
+    score = as_row(jnp.sum(gain, axis=1, keepdims=True), muts)
+    score_ref[...] = score
+    if peers:
+        me = where_ref[slots]
+        extra = jnp.concatenate(
+            [two_rows(square, vocab), two_rows(score, vocab), jnp.zeros((4, vocab), F32)], axis=0
+        ).astype(BF16)
+        for k in range(1, peers + 1):
+            their = part_ref[pl.ds(pl.multiple_of((me ^ k) * share, share), share), :]
+            msg_refs[k - 1][0:share, :] = their.astype(BF16)
+            msg_refs[k - 1][share : share + 8, :] = extra
+
+
+def logit_part(where, slots, un, mut_row, mut_id, mut_nat, peers):
     share, wide = slots[0].shape
     total = share * len(slots)
     vocab = un.shape[1]
     muts = mut_row.shape[0]
     whole = pl.BlockSpec(memory_space=pltpu.VMEM)
     return pl.pallas_call(
-        functools.partial(logit_kernel, share),
+        functools.partial(logit_kernel, share, peers),
         in_specs=[pl.BlockSpec(memory_space=pltpu.SMEM)] + [whole] * (4 + len(slots)),
-        out_specs=[whole] * 3,
+        out_specs=[whole] * (3 + peers),
         out_shape=[
             jax.ShapeDtypeStruct((total, vocab), F32),
             jax.ShapeDtypeStruct((1, total), F32),
             jax.ShapeDtypeStruct((1, muts), F32),
-        ],
+        ]
+        + [jax.ShapeDtypeStruct((share + 8, vocab), BF16)] * peers,
         scratch_shapes=[pltpu.VMEM((total, wide), F32)],
-        compiler_params=pltpu.CompilerParams(vmem_limit_bytes=40 * 2**20),
         name="logit_part",
     )(where, un, mut_row, mut_id, mut_nat, *slots)
 
 
-def final_kernel(feats, where_ref, log_ref, square_ref, score_ref, nat_ref, row_ref, out_ref):
+def final_kernel(feats, where_ref, log_ref, square_ref, score_ref, nat_ref, row_ref, *rest):
+    msg_refs, out_ref = rest[:-1], rest[-1]
     me, piece = where_ref[0], where_ref[1]
-    share, vocab = log_ref.shape
+    share = nat_ref.shape[0]
+    vocab = log_ref.shape[1]
     total = square_ref.shape[1]
     muts = score_ref.shape[1]
     width = out_ref.shape[1]
-    scale_row = lax.rsqrt(square_ref[...] / feats + EPS)
+    if msg_refs:
+        logits = log_ref[pl.ds(pl.multiple_of(me * share, share), share), :]
+    else:
+        logits = log_ref[...]
+    square, score = square_ref[...], score_ref[...]
+    for msg_ref in msg_refs:
+        logits = logits + msg_ref[0:share, :].astype(F32)
+        extra = msg_ref[share : share + 8, :].astype(F32)
+        square = square + (extra[0:1, 0:total] + extra[1:2, 0:total])
+        score = score + (extra[2:3, 0:muts] + extra[3:4, 0:muts])
+    scale_row = lax.rsqrt(square / feats + EPS)
     r = lax.broadcasted_iota(jnp.int32, (share, total), 0)
     c = lax.broadcasted_iota(jnp.int32, (share, total), 1)
     scale = jnp.sum(jnp.where(c == r + me * share, scale_row, 0.0), axis=1, keepdims=True)
-    logits = log_ref[...] * scale
+    logits = logits * scale
     top = jnp.max(logits, axis=1, keepdims=True)
     norm = top + jnp.log(jnp.sum(jnp.exp(logits - top), axis=1, keepdims=True))
     words = lax.broadcasted_iota(jnp.int32, (share, vocab), 1)
@@ -311,18 +340,36 @@
     r = lax.broadcasted_iota(jnp.int32, (muts, total), 0)
     c = lax.broadcasted_iota(jnp.int32, (muts, total), 1)
     at_mut = jnp.sum(jnp.where(c == row_ref[...], scale_row, 0.0), axis=1, keepdims=True)
-    out_ref[1:2, 0:muts] = score_ref[...] * as_row(at_mut, muts)
-
-
-def final_part(feats, where, logits, squares, scores, nat, mut_row, width):
+    out_ref[1:2, 0:muts] = score * as_row(at_mut, muts)
+
+
+def final_part(feats, where, logits, squares, scores, nat, mut_row, msgs, width):
     whole = pl.BlockSpec(memory_space=pltpu.VMEM)
     return pl.pallas_call(
         functools.partial(final_kernel, float(feats)),
-        in_specs=[pl.BlockSpec(memory_space=pltpu.SMEM)] + [whole] * 5,
+        in_specs=[pl.BlockSpec(memory_space=pltpu.SMEM)] + [whole] * (5 + len(msgs)),
         out_specs=whole,
         out_shape=jax.ShapeDtypeStruct((2, width), F32),
         name="final_part",
-    )(where, logits, squares, scores, nat, mut_row)
+    )(where, logits, squares, scores, nat, mut_row, *msgs)
+
+
+def total_kernel(*refs):
+    like_ref, score_ref = refs[-2:]
+    total = functools.reduce(lambda p, q: p + q, [ref[...] for ref in refs[:-2]])
+    like_ref[...] = total[0:1, 0 : like_ref.shape[1]]
+    score_ref[...] = total[1:2, 0 : score_ref.shape[1]]
+
+
+def total_part(pieces, rows, muts):
+    whole = pl.BlockSpec(memory_space=pltpu.VMEM)
+    return pl.pallas_call(
+        total_kernel,
+        in_specs=[whole] * len(pieces),
+        out_specs=[whole] * 2,
+        out_shape=[jax.ShapeDtypeStruct((1, rows), F32), jax.ShapeDtypeStruct((1, muts), F32)],
+        name="total_part",
+    )(*pieces)
 
 
 def spread_unembed(unembed, norm_gain, rows_wanted):
@@ -342,7 +389,8 @@
         pairs = [
             (i * shards + (owner[i] ^ h), i * shards + (owner[i] ^ h ^ bit)) for i in range(count) for h in holders
         ]
-        value = value + lax.ppermute(value, ("ctx", "mp"), pairs)
+        moved = lax.ppermute(value, ("ctx", "mp"), pairs)
+        value = value + moved
         holders = holders + [h ^ bit for h in holders]
         bit //= 2
     return value
@@ -384,16 +432,13 @@
 
 
 def body(streams, short_filter, mode_params, out_weight, norm_gain, unembed, native, mut_pos, mut_ids):
-    rows, width = streams.shape[1:]
+    rows, _ = streams.shape[1:]
     count, shards = lax.axis_size("ctx"), lax.axis_size("mp")
     z = lax.axis_index("ctx")
     quick = count == 4
     modes_t = jnp.swapaxes(mode_params, 1, 2)
     me = z.astype(jnp.int32)[None]
-    high = native // 256
-    nat_row = jnp.concatenate([high, native - high * 256]).astype(F32)
-    nat_row = jnp.pad(nat_row, (0, width - 2 * rows))[None, :]
-    y, gate, start, msg = local_part(streams, short_filter, modes_t, nat_row)
+    y, gate, start, msg = local_part(streams, short_filter, modes_t, native)
     nat_at = 2 * mode_params.shape[2] + 12
     if quick:
         msgs = [msg] + [swap(msg, "ctx", k) for k in range(1, count)]
@@ -407,6 +452,8 @@
     nat_rows = nat_rows.astype(jnp.int32)
     nat_all = (nat_rows[:, :rows] * 256 + nat_rows[:, rows:]).reshape(-1)
 
+    held, unembed, norm_gain = lax.optimization_barrier((gated, unembed, norm_gain)) if quick else (gated, unembed, norm_gain)
+    gated = held
     un = spread_unembed(unembed, norm_gain, out_weight.shape[1])
     piece = row_piece()
     share = rows // shards
@@ -421,36 +468,25 @@
         mid_b = lax.ppermute(beside, "ctx", middle)
         far_a = swap(mid_a, "ctx", 1)
         far_b = swap(mid_b, "ctx", 1)
-        blocks = [gated, beside, mid_a + far_a, mid_b + far_b]
+        third = mid_a + far_a
+        fourth = mid_b + far_b
+        blocks = [gated, beside, third, fourth]
         low = z < 2
-        where = jnp.stack([z, z ^ 1, jnp.where(low, 2, 1), jnp.where(low, 3, 0)]).astype(jnp.int32)
+        where = [z, z ^ 1, jnp.where(low, 2, 1), jnp.where(low, 3, 0)]
     else:
         every = lax.all_gather(gated, "ctx")
         blocks = [every[b] for b in range(count)]
-        where = jnp.arange(count, dtype=jnp.int32)
-    slots = [project(part, out_weight) for part in blocks]
-    part, squares, scores = logit_part(where, slots, un, mut_row, mut_ids[:, None], mut_nat)
-
+        where = list(range(count))
+    where = jnp.stack([jnp.asarray(w, jnp.int32) for w in where + [z]])
+    slots = []
+    for part in blocks:
+        slots.append(project(part, out_weight))
+    peers = count - 1 if quick else 0
+    part, squares, scores, *msgs = logit_part(where, slots, un, mut_row, mut_ids[:, None], mut_nat, peers)
     if quick:
-        vocab = part.shape[1]
-        own = lax.dynamic_slice_in_dim(part, z * share, share, 0)
-
-        def wide(value):
-            first = value.astype(BF16)
-            second = (value - first.astype(F32)).astype(BF16)
-            both = jnp.concatenate([first, second], axis=0)
-            return jnp.pad(both, ((0, 0), (0, vocab - both.shape[1])))
-
-        extra = jnp.concatenate([wide(squares), wide(scores)], axis=0)
-        logits = own
-        for k in range(1, count):
-            theirs = lax.dynamic_slice_in_dim(part, (z ^ k) * share, share, 0).astype(BF16)
-            got = swap(jnp.concatenate([theirs, extra], axis=0), "ctx", k).astype(F32)
-            logits = logits + got[:share]
-            squares = squares + (got[share : share + 1] + got[share + 1 : share + 2])[:, : squares.shape[1]]
-            scores = scores + (got[share + 2 : share + 3] + got[share + 3 : share + 4])[:, : scores.shape[1]]
+        msgs = [swap(msgs[k - 1], "ctx", k) for k in range(1, count)]
     else:
-        logits = lax.psum_scatter(part, "ctx", scatter_dimension=0, tiled=True)
+        part = lax.psum_scatter(part, "ctx", scatter_dimension=0, tiled=True)
         squares = lax.psum(squares, "ctx")
         scores = lax.psum(scores, "ctx")
 
@@ -458,11 +494,10 @@
     spot = jnp.stack([z, piece]).astype(jnp.int32)
     feats = norm_gain.shape[0] * shards
     span = max(rows, mut_pos.shape[0])
-    result = final_part(feats, spot, logits, squares, scores, own_nat, mut_row, span)
-    total = result
-    for k in range(1, shards):
-        total = total + swap(result, "mp", k)
-    return total[0, :rows], total[1, : mut_pos.shape[0]]
+    result = final_part(feats, spot, part, squares, scores, own_nat, mut_row, msgs, span)
+    pieces = [result] + [swap(result, "mp", k) for k in range(1, shards)]
+    like, score = total_part(pieces, rows, mut_pos.shape[0])
+    return like[0], score[0]
 
 
 def solution(mesh):

time: 111 us -> 107 us (0.964)
  Pallas kernels: 9.12 us -> 16.9 us
  waiting for transfers between devices: 30.7 us -> 26.1 us
  local copies, waits for them, and re-layouts: 15.3 us -> 11.3 us
  other arithmetic: 10.2 us -> 7.8 us
  starting transfers between devices: 37.4 us -> 35.7 us
    unnamed x47 -> x29, local copies, waits for them, and re-layouts: 11.4 us -> 1.87 us
    pallas_call x2 -> x3, Pallas kernels: 5.47 us -> 10.5 us  [the longest x1 6.01 us: local_part(): pl.pallas_call(functools.partial(local_kernel, steps, modes, rows // bloc...]
    ppermute x20, waiting for transfers between devices: 30.7 us -> 26.1 us  [swap(): return lax.ppermute(value, axis, [(i, i ^ bit) for i in range(count)])]
    slice x4, local copies, waits for them, and re-layouts: 0.03 us -> 2.87 us  [body(): nat_rows = jnp.stack([msgs[k][nat_at, :2 * rows] for k in range(count)])]
    add x4, other arithmetic: 0.11 us -> 2.93 us  [project(): value = keep + swap(sent, 'mp', bit).astype(F32)]
    add x8 -> x4, other arithmetic: 5.89 us -> 3.19 us  [the longest x2 1.76 us: spread_unembed(): value = value + moved]
    pallas_call x1, Pallas kernels: 1.74 us -> 4.22 us  [carry_part(): pl.pallas_call(functools.partial(carry_kernel, steps, modes, stacked, cou...]
    select_n x1, other arithmetic: 2.55 us -> 0.3 us  [spread_unembed(): value = jnp.where(m == z // ratio, piece, jnp.zeros_like(piece))]
  transfers between devices with their start and end apart: 24 -> 24, of which waited for: 9 -> 9; matrix products, arithmetic and copies ran while one was open for 14% -> 22% of each run, Pallas kernels for 2% -> 0%
where the time goes in v2:
time: 107 us; the launch traced here: 106 us
  starting transfers between devices  35.7 us (33%)
  waiting for transfers between devices  26.1 us (24%)
  Pallas kernels  16.9 us (16%)
  local copies, waits for them, and re-layouts  11.3 us (11%)
  other arithmetic  7.8 us (7%)
  matrix products  7.15 us (7%)
    ppermute x20, starting transfers between devices, swap(): return lax.ppermute(value, axis, [(i, i ^ bit) for i in range(count)])  27.5 us
    ppermute x20, waiting for transfers between devices, swap(): return lax.ppermute(value, axis, [(i, i ^ bit) for i in range(count)])  26.1 us
    pallas_call x1, Pallas kernels, local_part(): pl.pallas_call(functools.partial(local_kernel, steps, modes, rows // bloc...  6.01 us
    ppermute x2, starting transfers between devices, spread_unembed(): moved = lax.ppermute(value, ('ctx', 'mp'), pairs)  5.92 us
    dot_general x4, matrix products, project(): sent = jnp.dot(send, weight, preferred_element_type=F32).astype(BF16)  4.39 us
    pallas_call x1, Pallas kernels, carry_part(): pl.pallas_call(functools.partial(carry_kernel, steps, modes, stacked, cou...  4.22 us
    pallas_call x1, Pallas kernels, logit_part(): pl.pallas_call(functools.partial(logit_kernel, share, peers), in_specs=[p...  3.29 us
    add x4, other arithmetic, project(): value = keep + swap(sent, 'mp', bit).astype(F32)  2.93 us
  transfers between devices with their start and end apart: 24, of which 9 were waited for; matrix products, arithmetic and copies ran while one was open for 22% of the time, Pallas kernels for 0%

profile of v2, /device:TPU:0, one launch (start us, length us, event | category | flops | bytes accessed | tf_op | source)
XLA Modules:
  0.0 105.8 jit_solution(4370417412654968496)
XLA Ops:
  0.7 6.0 %local_part.1 = (f32[256,1024]{1,0:T(8,128)}, bf16[256,1024]{1,0:T(8,128)(2,1)}, f32[64,1024]{1,0:T(8,128)}, bf16[32,1024]{1,0:T(8,128)(2,1)}) custom-call(bf16[3,256,1024]{2,1,0:T(8,128)(2,1)} %x_ref.1, f32[3,3,1024]{2,1,0:T(4,128)} %filt_ref.3, f32[2,8,1024]{2,1,0:T(8,128)} %bitcast.28, s32[1,256]{1,0:T(1,128)} %bitcast.33), custom_call_target="tpu_custom_call" | custom-call | flops 16777216 | bytes 3145728 | tf_op jit(solution)/shard_map/local_part/pallas_call | solution.py:97
  6.7 3.1 %collective-permute-start = (bf16[32,1024]{1,0:T(8,128)(2,1)}, bf16[32,1024]{1,0:T(8,128)(2,1)S(1)}, u32[]{:S(2)}, u32[]{:S(2)}) collective-permute-start(bf16[32,1024]{1,0:T(8,128)(2,1)} %get-tuple-element.20.rest_0_), channel_id=1, source_target_pairs={{0,4},{4,0},{8,12},{12,8},{1,5},{5,1},{9,13},{13,9},{2,6},{6,2},{1... | collective-permute-start | bytes 196616 | tf_op jit(solution)/shard_map/ppermute | solution.py:20
  9.8 2.6 %collective-permute-start.1 = (bf16[32,1024]{1,0:T(8,128)(2,1)}, bf16[32,1024]{1,0:T(8,128)(2,1)S(1)}, u32[]{:S(2)}, u32[]{:S(2)}) collective-permute-start(bf16[32,1024]{1,0:T(8,128)(2,1)} %get-tuple-element.20.rest_0_), channel_id=1, source_target_pairs={{0,8},{4,12},{8,0},{12,4},{1,9},{5,13},{9,1},{13,5},{2,10},{6,14},... | collective-permute-start | bytes 196616 | tf_op jit(solution)/shard_map/ppermute | solution.py:20
  14.6 1.5 %copy.13.id_ref = s32[256,1]{1,0:T(8,128)} copy(s32[256,1]{0,1:T(1,128)} %bitcast.32) | data formatting | bytes 2048 | tf_op jit(solution)/shard_map/broadcast_in_dim | solution.py:485
  17.6 1.1 collective-permute-done.2.rest_3_
  19.3 4.2 %carry_part.1 = bf16[256,1024]{1,0:T(8,128)(2,1)} custom-call(s32[1]{0:T(128)} %bitcast.where_ref, f32[3,3,1024]{2,1,0:T(4,128)} %filt_ref.3, f32[2,8,1024]{2,1,0:T(8,128)} %bitcast.29, f32[256,1024]{1,0:T(8,128)} %get-tuple-element.17.y_ref, bf16[256,1024]{1,0:T(8,128)(2,1)} %get-tuple-element.18.gate_ref, f32[64,1024]{1,0:T(8,128)} %get-tuple-element.19.start_ref, ...), custom_call_target="tpu_custom_call" | custom-call | flops 8388608 | bytes 2097152 | tf_op jit(solution)/shard_map/carry_part/pallas_call | solution.py:216
  23.6 1.6 %collective-permute-start.10 = (bf16[256,1024]{1,0:T(8,128)(2,1)}, bf16[256,1024]{1,0:T(8,128)(2,1)}, u32[]{:S(2)}, u32[]{:S(2)}) collective-permute-start(bf16[256,1024]{1,0:T(8,128)(2,1)} %carry_part.1), channel_id=1, source_target_pairs={{4,8},{8,4},{5,9},{9,5},{6,10},{10,6},{7,11},{11,7},{20,24},{24,20... | collective-permute-start | bytes 1572872 | tf_op jit(solution)/shard_map/ppermute | solution.py:467
  25.2 2.1 %convolution_convert_fusion.3 = bf16[128,1024]{1,0:T(8,128)(2,1)} fusion(bf16[1024,1024]{1,0:T(8,128)(2,1)S(1)} %copy-done, bf16[256,1024]{1,0:T(8,128)(2,1)} %carry_part.1, s32[]{:T(128)S(6)} %select_n.139), kind=kOutput, calls=%fused_computation.9 | convolution fusion | flops 268566528 | bytes 2621444 | tf_op jit(solution)/shard_map/dot_general | solution.py:415
  30.0 1.4 %gather_fusion.1 = s32[256]{0:T(256)S(1)} fusion(s32[1024]{0:T(1024)S(1)} %bitcast.27, s32[1024]{0:T(1024)S(1)} %pad_clamp_fusion), kind=kCustom, calls=%fused_computation.1 | custom fusion | bytes 3072 | tf_op jit(solution)/shard_map/gather | solution.py:462
  32.5 3.5 %collective-permute-start.3 = (bf16[1024,512]{1,0:T(8,128)(2,1)S(1)}, bf16[1024,512]{1,0:T(8,128)(2,1)S(1)}, u32[]{:S(2)}, u32[]{:S(2)}) collective-permute-start(bf16[1024,512]{1,0:T(8,128)(2,1)S(1)} %fusion), channel_id=1, source_target_pairs={{0,2},{5,7},{10,8},{15,13},{16,18},{21,23},{26,24},{31,29}} | collective-permute-start | bytes 3145736 | tf_op jit(solution)/shard_map/ppermute | solution.py:392
  36.0 1.4 %convolution_convert_fusion.2 = bf16[128,1024]{1,0:T(8,128)(2,1)S(1)} fusion(bf16[1024,1024]{1,0:T(8,128)(2,1)S(1)} %copy-done, bf16[256,1024]{1,0:T(8,128)(2,1)} %collective-permute-done.7, s32[]{:T(128)S(6)} %select_n.139), kind=kOutput, calls=%fused_computation.8 | convolution fusion | flops 268566528 | bytes 2621444 | tf_op jit(solution)/shard_map/dot_general | solution.py:415
  38.0 1.5 %collective-permute-start.6 = (bf16[64,1024]{1,0:T(8,128)(2,1)S(1)}, bf16[64,1024]{1,0:T(8,128)(2,1)S(1)}, u32[]{:S(2)}, u32[]{:S(2)}) collective-permute-start(bf16[64,1024]{1,0:T(8,128)(2,1)S(1)} %dynamic-slice_convert_fusion.3), channel_id=1, source_target_pairs={{0,2},{1,3},{2,0},{3,1},{4,6},{5,7},{6,4},{7,5},{8,10},{9,11},{10,... | collective-permute-start | bytes 393224 | tf_op jit(solution)/shard_map/ppermute | solution.py:20
  40.2 4.7 %collective-permute-start.11 = (bf16[256,1024]{1,0:T(8,128)(2,1)}, bf16[256,1024]{1,0:T(8,128)(2,1)S(1)}, u32[]{:S(2)}, u32[]{:S(2)}) collective-permute-start(bf16[256,1024]{1,0:T(8,128)(2,1)} %collective-permute-done.10), channel_id=1, source_target_pairs={{0,4},{4,0},{8,12},{12,8},{1,5},{5,1},{9,13},{13,9},{2,6},{6,2},{1... | collective-permute-start | bytes 1572872 | tf_op jit(solution)/shard_map/ppermute | solution.py:20
  44.9 1.4 %convolution_add_fusion.2 = f32[128,1024]{1,0:T(8,128)S(1)} fusion(bf16[1024,1024]{1,0:T(8,128)(2,1)S(1)} %copy-done, bf16[128,1024]{1,0:T(8,128)(2,1)S(1)} %collective-permute-done.8, bf16[256,1024]{1,0:T(8,128)(2,1)} %collective-permute-done.7, s32[]{:T(128)S(6)} %select_n.138), kind=kOutput, calls=%fused_computation.5 | convolution fusion | flops 268697600 | bytes 3145732 | tf_op jit(solution)/shard_map/dot_general | solution.py:416
  46.4 1.6 %collective-permute-start.9 = (bf16[64,1024]{1,0:T(8,128)(2,1)S(1)}, bf16[64,1024]{1,0:T(8,128)(2,1)S(1)}, u32[]{:S(2)}, u32[]{:S(2)}) collective-permute-start(bf16[64,1024]{1,0:T(8,128)(2,1)S(1)} %dynamic-slice_convert_fusion.2), channel_id=1, source_target_pairs={{0,2},{1,3},{2,0},{3,1},{4,6},{5,7},{6,4},{7,5},{8,10},{9,11},{10,... | collective-permute-start | bytes 393224 | tf_op jit(solution)/shard_map/ppermute | solution.py:20
  48.0 4.4 %collective-permute-done.6 = bf16[64,1024]{1,0:T(8,128)(2,1)S(1)} collective-permute-done((bf16[64,1024]{1,0:T(8,128)(2,1)S(1)}, bf16[64,1024]{1,0:T(8,128)(2,1)S(1)}, u32[]{:S(2)}, u32[]{:S(2)}) %collective-permute-start.6) | collective-permute-done | bytes 131104 | tf_op jit(solution)/shard_map/ppermute | solution.py:20
  54.6 3.9 %collective-permute-start.15 = (bf16[256,1024]{1,0:T(8,128)(2,1)S(1)}, bf16[256,1024]{1,0:T(8,128)(2,1)S(1)}, u32[]{:S(2)}, u32[]{:S(2)}) collective-permute-start(bf16[256,1024]{1,0:T(8,128)(2,1)S(1)} %collective-permute-done.14), channel_id=1, source_target_pairs={{0,4},{4,0},{8,12},{12,8},{1,5},{5,1},{9,13},{13,9},{2,6},{6,2},{1... | collective-permute-start | bytes 1572872 | tf_op jit(solution)/shard_map/ppermute | solution.py:20
  58.5 1.2 %add.140 = bf16[256,1024]{1,0:T(8,128)(2,1)S(1)} add(bf16[256,1024]{1,0:T(8,128)(2,1)} %collective-permute-done.10, bf16[256,1024]{1,0:T(8,128)(2,1)S(1)} %collective-permute-done.11) | non-fusion elementwise | flops 262144 | bytes 1572864 | tf_op jit(solution)/shard_map/add | solution.py:471
  60.7 2.5 %collective-permute-start.4 = (bf16[1024,512]{1,0:T(8,128)(2,1)S(1)}, bf16[1024,512]{1,0:T(8,128)(2,1)S(1)}, u32[]{:S(2)}, u32[]{:S(2)}) collective-permute-start(bf16[1024,512]{1,0:T(8,128)(2,1)S(1)} %fusion.31), channel_id=1, source_target_pairs={{0,1},{2,3},{5,4},{7,6},{10,11},{8,9},{15,14},{13,12},{16,17},{18,... | collective-permute-start | bytes 3145736 | tf_op jit(solution)/shard_map/ppermute | solution.py:392
  63.2 7.3 %collective-permute-done.15 = bf16[256,1024]{1,0:T(8,128)(2,1)S(1)} collective-permute-done((bf16[256,1024]{1,0:T(8,128)(2,1)S(1)}, bf16[256,1024]{1,0:T(8,128)(2,1)S(1)}, u32[]{:S(2)}, u32[]{:S(2)}) %collective-permute-start.15) | collective-permute-done | bytes 524320 | tf_op jit(solution)/shard_map/ppermute | solution.py:20
  71.8 2.5 %collective-permute-start.13 = (bf16[64,1024]{1,0:T(8,128)(2,1)S(1)}, bf16[64,1024]{1,0:T(8,128)(2,1)S(1)}, u32[]{:S(2)}, u32[]{:S(2)}) collective-permute-start(bf16[64,1024]{1,0:T(8,128)(2,1)S(1)} %dynamic-slice_convert_fusion.1), channel_id=1, source_target_pairs={{0,2},{1,3},{2,0},{3,1},{4,6},{5,7},{6,4},{7,5},{8,10},{9,11},{10,... | collective-permute-start | bytes 393224 | tf_op jit(solution)/shard_map/ppermute | solution.py:20
  75.7 2.9 %collective-permute-done.13 = bf16[64,1024]{1,0:T(8,128)(2,1)S(1)} collective-permute-done((bf16[64,1024]{1,0:T(8,128)(2,1)S(1)}, bf16[64,1024]{1,0:T(8,128)(2,1)S(1)}, u32[]{:S(2)}, u32[]{:S(2)}) %collective-permute-start.13) | collective-permute-done | bytes 131104 | tf_op jit(solution)/shard_map/ppermute | solution.py:20
  79.4 1.8 %collective-permute-done.17 = bf16[64,1024]{1,0:T(8,128)(2,1)S(1)} collective-permute-done((bf16[64,1024]{1,0:T(8,128)(2,1)S(1)}, bf16[64,1024]{1,0:T(8,128)(2,1)S(1)}, u32[]{:S(2)}, u32[]{:S(2)}) %collective-permute-start.17) | collective-permute-done | bytes 131104 | tf_op jit(solution)/shard_map/ppermute | solution.py:20
  81.9 1.3 %add.124.un_ref = bf16[1024,512]{1,0:T(8,128)(2,1)} add(bf16[1024,512]{1,0:T(8,128)(2,1)S(1)} %fusion.31, bf16[1024,512]{1,0:T(8,128)(2,1)S(1)} %collective-permute-done.4) | non-fusion elementwise | flops 524288 | bytes 3145728 | tf_op jit(solution)/shard_map/add | solution.py:393
  83.2 3.3 %logit_part.1 = (f32[256,512]{1,0:T(8,128)}, f32[1,256]{1,0:T(1,128)}, f32[1,256]{1,0:T(1,128)}, bf16[72,512]{1,0:T(8,128)(2,1)}, bf16[72,512]{1,0:T(8,128)(2,1)}, /*index=5*/bf16[72,512]{1,0:T(8,128)(2,1)}) custom-call(s32[5]{0:T(128)} %stack.32.where_ref, bf16[1024,512]{1,0:T(8,128)(2,1)} %add.124.un_ref, s32[256,1]{1,0:T(8,128)} %copy.12.row_ref, ...), custom_call_target="tpu_custom_call" | custom-call | tf_op jit(solution)/shard_map/logit_part/pallas_call | solution.py:295
  86.5 1.8 %collective-permute-start.18 = (bf16[72,512]{1,0:T(8,128)(2,1)}, bf16[72,512]{1,0:T(8,128)(2,1)S(1)}, u32[]{:S(2)}, u32[]{:S(2)}) collective-permute-start(bf16[72,512]{1,0:T(8,128)(2,1)} %get-tuple-element.27), channel_id=1, source_target_pairs={{0,4},{4,0},{8,12},{12,8},{1,5},{5,1},{9,13},{13,9},{2,6},{6,2},{1... | collective-permute-start | bytes 221192 | tf_op jit(solution)/shard_map/ppermute | solution.py:20
  88.4 2.5 %collective-permute-start.20 = (bf16[72,512]{1,0:T(8,128)(2,1)}, bf16[72,512]{1,0:T(8,128)(2,1)S(1)}, u32[]{:S(2)}, u32[]{:S(2)}) collective-permute-start(bf16[72,512]{1,0:T(8,128)(2,1)} %get-tuple-element.29), channel_id=1, source_target_pairs={{0,12},{4,8},{8,4},{12,0},{1,13},{5,9},{9,5},{13,1},{2,14},{6,10},... | collective-permute-start | bytes 221192 | tf_op jit(solution)/shard_map/ppermute | solution.py:20
  91.6 5.0 %collective-permute-done.19.rest_1_ = bf16[72,512]{1,0:T(8,128)(2,1)S(1)} collective-permute-done((bf16[72,512]{1,0:T(8,128)(2,1)}, bf16[72,512]{1,0:T(8,128)(2,1)S(1)}, u32[]{:S(2)}, u32[]{:S(2)}) %collective-permute-start.19) | collective-permute-done | bytes 73760 | tf_op jit(solution)/shard_map/ppermute | solution.py:20
  97.2 2.1 %final_part.1.refs_0_ = f32[2,256]{1,0:T(2,128)} custom-call(s32[2]{0:T(128)} %pad_add_fusion.where_ref, f32[256,512]{1,0:T(8,128)} %get-tuple-element.24.log_ref, f32[1,256]{1,0:T(1,128)} %get-tuple-element.25.square_ref, f32[1,256]{1,0:T(1,128)} %get-tuple-element.26.score_ref, s32[64,1]{1,0:T(8,128)} %copy.15.nat_ref, s32[256,1]{1,0:T(8,128)} %copy.12.row_ref, ...), custom_call_target="tpu_custom_call" | custom-call | tf_op jit(solution)/shard_map/final_part/pallas_call | solution.py:348
  99.3 1.5 %collective-permute-start.22 = (f32[2,256]{1,0:T(2,128)}, f32[2,256]{1,0:T(2,128)S(1)}, u32[]{:S(2)}, u32[]{:S(2)}) collective-permute-start(f32[2,256]{1,0:T(2,128)} %final_part.1.refs_0_), channel_id=1, source_target_pairs={{0,2},{1,3},{2,0},{3,1},{4,6},{5,7},{6,4},{7,5},{8,10},{9,11},{10,... | collective-permute-start | bytes 6152 | tf_op jit(solution)/shard_map/ppermute | solution.py:20
  101.2 1.9 %collective-permute-done.22.refs_2_ = f32[2,256]{1,0:T(2,128)S(1)} collective-permute-done((f32[2,256]{1,0:T(2,128)}, f32[2,256]{1,0:T(2,128)S(1)}, u32[]{:S(2)}, u32[]{:S(2)}) %collective-permute-start.22) | collective-permute-done | bytes 2080 | tf_op jit(solution)/shard_map/ppermute | solution.py:20
  104.6 1.3 %total_part.1 = (f32[1,256]{1,0:T(1,128)}, f32[1,256]{1,0:T(1,128)}) custom-call(f32[2,256]{1,0:T(2,128)} %final_part.1.refs_0_, f32[2,256]{1,0:T(2,128)} %copy-done.10, f32[2,256]{1,0:T(2,128)} %copy-done.11, f32[2,256]{1,0:T(2,128)} %copy-done.12), custom_call_target="tpu_custom_call" | custom-call | tf_op jit(solution)/shard_map/total_part/pallas_call | solution.py:366
  (91 shorter events, 19.8 us)
Async XLA Ops:
  0.6 24.6 %copy-start = (bf16[1024,1024]{1,0:T(8,128)(2,1)S(1)}, bf16[1024,1024]{1,0:T(8,128)(2,1)}, u32[]{:S(2)}) copy-start(bf16[1024,1024]{1,0:T(8,128)(2,1)} %param.12) | copy-start | bytes 6291460
  0.6 15.5 %copy-start.13 = (s32[256]{0:T(256)S(1)}, s32[256]{0:T(256)}, u32[]{:S(2)}) copy-start(s32[256]{0:T(256)} %param.15) | copy-start | bytes 3076
  6.7 10.9 %collective-permute-start = (bf16[32,1024]{1,0:T(8,128)(2,1)}, bf16[32,1024]{1,0:T(8,128)(2,1)S(1)}, u32[]{:S(2)}, u32[]{:S(2)}) collective-permute-start(bf16[32,1024]{1,0:T(8,128)(2,1)} %get-tuple-element.20.rest_0_), channel_id=1, source_target_pairs={{0,4},{4,0},{8,12},{12,8},{1,5},{5,1},{9,13},{13,9},{2,6},{6,2},{1... | collective-permute-start | bytes 196616 | tf_op jit(solution)/shard_map/ppermute | solution.py:20
  9.8 7.8 %collective-permute-start.1 = (bf16[32,1024]{1,0:T(8,128)(2,1)}, bf16[32,1024]{1,0:T(8,128)(2,1)S(1)}, u32[]{:S(2)}, u32[]{:S(2)}) collective-permute-start(bf16[32,1024]{1,0:T(8,128)(2,1)} %get-tuple-element.20.rest_0_), channel_id=1, source_target_pairs={{0,8},{4,12},{8,0},{12,4},{1,9},{5,13},{9,1},{13,5},{2,10},{6,14},... | collective-permute-start | bytes 196616 | tf_op jit(solution)/shard_map/ppermute | solution.py:20
  12.4 6.3 %collective-permute-start.2 = (bf16[32,1024]{1,0:T(8,128)(2,1)}, bf16[32,1024]{1,0:T(8,128)(2,1)S(1)}, u32[]{:S(2)}, u32[]{:S(2)}) collective-permute-start(bf16[32,1024]{1,0:T(8,128)(2,1)} %get-tuple-element.20.rest_0_), channel_id=1, source_target_pairs={{0,12},{4,8},{8,4},{12,0},{1,13},{5,9},{9,5},{13,1},{2,14},{6,10},... | collective-permute-start | bytes 196616 | tf_op jit(solution)/shard_map/ppermute | solution.py:20
  17.6 1.1 %copy-start.6 = (bf16[32,1024]{1,0:T(8,128)(2,1)}, bf16[32,1024]{1,0:T(8,128)(2,1)S(1)}, u32[]{:S(2)}) copy-start(bf16[32,1024]{1,0:T(8,128)(2,1)S(1)} %collective-permute-done.rest_1_) | copy-start | bytes 196612
  23.5 8.7 %copy-start.1 = (bf16[1024,512]{1,0:T(8,128)(2,1)S(1)}, bf16[1024,512]{1,0:T(8,128)(2,1)}, u32[]{:S(2)}) copy-start(bf16[1024,512]{1,0:T(8,128)(2,1)} %param.14) | copy-start | bytes 3145732
  23.5 8.7 %copy-start.9 = (f32[1024]{0:T(1024)S(1)}, f32[1024]{0:T(1024)}, u32[]{:S(2)}) copy-start(f32[1024]{0:T(1024)} %param.13) | copy-start | bytes 12292
  23.5 12.5 %collective-permute-start.7 = (bf16[256,1024]{1,0:T(8,128)(2,1)}, bf16[256,1024]{1,0:T(8,128)(2,1)}, u32[]{:S(2)}, u32[]{:S(2)}) collective-permute-start(bf16[256,1024]{1,0:T(8,128)(2,1)} %carry_part.1), channel_id=1, source_target_pairs={{0,4},{4,0},{8,12},{12,8},{1,5},{5,1},{9,13},{13,9},{2,6},{6,2},{1... | collective-permute-start | bytes 1572872 | tf_op jit(solution)/shard_map/ppermute | solution.py:20
  23.6 16.6 %collective-permute-start.10 = (bf16[256,1024]{1,0:T(8,128)(2,1)}, bf16[256,1024]{1,0:T(8,128)(2,1)}, u32[]{:S(2)}, u32[]{:S(2)}) collective-permute-start(bf16[256,1024]{1,0:T(8,128)(2,1)} %carry_part.1), channel_id=1, source_target_pairs={{4,8},{8,4},{5,9},{9,5},{6,10},{10,6},{7,11},{11,7},{20,24},{24,20... | collective-permute-start | bytes 1572872 | tf_op jit(solution)/shard_map/ppermute | solution.py:467
  27.3 10.2 %collective-permute-start.5 = (bf16[128,1024]{1,0:T(8,128)(2,1)}, bf16[128,1024]{1,0:T(8,128)(2,1)S(1)}, u32[]{:S(2)}, u32[]{:S(2)}) collective-permute-start(bf16[128,1024]{1,0:T(8,128)(2,1)} %convolution_convert_fusion.3), channel_id=1, source_target_pairs={{0,1},{1,0},{2,3},{3,2},{4,5},{5,4},{6,7},{7,6},{8,9},{9,8},{10,11... | collective-permute-start | bytes 786440 | tf_op jit(solution)/shard_map/ppermute | solution.py:20
  32.2 5.3 %copy-start.2 = (bf16[256,1024]{1,0:T(8,128)(2,1)S(1)}, bf16[256,1024]{1,0:T(8,128)(2,1)}, u32[]{:S(2)}) copy-start(bf16[256,1024]{1,0:T(8,128)(2,1)} %carry_part.1) | copy-start | bytes 1572868
  32.5 27.7 %collective-permute-start.3 = (bf16[1024,512]{1,0:T(8,128)(2,1)S(1)}, bf16[1024,512]{1,0:T(8,128)(2,1)S(1)}, u32[]{:S(2)}, u32[]{:S(2)}) collective-permute-start(bf16[1024,512]{1,0:T(8,128)(2,1)S(1)} %fusion), channel_id=1, source_target_pairs={{0,2},{5,7},{10,8},{15,13},{16,18},{21,23},{26,24},{31,29}} | collective-permute-start | bytes 3145736 | tf_op jit(solution)/shard_map/ppermute | solution.py:392
  37.4 7.5 %collective-permute-start.8 = (bf16[128,1024]{1,0:T(8,128)(2,1)S(1)}, bf16[128,1024]{1,0:T(8,128)(2,1)S(1)}, u32[]{:S(2)}, u32[]{:S(2)}) collective-permute-start(bf16[128,1024]{1,0:T(8,128)(2,1)S(1)} %convolution_convert_fusion.2), channel_id=1, source_target_pairs={{0,1},{1,0},{2,3},{3,2},{4,5},{5,4},{6,7},{7,6},{8,9},{9,8},{10,11... | collective-permute-start | bytes 786440 | tf_op jit(solution)/shard_map/ppermute | solution.py:20
  38.0 14.4 %collective-permute-start.6 = (bf16[64,1024]{1,0:T(8,128)(2,1)S(1)}, bf16[64,1024]{1,0:T(8,128)(2,1)S(1)}, u32[]{:S(2)}, u32[]{:S(2)}) collective-permute-start(bf16[64,1024]{1,0:T(8,128)(2,1)S(1)} %dynamic-slice_convert_fusion.3), channel_id=1, source_target_pairs={{0,2},{1,3},{2,0},{3,1},{4,6},{5,7},{6,4},{7,5},{8,10},{9,11},{10,... | collective-permute-start | bytes 393224 | tf_op jit(solution)/shard_map/ppermute | solution.py:20
  39.5 15.0 %collective-permute-start.14 = (bf16[256,1024]{1,0:T(8,128)(2,1)}, bf16[256,1024]{1,0:T(8,128)(2,1)S(1)}, u32[]{:S(2)}, u32[]{:S(2)}) collective-permute-start(bf16[256,1024]{1,0:T(8,128)(2,1)} %collective-permute-done.7), channel_id=1, source_target_pairs={{4,8},{8,4},{5,9},{9,5},{6,10},{10,6},{7,11},{11,7},{20,24},{24,20... | collective-permute-start | bytes 1572872 | tf_op jit(solution)/shard_map/ppermute | solution.py:468
  40.2 18.2 %collective-permute-start.11 = (bf16[256,1024]{1,0:T(8,128)(2,1)}, bf16[256,1024]{1,0:T(8,128)(2,1)S(1)}, u32[]{:S(2)}, u32[]{:S(2)}) collective-permute-start(bf16[256,1024]{1,0:T(8,128)(2,1)} %collective-permute-done.10), channel_id=1, source_target_pairs={{0,4},{4,0},{8,12},{12,8},{1,5},{5,1},{9,13},{13,9},{2,6},{6,2},{1... | collective-permute-start | bytes 1572872 | tf_op jit(solution)/shard_map/ppermute | solution.py:20
  46.4 7.5 %collective-permute-start.9 = (bf16[64,1024]{1,0:T(8,128)(2,1)S(1)}, bf16[64,1024]{1,0:T(8,128)(2,1)S(1)}, u32[]{:S(2)}, u32[]{:S(2)}) collective-permute-start(bf16[64,1024]{1,0:T(8,128)(2,1)S(1)} %dynamic-slice_convert_fusion.2), channel_id=1, source_target_pairs={{0,2},{1,3},{2,0},{3,1},{4,6},{5,7},{6,4},{7,5},{8,10},{9,11},{10,... | collective-permute-start | bytes 393224 | tf_op jit(solution)/shard_map/ppermute | solution.py:20
  54.6 16.0 %collective-permute-start.15 = (bf16[256,1024]{1,0:T(8,128)(2,1)S(1)}, bf16[256,1024]{1,0:T(8,128)(2,1)S(1)}, u32[]{:S(2)}, u32[]{:S(2)}) collective-permute-start(bf16[256,1024]{1,0:T(8,128)(2,1)S(1)} %collective-permute-done.14), channel_id=1, source_target_pairs={{0,4},{4,0},{8,12},{12,8},{1,5},{5,1},{9,13},{13,9},{2,6},{6,2},{1... | collective-permute-start | bytes 1572872 | tf_op jit(solution)/shard_map/ppermute | solution.py:20
  60.2 11.1 %collective-permute-start.12 = (bf16[128,1024]{1,0:T(8,128)(2,1)S(1)}, bf16[128,1024]{1,0:T(8,128)(2,1)S(1)}, u32[]{:S(2)}, u32[]{:S(2)}) collective-permute-start(bf16[128,1024]{1,0:T(8,128)(2,1)S(1)} %convolution_convert_fusion.1), channel_id=1, source_target_pairs={{0,1},{1,0},{2,3},{3,2},{4,5},{5,4},{6,7},{7,6},{8,9},{9,8},{10,11... | collective-permute-start | bytes 786440 | tf_op jit(solution)/shard_map/ppermute | solution.py:20
  60.7 21.2 %collective-permute-start.4 = (bf16[1024,512]{1,0:T(8,128)(2,1)S(1)}, bf16[1024,512]{1,0:T(8,128)(2,1)S(1)}, u32[]{:S(2)}, u32[]{:S(2)}) collective-permute-start(bf16[1024,512]{1,0:T(8,128)(2,1)S(1)} %fusion.31), channel_id=1, source_target_pairs={{0,1},{2,3},{5,4},{7,6},{10,11},{8,9},{15,14},{13,12},{16,17},{18,... | collective-permute-start | bytes 3145736 | tf_op jit(solution)/shard_map/ppermute | solution.py:392
  71.2 3.1 %collective-permute-start.16 = (bf16[128,1024]{1,0:T(8,128)(2,1)S(1)}, bf16[128,1024]{1,0:T(8,128)(2,1)S(1)}, u32[]{:S(2)}, u32[]{:S(2)}) collective-permute-start(bf16[128,1024]{1,0:T(8,128)(2,1)S(1)} %convolution_convert_fusion), channel_id=1, source_target_pairs={{0,1},{1,0},{2,3},{3,2},{4,5},{5,4},{6,7},{7,6},{8,9},{9,8},{10,11... | collective-permute-start | bytes 786440 | tf_op jit(solution)/shard_map/ppermute | solution.py:20
  71.8 6.9 %collective-permute-start.13 = (bf16[64,1024]{1,0:T(8,128)(2,1)S(1)}, bf16[64,1024]{1,0:T(8,128)(2,1)S(1)}, u32[]{:S(2)}, u32[]{:S(2)}) collective-permute-start(bf16[64,1024]{1,0:T(8,128)(2,1)S(1)} %dynamic-slice_convert_fusion.1), channel_id=1, source_target_pairs={{0,2},{1,3},{2,0},{3,1},{4,6},{5,7},{6,4},{7,5},{8,10},{9,11},{10,... | collective-permute-start | bytes 393224 | tf_op jit(solution)/shard_map/ppermute | solution.py:20
  74.8 6.4 %collective-permute-start.17 = (bf16[64,1024]{1,0:T(8,128)(2,1)S(1)}, bf16[64,1024]{1,0:T(8,128)(2,1)S(1)}, u32[]{:S(2)}, u32[]{:S(2)}) collective-permute-start(bf16[64,1024]{1,0:T(8,128)(2,1)S(1)} %dynamic-slice_convert_fusion), channel_id=1, source_target_pairs={{0,2},{1,3},{2,0},{3,1},{4,6},{5,7},{6,4},{7,5},{8,10},{9,11},{10,... | collective-permute-start | bytes 393224 | tf_op jit(solution)/shard_map/ppermute | solution.py:20
  86.5 5.0 %collective-permute-start.18 = (bf16[72,512]{1,0:T(8,128)(2,1)}, bf16[72,512]{1,0:T(8,128)(2,1)S(1)}, u32[]{:S(2)}, u32[]{:S(2)}) collective-permute-start(bf16[72,512]{1,0:T(8,128)(2,1)} %get-tuple-element.27), channel_id=1, source_target_pairs={{0,4},{4,0},{8,12},{12,8},{1,5},{5,1},{9,13},{13,9},{2,6},{6,2},{1... | collective-permute-start | bytes 221192 | tf_op jit(solution)/shard_map/ppermute | solution.py:20
  88.4 8.2 %collective-permute-start.19 = (bf16[72,512]{1,0:T(8,128)(2,1)}, bf16[72,512]{1,0:T(8,128)(2,1)S(1)}, u32[]{:S(2)}, u32[]{:S(2)}) collective-permute-start(bf16[72,512]{1,0:T(8,128)(2,1)} %get-tuple-element.28), channel_id=1, source_target_pairs={{0,8},{4,12},{8,0},{12,4},{1,9},{5,13},{9,1},{13,5},{2,10},{6,14},... | collective-permute-start | bytes 221192 | tf_op jit(solution)/shard_map/ppermute | solution.py:20
  88.4 8.2 %collective-permute-start.20 = (bf16[72,512]{1,0:T(8,128)(2,1)}, bf16[72,512]{1,0:T(8,128)(2,1)S(1)}, u32[]{:S(2)}, u32[]{:S(2)}) collective-permute-start(bf16[72,512]{1,0:T(8,128)(2,1)} %get-tuple-element.29), channel_id=1, source_target_pairs={{0,12},{4,8},{8,4},{12,0},{1,13},{5,9},{9,5},{13,1},{2,14},{6,10},... | collective-permute-start | bytes 221192 | tf_op jit(solution)/shard_map/ppermute | solution.py:20
  91.6 5.0 %copy-start.3 = (bf16[72,512]{1,0:T(8,128)(2,1)}, bf16[72,512]{1,0:T(8,128)(2,1)S(1)}, u32[]{:S(2)}) copy-start(bf16[72,512]{1,0:T(8,128)(2,1)S(1)} %collective-permute-done.18.rest_0_) | copy-start | bytes 221188
  99.3 1.9 %collective-permute-start.21 = (f32[2,256]{1,0:T(2,128)}, f32[2,256]{1,0:T(2,128)S(1)}, u32[]{:S(2)}, u32[]{:S(2)}) collective-permute-start(f32[2,256]{1,0:T(2,128)} %final_part.1.refs_0_), channel_id=1, source_target_pairs={{0,1},{1,0},{2,3},{3,2},{4,5},{5,4},{6,7},{7,6},{8,9},{9,8},{10,11... | collective-permute-start | bytes 6152 | tf_op jit(solution)/shard_map/ppermute | solution.py:20
  99.3 3.8 %collective-permute-start.22 = (f32[2,256]{1,0:T(2,128)}, f32[2,256]{1,0:T(2,128)S(1)}, u32[]{:S(2)}, u32[]{:S(2)}) collective-permute-start(f32[2,256]{1,0:T(2,128)} %final_part.1.refs_0_), channel_id=1, source_target_pairs={{0,2},{1,3},{2,0},{3,1},{4,6},{5,7},{6,4},{7,5},{8,10},{9,11},{10,... | collective-permute-start | bytes 6152 | tf_op jit(solution)/shard_map/ppermute | solution.py:20
  100.7 3.2 %collective-permute-start.23 = (f32[2,256]{1,0:T(2,128)}, f32[2,256]{1,0:T(2,128)S(1)}, u32[]{:S(2)}, u32[]{:S(2)}) collective-permute-start(f32[2,256]{1,0:T(2,128)} %final_part.1.refs_0_), channel_id=1, source_target_pairs={{0,3},{1,2},{2,1},{3,0},{4,7},{5,6},{6,5},{7,4},{8,11},{9,10},{10,... | collective-permute-start | bytes 6152 | tf_op jit(solution)/shard_map/ppermute | solution.py:20
  101.2 2.8 %copy-start.10 = (f32[2,256]{1,0:T(2,128)}, f32[2,256]{1,0:T(2,128)S(1)}, u32[]{:S(2)}) copy-start(f32[2,256]{1,0:T(2,128)S(1)} %collective-permute-done.21.refs_1_) | copy-start | bytes 6148
  (6 other events, 4.4 us)

commit v3 on v2

--- a/solution.py
+++ b/solution.py
@@ -32,20 +32,49 @@
     return [filt_ref[stream, j : j + 1, cols] for j in range(3)]
 
 
-def local_kernel(steps, modes, spread, x_ref, filt_ref, mode_ref, nat_ref, y_ref, gate_ref, start_ref, msg_ref, xs, gs):
+def lane_slice(tile):
+    return pl.ds(pl.multiple_of(tile * LANES, LANES), LANES)
+
+
+def local_kernel(
+    steps, modes, x_any, filt_any, mode_any, nat_any, y_ref, gate_ref, start_ref, msg_ref,
+    filt_ref, mode_ref, held, nat_ref, xs, gs, sems, side_sems
+):
     rows = steps * SUBS
-    turn = pl.program_id(0)
-    ids = nat_ref[...]
-    ids = jnp.where(turn < spread, ids // 256, jnp.where(turn < 2 * spread, ids % 256, 0)).astype(F32)
-    for tile in range(x_ref.shape[2] // LANES):
-        cols = slice(tile * LANES, (tile + 1) * LANES)
+    tiles = held.shape[0]
+    spread = rows // LANES
+
+    def fetch(tile):
+        return pltpu.make_async_copy(x_any.at[:, :, lane_slice(tile)], held.at[tile], sems.at[tile])
+
+    sides = [
+        pltpu.make_async_copy(src, dst, side_sems.at[k])
+        for k, (src, dst) in enumerate(((filt_any, filt_ref), (mode_any, mode_ref), (nat_any, nat_ref)))
+    ]
+    fetch(0).start()
+    for side in sides:
+        side.start()
+
+    @pl.loop(1, tiles)
+    def _(tile):
+        fetch(tile).start()
+
+    for side in sides:
+        side.wait()
+
+    @pl.loop(0, tiles)
+    def _(tile):
+        cols = lane_slice(tile)
         sub = lax.broadcasted_iota(jnp.int32, (SUBS, LANES), 0)
-        for i in range(3):
-            xs[i] = x_ref[i, :, cols].astype(F32)
         decay = [jnp.broadcast_to(mode_ref[0, m : m + 1, cols], (SUBS, LANES)) for m in range(modes)]
         res = [jnp.broadcast_to(mode_ref[1, m : m + 1, cols], (SUBS, LANES)) for m in range(modes)]
         fall = [jnp.exp(-d) for d in decay]
         taps = [taps_of(filt_ref, i, cols) for i in range(3)]
+        ids = nat_ref[0:1, lane_slice(tile % spread)]
+        ids = jnp.where(tile < spread, ids // 256, jnp.where(tile < 2 * spread, ids % 256, 0)).astype(F32)
+        fetch(tile).wait()
+        for i in range(3):
+            xs[i] = held[tile, i].astype(F32)
 
         def at(i, t):
             return xs[i, pl.ds(t, SUBS, stride=steps), :]
@@ -82,43 +111,47 @@
         first = [xs[i, 0:2, :] for i in range(3)]
         last = [xs[i, rows - 2 : rows, :] for i in range(3)]
         edge = jnp.concatenate([first[1], first[2], last[1], last[2]], axis=0)
-        other = jnp.concatenate(
-            [last[0], first[0], ids[:, cols], jnp.zeros((3, LANES), F32)], axis=0
-        )
+        other = jnp.concatenate([last[0], first[0], ids, jnp.zeros((3, LANES), F32)], axis=0)
         msg_ref[:, cols] = jnp.concatenate([high, end - high, edge, other], axis=0).astype(BF16)
+
+
+SMALL = pltpu.CompilerParams(vmem_limit_bytes=16 * 2**20)
+
+
+def in_vmem():
+    return pl.BlockSpec(memory_space=pltpu.VMEM)
 
 
 def local_part(streams, filt, modes_t, native):
     rows, width = streams.shape[1:]
     modes = modes_t.shape[1]
     steps = rows // SUBS
-    block = 2 * LANES
+    tiles = width // LANES
     msg_rows = 2 * modes + 16
     return pl.pallas_call(
-        functools.partial(local_kernel, steps, modes, rows // block),
-        grid=(width // block,),
-        in_specs=[
-            pl.BlockSpec((3, rows, block), lambda c: (0, 0, c)),
-            pl.BlockSpec((3, 3, block), lambda c: (0, 0, c)),
-            pl.BlockSpec((2, modes, block), lambda c: (0, 0, c)),
-            pl.BlockSpec((1, block), lambda c: (0, c % (rows // block))),
+        functools.partial(local_kernel, steps, modes),
+        in_specs=[pl.BlockSpec(memory_space=pltpu.HBM)] * 4,
+        out_specs=[in_vmem()] * 6,
+        out_shape=[
+            pltpu.VMEM((rows, width), F32),
+            pltpu.VMEM((rows, width), BF16),
+            pltpu.VMEM((modes * SUBS, width), F32),
+            pltpu.VMEM((msg_rows, width), BF16),
+            pltpu.VMEM(filt.shape, F32),
+            pltpu.VMEM(modes_t.shape, F32),
         ],
-        out_specs=[
-            pl.BlockSpec((rows, block), lambda c: (0, c)),
-            pl.BlockSpec((rows, block), lambda c: (0, c)),
-            pl.BlockSpec((modes * SUBS, block), lambda c: (0, c)),
-            pl.BlockSpec((msg_rows, block), lambda c: (0, c)),
+        scratch_shapes=[
+            pltpu.VMEM((tiles, 3, rows, LANES), BF16),
+            pltpu.VMEM((1, rows), jnp.int32),
+            pltpu.VMEM((3, rows, LANES), F32),
+            pltpu.VMEM((rows, LANES), F32),
+            pltpu.SemaphoreType.DMA((tiles,)),
+            pltpu.SemaphoreType.DMA((3,)),
         ],
-        out_shape=[
-            jax.ShapeDtypeStruct((rows, width), F32),
-            jax.ShapeDtypeStruct((rows, width), BF16),
-            jax.ShapeDtypeStruct((modes * SUBS, width), F32),
-            jax.ShapeDtypeStruct((msg_rows, width), BF16),
-        ],
-        scratch_shapes=[pltpu.VMEM((3, rows, LANES), F32), pltpu.VMEM((rows, LANES), F32)],
+        compiler_params=SMALL,
         cost_estimate=pl.CostEstimate(flops=rows * width * 64, bytes_accessed=rows * width * 12, transcendentals=0),
         name="local_part",
-    )(streams, filt, modes_t, native[None, :])
+    )(*[pltpu.with_memory_space_constraint(v, pltpu.HBM) for v in (streams, filt, modes_t, native[None, :])])
 
 
 def carry_kernel(steps, modes, stacked, count, where_ref, filt_ref, mode_ref, y_ref, gate_ref, start_ref, *rest):
@@ -126,8 +159,10 @@
     me = where_ref[0]
     rows = steps * SUBS
     base = 2 * modes
-    for tile in range(y_ref.shape[1] // LANES):
-        cols = slice(tile * LANES, (tile + 1) * LANES)
+
+    @pl.loop(0, y_ref.shape[1] // LANES)
+    def _(tile):
+        cols = lane_slice(tile)
         sub = lax.broadcasted_iota(jnp.int32, (SUBS, LANES), 0)
         for k in range(count):
             if stacked:
@@ -206,33 +241,36 @@
     rows, width = y.shape
     modes = modes_t.shape[1]
     steps = rows // SUBS
-    block = 2 * LANES
     count = msgs[0].shape[0] if stacked else len(msgs)
     msg_rows = msgs[0].shape[-2]
-    if stacked:
-        msg_specs = [pl.BlockSpec((count, msg_rows, block), lambda c, w: (0, 0, c))]
-    else:
-        msg_specs = [pl.BlockSpec((msg_rows, block), lambda c, w: (0, c))] * count
     return pl.pallas_call(
         functools.partial(carry_kernel, steps, modes, stacked, count),
-        grid_spec=pltpu.PrefetchScalarGridSpec(
-            num_scalar_prefetch=1,
-            grid=(width // block,),
-            in_specs=[
-                pl.BlockSpec((3, 3, block), lambda c, w: (0, 0, c)),
-                pl.BlockSpec((2, modes, block), lambda c, w: (0, 0, c)),
-                pl.BlockSpec((rows, block), lambda c, w: (0, c)),
-                pl.BlockSpec((rows, block), lambda c, w: (0, c)),
-                pl.BlockSpec((modes * SUBS, block), lambda c, w: (0, c)),
-            ]
-            + msg_specs,
-            out_specs=pl.BlockSpec((rows, block), lambda c, w: (0, c)),
-            scratch_shapes=[pltpu.VMEM((count, msg_rows, LANES), F32), pltpu.VMEM((rows, LANES), F32)],
-        ),
+        in_specs=[pl.BlockSpec(memory_space=pltpu.SMEM)] + [in_vmem()] * (5 + len(msgs)),
+        out_specs=in_vmem(),
         out_shape=jax.ShapeDtypeStruct((rows, width), BF16),
+        scratch_shapes=[pltpu.VMEM((count, msg_rows, LANES), F32), pltpu.VMEM((rows, LANES), F32)],
+        compiler_params=SMALL,
         cost_estimate=pl.CostEstimate(flops=rows * width * 32, bytes_accessed=rows * width * 8, transcendentals=0),
         name="carry_part",
-    )(me, filt, modes_t, y, gate, start, *msgs)
+    )(me, *[pltpu.with_memory_space_constraint(v, pltpu.VMEM) for v in (filt, modes_t, y, gate, start, *msgs)])
+
+
+def bring_kernel(later_any, src_any, out_ref, sem):
+    copy = pltpu.make_async_copy(src_any, out_ref, sem)
+    copy.start()
+    copy.wait()
+
+
+def bring(later, weight):
+    return pl.pallas_call(
+        bring_kernel,
+        in_specs=[pl.BlockSpec(memory_space=pl.ANY), pl.BlockSpec(memory_space=pltpu.HBM)],
+        out_specs=in_vmem(),
+        out_shape=pltpu.VMEM(weight.shape, weight.dtype),
+        scratch_shapes=[pltpu.SemaphoreType.DMA],
+        compiler_params=SMALL,
+        name="bring",
+    )(later, pltpu.with_memory_space_constraint(weight, pltpu.HBM))
 
 
 def as_row(col, width):
@@ -254,7 +292,7 @@
     return jnp.concatenate([both, jnp.zeros((2, width - row.shape[1]), F32)], axis=1)
 
 
-def logit_kernel(share, peers, where_ref, un_ref, row_ref, id_ref, nat_ref, *rest):
+def logit_kernel(share, peers, where_ref, un_ref, gain_ref, row_ref, id_ref, nat_ref, *rest):
     slots = where_ref.shape[0] - 1
     slot_refs, rest = rest[:slots], rest[slots:]
     part_ref, square_ref, score_ref = rest[:3]
@@ -265,7 +303,7 @@
     total = values.shape[0]
     square = as_row(jnp.sum(values * values, axis=1, keepdims=True), total)
     square_ref[...] = square
-    part = jnp.dot(values.astype(BF16), un_ref[...], preferred_element_type=F32)
+    part = jnp.dot((values * gain_ref[...]).astype(BF16), un_ref[...], preferred_element_type=F32)
     part_ref[...] = part
     muts = row_ref.shape[0]
     vocab = part.shape[1]
@@ -286,7 +324,7 @@
             msg_refs[k - 1][share : share + 8, :] = extra
 
 
-def logit_part(where, slots, un, mut_row, mut_id, mut_nat, peers):
+def logit_part(where, slots, un, gains, mut_row, mut_id, mut_nat, peers):
     share, wide = slots[0].shape
     total = share * len(slots)
     vocab = un.shape[1]
@@ -294,7 +332,7 @@
     whole = pl.BlockSpec(memory_space=pltpu.VMEM)
     return pl.pallas_call(
         functools.partial(logit_kernel, share, peers),
-        in_specs=[pl.BlockSpec(memory_space=pltpu.SMEM)] + [whole] * (4 + len(slots)),
+        in_specs=[pl.BlockSpec(memory_space=pltpu.SMEM)] + [whole] * (5 + len(slots)),
         out_specs=[whole] * (3 + peers),
         out_shape=[
             jax.ShapeDtypeStruct((total, vocab), F32),
@@ -303,8 +341,9 @@
         ]
         + [jax.ShapeDtypeStruct((share + 8, vocab), BF16)] * peers,
         scratch_shapes=[pltpu.VMEM((total, wide), F32)],
+        compiler_params=SMALL,
         name="logit_part",
-    )(where, un, mut_row, mut_id, mut_nat, *slots)
+    )(where, un, gains, mut_row, mut_id, mut_nat, *slots)
 
 
 def final_kernel(feats, where_ref, log_ref, square_ref, score_ref, nat_ref, row_ref, *rest):
@@ -350,6 +389,7 @@
         in_specs=[pl.BlockSpec(memory_space=pltpu.SMEM)] + [whole] * (5 + len(msgs)),
         out_specs=whole,
         out_shape=jax.ShapeDtypeStruct((2, width), F32),
+        compiler_params=SMALL,
         name="final_part",
     )(where, logits, squares, scores, nat, mut_row, *msgs)
 
@@ -368,32 +408,44 @@
         in_specs=[whole] * len(pieces),
         out_specs=[whole] * 2,
         out_shape=[jax.ShapeDtypeStruct((1, rows), F32), jax.ShapeDtypeStruct((1, muts), F32)],
+        compiler_params=SMALL,
         name="total_part",
     )(*pieces)
 
 
-def spread_unembed(unembed, norm_gain, rows_wanted):
+def owners(rows_held, rows_wanted):
+    return [i * rows_wanted // rows_held for i in range(lax.axis_size("ctx"))]
+
+
+def hand_on(value, owner, bit, holders):
     count, shards = lax.axis_size("ctx"), lax.axis_size("mp")
-    scaled = (unembed.astype(F32) * norm_gain[:, None]).astype(BF16)
+    pairs = [(i * shards + (owner[i] ^ h), i * shards + (owner[i] ^ h ^ bit)) for i in range(count) for h in holders]
+    return lax.ppermute(value, ("ctx", "mp"), pairs)
+
+
+def feature_rows(unembed, norm_gain, rows_wanted, z, m, first_move):
+    shards = lax.axis_size("mp")
     held = unembed.shape[0]
-    z, m = lax.axis_index("ctx"), lax.axis_index("mp")
     if held % rows_wanted != 0:
-        every = lax.all_gather(scaled, "mp", axis=0, tiled=True)
-        return lax.dynamic_slice_in_dim(every, z * rows_wanted, rows_wanted, 0)
+        unembed = lax.all_gather(unembed, "mp", axis=0, tiled=True)
+        norm_gain = lax.all_gather(norm_gain, "mp", axis=0, tiled=True)
+        return tuple(lax.dynamic_slice_in_dim(v, z * rows_wanted, rows_wanted, 0) for v in (unembed, norm_gain))
+    owner = owners(held, rows_wanted)
     ratio = held // rows_wanted
-    owner = [i // ratio for i in range(count)]
-    piece = lax.dynamic_slice_in_dim(scaled, (z % ratio) * rows_wanted, rows_wanted, 0)
-    value = jnp.where(m == z // ratio, piece, jnp.zeros_like(piece))
-    bit, holders = shards // 2, [0]
-    while bit:
-        pairs = [
-            (i * shards + (owner[i] ^ h), i * shards + (owner[i] ^ h ^ bit)) for i in range(count) for h in holders
-        ]
-        moved = lax.ppermute(value, ("ctx", "mp"), pairs)
-        value = value + moved
-        holders = holders + [h ^ bit for h in holders]
-        bit //= 2
-    return value
+    place = m ^ (z // ratio)
+    result = []
+    for value, moved in ((unembed, first_move), (norm_gain, None)):
+        value = lax.dynamic_slice_in_dim(value, (z % ratio) * rows_wanted, rows_wanted, 0)
+        bit, holders, known = shards // 2, [0], place == 0
+        while bit:
+            if moved is None:
+                moved = hand_on(value, owner, bit, holders)
+            value = jnp.where(known, value, moved)
+            holders = holders + [h ^ bit for h in holders]
+            known = sum((place == h).astype(jnp.int32) for h in holders) > 0
+            bit, moved = bit // 2, None
+        result.append(value)
+    return tuple(result)
 
 
 def split_half(value, upper):
@@ -403,9 +455,8 @@
     return keep, send
 
 
-def project(gated, weight):
+def project(gated, weight, m):
     shards = lax.axis_size("mp")
-    m = lax.axis_index("mp")
     bit = 1
     value = None
     while bit < shards:
@@ -416,14 +467,14 @@
             keep = jnp.dot(keep, weight, preferred_element_type=F32)
         else:
             sent = send.astype(BF16)
-        value = keep + swap(sent, "mp", bit).astype(F32)
+        got = swap(sent, "mp", bit)
+        value = keep + got.astype(F32)
         bit *= 2
     return jnp.dot(gated, weight, preferred_element_type=F32) if value is None else value
 
 
-def row_piece():
+def row_piece(m):
     shards = lax.axis_size("mp")
-    m = lax.axis_index("mp")
     piece, bit = 0, 1
     while bit < shards:
         piece = piece * 2 + (m // bit) % 2
@@ -438,24 +489,35 @@
     quick = count == 4
     modes_t = jnp.swapaxes(mode_params, 1, 2)
     me = z.astype(jnp.int32)[None]
-    y, gate, start, msg = local_part(streams, short_filter, modes_t, native)
+    y, gate, start, msg, filt, modes_t = local_part(streams, short_filter, modes_t, native)
     nat_at = 2 * mode_params.shape[2] + 12
     if quick:
-        msgs = [msg] + [swap(msg, "ctx", k) for k in range(1, count)]
-        gated = carry_part(me, short_filter, modes_t, y, gate, start, msgs, False)
-        nat_rows = jnp.stack([msgs[k][nat_at, : 2 * rows] for k in range(count)])
-        nat_rows = nat_rows[z ^ jnp.arange(count)]
+        msgs = [msg]
+        for k in range(1, count):
+            msgs.append(swap(msg, "ctx", k))
+        width_out = out_weight.shape[1]
+        moved = None
+        if unembed.shape[0] == width_out and shards > 1:
+            moved = hand_on(unembed, owners(width_out, width_out), shards // 2, [0])
+        gated = carry_part(me, filt, modes_t, y, gate, start, msgs, False)
+        nat_rows = msgs
     else:
+        moved = None
         every = lax.all_gather(msg, "ctx")
-        gated = carry_part(me, short_filter, modes_t, y, gate, start, [every], True)
-        nat_rows = every[:, nat_at, : 2 * rows]
+        gated = carry_part(me, filt, modes_t, y, gate, start, [every], True)
+        nat_rows = every
+    gated, nat_rows, native, mut_pos, mut_ids, z, m, norm_gain = lax.optimization_barrier(
+        (gated, nat_rows, native, mut_pos, mut_ids, z, lax.axis_index("mp"), norm_gain)
+    )
+    if quick:
+        nat_rows = jnp.stack([nat_rows[k][nat_at, : 2 * rows] for k in range(count)])[z ^ jnp.arange(count)]
+    else:
+        nat_rows = nat_rows[:, nat_at, : 2 * rows]
     nat_rows = nat_rows.astype(jnp.int32)
     nat_all = (nat_rows[:, :rows] * 256 + nat_rows[:, rows:]).reshape(-1)
 
-    held, unembed, norm_gain = lax.optimization_barrier((gated, unembed, norm_gain)) if quick else (gated, unembed, norm_gain)
-    gated = held
-    un = spread_unembed(unembed, norm_gain, out_weight.shape[1])
-    piece = row_piece()
+    un, gains = feature_rows(unembed, norm_gain, out_weight.shape[1], z, m, moved)
+    piece = row_piece(m)
     share = rows // shards
     block, inner = mut_pos // rows, mut_pos % rows
     mut_row = jnp.where(inner // share == piece, block * share + inner % share, -1)[:, None]
@@ -478,13 +540,16 @@
         blocks = [every[b] for b in range(count)]
         where = list(range(count))
     where = jnp.stack([jnp.asarray(w, jnp.int32) for w in where + [z]])
+    if quick:
+        out_weight = bring(gated, out_weight)
     slots = []
     for part in blocks:
-        slots.append(project(part, out_weight))
+        slots.append(project(part, out_weight, m))
     peers = count - 1 if quick else 0
-    part, squares, scores, *msgs = logit_part(where, slots, un, mut_row, mut_ids[:, None], mut_nat, peers)
+    part, squares, scores, *msgs = logit_part(where, slots, un, gains[None, :], mut_row, mut_ids[:, None], mut_nat, peers)
     if quick:
-        msgs = [swap(msgs[k - 1], "ctx", k) for k in range(1, count)]
+        for k in range(1, count):
+            msgs[k - 1] = swap(msgs[k - 1], "ctx", k)
     else:
         part = lax.psum_scatter(part, "ctx", scatter_dimension=0, tiled=True)
         squares = lax.psum(squares, "ctx")

time: 107 us -> 95.4 us (0.89)
  starting transfers between devices: 35.7 us -> 44.4 us
  local copies, waits for them, and re-layouts: 11.3 us -> 2.75 us
  Pallas kernels: 16.9 us -> 10.9 us
  other arithmetic: 7.8 us -> 1.94 us
  waiting for transfers between devices: 26.1 us -> 27.6 us
    ppermute x2 -> x4, starting transfers between devices: 5.92 us -> 11.1 us  [hand_on(): return lax.ppermute(value, ('ctx', 'mp'), pairs)]
    add x6 -> x4, other arithmetic: 4.68 us -> 0.11 us  [project(): value = keep + got.astype(F32)]
    ppermute x20, starting transfers between devices: 27.5 us -> 31.1 us  [swap(): return lax.ppermute(value, axis, [(i, i ^ bit) for i in range(count)])]
    slice x4, local copies, waits for them, and re-layouts: 2.87 us -> 0.03 us  [body(): nat_rows[k][nat_at, :2 * rows]]
    pallas_call x1, Pallas kernels: 4.22 us -> 1.54 us  [carry_part(): pl.pallas_call(functools.partial(carry_kernel, steps, modes, stacked, cou...]
    unnamed x29 -> x11, local copies, waits for them, and re-layouts: 1.87 us -> 0.03 us
    pallas_call x1, Pallas kernels: 3.29 us -> 1.5 us  [logit_part(): pl.pallas_call(functools.partial(logit_kernel, share, peers), in_specs=[p...]
    broadcast_in_dim x1, local copies, waits for them, and re-layouts: 1.48 us -> 0.13 us  [body(): mut_ids[:, None]]
  transfers between devices with their start and end apart: 24 -> 26, of which waited for: 9 -> 12; matrix products, arithmetic and copies ran while one was open for 22% -> 11% of each run, Pallas kernels for 0% -> 3%
where the time goes in v3:
time: 95.4 us; the launch traced here: 95 us
  starting transfers between devices  44.4 us (47%)
  waiting for transfers between devices  27.6 us (29%)
  Pallas kernels  10.9 us (11%)
  matrix products  6.21 us (7%)
  local copies, waits for them, and re-layouts  2.75 us (3%)
  other arithmetic  1.94 us (2%)
  between operations  1.21 us (1%)
    ppermute x20, starting transfers between devices, swap(): return lax.ppermute(value, axis, [(i, i ^ bit) for i in range(count)])  31.1 us
    ppermute x20, waiting for transfers between devices, swap(): return lax.ppermute(value, axis, [(i, i ^ bit) for i in range(count)])  26.4 us
    ppermute x4, starting transfers between devices, hand_on(): return lax.ppermute(value, ('ctx', 'mp'), pairs)  11.1 us
    pallas_call x1, Pallas kernels, local_part(): pl.pallas_call(functools.partial(local_kernel, steps, modes), in_specs=[p...  4.8 us
    dot_general x4, matrix products, project(): sent = jnp.dot(send, weight, preferred_element_type=F32).astype(BF16)  3.46 us
    dot_general x4, matrix products, project(): keep = jnp.dot(keep, weight, preferred_element_type=F32)  2.75 us
  transfers between devices with their start and end apart: 26, of which 12 were waited for; matrix products, arithmetic and copies ran while one was open for 11% of the time, Pallas kernels for 3%

profile of v3, /device:TPU:0, one launch (start us, length us, event | category | flops | bytes accessed | tf_op | source)
XLA Modules:
  0.0 95.0 jit_solution(609093303201855744)
XLA Ops:
  0.6 4.8 %local_part.1 = (f32[256,1024]{1,0:T(8,128)S(1)}, bf16[256,1024]{1,0:T(8,128)(2,1)S(1)}, f32[64,1024]{1,0:T(8,128)S(1)}, bf16[32,1024]{1,0:T(8,128)(2,1)S(1)}, f...) custom-call(bf16[3,256,1024]{2,1,0:T(8,128)(2,1)} %x_any.1, f32[3,3,1024]{2,1,0:T(4,128)} %filt_any.1, ...), custom_call_target="tpu_custom_call" | custom-call | flops 16777216 | bytes 3145728 | tf_op jit(solution)/shard_map/local_part/pallas_call | solution.py:131
  5.4 3.1 %collective-permute-start = (bf16[32,1024]{1,0:T(8,128)(2,1)S(1)}, bf16[32,1024]{1,0:T(8,128)(2,1)S(1)}, u32[]{:S(2)}, u32[]{:S(2)}) collective-permute-start(bf16[32,1024]{1,0:T(8,128)(2,1)S(1)} %get-tuple-element.38.rest_0_), channel_id=1, source_target_pairs={{0,4},{4,0},{8,12},{12,8},{1,5},{5,1},{9,13},{13,9},{2,6},{6,2},{1... | collective-permute-start | bytes 196616 | tf_op jit(solution)/shard_map/ppermute | solution.py:20
  8.6 2.6 %collective-permute-start.1 = (bf16[32,1024]{1,0:T(8,128)(2,1)S(1)}, bf16[32,1024]{1,0:T(8,128)(2,1)S(1)}, u32[]{:S(2)}, u32[]{:S(2)}) collective-permute-start(bf16[32,1024]{1,0:T(8,128)(2,1)S(1)} %get-tuple-element.38.rest_0_), channel_id=1, source_target_pairs={{0,8},{4,12},{8,0},{12,4},{1,9},{5,13},{9,1},{13,5},{2,10},{6,14},... | collective-permute-start | bytes 196616 | tf_op jit(solution)/shard_map/ppermute | solution.py:20
  11.2 4.6 %collective-permute-start.3 = (bf16[1024,512]{1,0:T(8,128)(2,1)}, bf16[1024,512]{1,0:T(8,128)(2,1)}, u32[]{:S(2)}, u32[]{:S(2)}) collective-permute-start(bf16[1024,512]{1,0:T(8,128)(2,1)} %param.14), channel_id=1, source_target_pairs={{0,2},{5,7},{10,8},{15,13},{16,18},{21,23},{26,24},{31,29}} | collective-permute-start | bytes 3145736 | tf_op jit(solution)/shard_map/ppermute | solution.py:423
  15.8 1.4 %collective-permute-done.2.rest_3_ = bf16[32,1024]{1,0:T(8,128)(2,1)S(1)} collective-permute-done((bf16[32,1024]{1,0:T(8,128)(2,1)S(1)}, bf16[32,1024]{1,0:T(8,128)(2,1)S(1)}, u32[]{:S(2)}, u32[]{:S(2)}) %collective-permute-start.2) | collective-permute-done | bytes 65568 | tf_op jit(solution)/shard_map/ppermute | solution.py:20
  17.2 1.5 %carry_part.1.later_any = bf16[256,1024]{1,0:T(8,128)(2,1)S(1)} custom-call(s32[1]{0:T(128)} %bitcast.where_ref, f32[3,3,1024]{2,1,0:T(4,128)S(1)} %get-tuple-element.27.filt_ref, f32[2,8,1024]{2,1,0:T(8,128)S(1)} %get-tuple-element.28.mode_ref, f32[256,1024]{1,0:T(8,128)S(1)} %get-tuple-element.29.y_ref, bf16[256,1024]{1,0:T(8,128)(2,1)S(1)} %get-tuple-element.30.gate_ref, ...), custom_call_target="tpu_custom_call" | custom-call | flops 8388608 | bytes 2097152 | tf_op jit(solution)/shard_map/carry_part/pallas_call | solution.py:246
  18.9 1.5 %collective-permute-start.12 = (bf16[256,1024]{1,0:T(8,128)(2,1)S(1)}, bf16[256,1024]{1,0:T(8,128)(2,1)}, u32[]{:S(2)}, u32[]{:S(2)}) collective-permute-start(bf16[256,1024]{1,0:T(8,128)(2,1)S(1)} %carry_part.1.later_any), channel_id=1, source_target_pairs={{4,8},{8,4},{5,9},{9,5},{6,10},{10,6},{7,11},{11,7},{20,24},{24,20... | collective-permute-start | bytes 1572872 | tf_op jit(solution)/shard_map/ppermute | solution.py:529
  20.3 1.6 %bring.1 = bf16[1024,1024]{1,0:T(8,128)(2,1)S(1)} custom-call(bf16[256,1024]{1,0:T(8,128)(2,1)S(1)} %carry_part.1.later_any, bf16[1024,1024]{1,0:T(8,128)(2,1)} %src_any.1), custom_call_target="tpu_custom_call" | custom-call | tf_op jit(solution)/shard_map/bring/pallas_call | solution.py:265
  22.0 1.2 %convolution_convert_fusion.3 = bf16[128,1024]{1,0:T(8,128)(2,1)} fusion(bf16[1024,1024]{1,0:T(8,128)(2,1)S(1)} %bring.1, bf16[256,1024]{1,0:T(8,128)(2,1)S(1)} %carry_part.1.later_any, s32[]{:T(128)S(6)} %select_n.168), kind=kOutput, calls=%fused_computation.9 | convolution fusion | flops 268566528 | bytes 2621444 | tf_op jit(solution)/shard_map/dot_general | solution.py:466
  23.9 3.4 %collective-permute-start.5 = (f32[1024]{0:T(1024)S(1)}, f32[1024]{0:T(1024)S(1)}, u32[]{:S(2)}, u32[]{:S(2)}) collective-permute-start(f32[1024]{0:T(1024)S(1)} %copy-done.1), channel_id=1, source_target_pairs={{0,2},{5,7},{10,8},{15,13},{16,18},{21,23},{26,24},{31,29}} | collective-permute-start | bytes 12296 | tf_op jit(solution)/shard_map/ppermute | solution.py:423
  27.4 1.2 %collective-permute-done.5 = f32[1024]{0:T(1024)S(1)} collective-permute-done((f32[1024]{0:T(1024)S(1)}, f32[1024]{0:T(1024)S(1)}, u32[]{:S(2)}, u32[]{:S(2)}) %collective-permute-start.5) | collective-permute-done | bytes 4128 | tf_op jit(solution)/shard_map/ppermute | solution.py:423
  28.6 1.3 %collective-permute-start.6 = (f32[1024]{0:T(1024)S(1)}, f32[1024]{0:T(1024)S(1)}, u32[]{:S(2)}, u32[]{:S(2)}) collective-permute-start(f32[1024]{0:T(1024)S(1)} %broadcast_select_fusion.2), channel_id=1, source_target_pairs={{0,1},{2,3},{5,4},{7,6},{10,11},{8,9},{15,14},{13,12},{16,17},{18,... | collective-permute-start | bytes 12296 | tf_op jit(solution)/shard_map/ppermute | solution.py:423
  30.0 1.4 %gather_fusion.1 = s32[256]{0:T(256)S(1)} fusion(s32[1024]{0:T(1024)S(1)} %bitcast.30, s32[1024]{0:T(1024)S(1)} %pad_clamp_fusion), kind=kCustom, calls=%fused_computation.1 | custom fusion | bytes 3072 | tf_op jit(solution)/shard_map/gather | solution.py:524
  32.0 1.4 %convolution_convert_fusion.2 = bf16[128,1024]{1,0:T(8,128)(2,1)S(1)} fusion(bf16[1024,1024]{1,0:T(8,128)(2,1)S(1)} %bring.1, bf16[256,1024]{1,0:T(8,128)(2,1)} %collective-permute-done.9, s32[]{:T(128)S(6)} %select_n.168), kind=kOutput, calls=%fused_computation.8 | convolution fusion | flops 268566528 | bytes 2621444 | tf_op jit(solution)/shard_map/dot_general | solution.py:466
  34.0 2.3 %collective-permute-start.8 = (bf16[64,1024]{1,0:T(8,128)(2,1)S(1)}, bf16[64,1024]{1,0:T(8,128)(2,1)S(1)}, u32[]{:S(2)}, u32[]{:S(2)}) collective-permute-start(bf16[64,1024]{1,0:T(8,128)(2,1)S(1)} %dynamic-slice_convert_fusion.3), channel_id=1, source_target_pairs={{0,2},{1,3},{2,0},{3,1},{4,6},{5,7},{6,4},{7,5},{8,10},{9,11},{10,... | collective-permute-start | bytes 393224 | tf_op jit(solution)/shard_map/ppermute | solution.py:20
  37.1 1.4 %convolution_add_fusion.2 = f32[128,1024]{1,0:T(8,128)S(1)} fusion(bf16[1024,1024]{1,0:T(8,128)(2,1)S(1)} %bring.1, bf16[128,1024]{1,0:T(8,128)(2,1)S(1)} %collective-permute-done.10, bf16[256,1024]{1,0:T(8,128)(2,1)} %collective-permute-done.9, s32[]{:T(128)S(6)} %select_n.167), kind=kOutput, calls=%fused_computation.4 | convolution fusion | flops 268697600 | bytes 3145732 | tf_op jit(solution)/shard_map/dot_general | solution.py:467
  38.8 1.7 %collective-permute-done.8 = bf16[64,1024]{1,0:T(8,128)(2,1)S(1)} collective-permute-done((bf16[64,1024]{1,0:T(8,128)(2,1)S(1)}, bf16[64,1024]{1,0:T(8,128)(2,1)S(1)}, u32[]{:S(2)}, u32[]{:S(2)}) %collective-permute-start.8) | collective-permute-done | bytes 131104 | tf_op jit(solution)/shard_map/ppermute | solution.py:20
  40.6 4.4 %collective-permute-start.13 = (bf16[256,1024]{1,0:T(8,128)(2,1)}, bf16[256,1024]{1,0:T(8,128)(2,1)S(1)}, u32[]{:S(2)}, u32[]{:S(2)}) collective-permute-start(bf16[256,1024]{1,0:T(8,128)(2,1)} %collective-permute-done.12), channel_id=1, source_target_pairs={{0,4},{4,0},{8,12},{12,8},{1,5},{5,1},{9,13},{13,9},{2,6},{6,2},{1... | collective-permute-start | bytes 1572872 | tf_op jit(solution)/shard_map/ppermute | solution.py:20
  45.0 10.1 %collective-permute-start.17 = (bf16[256,1024]{1,0:T(8,128)(2,1)S(1)}, bf16[256,1024]{1,0:T(8,128)(2,1)S(1)}, u32[]{:S(2)}, u32[]{:S(2)}) collective-permute-start(bf16[256,1024]{1,0:T(8,128)(2,1)S(1)} %collective-permute-done.16), channel_id=1, source_target_pairs={{0,4},{4,0},{8,12},{12,8},{1,5},{5,1},{9,13},{13,9},{2,6},{6,2},{1... | collective-permute-start | bytes 1572872 | tf_op jit(solution)/shard_map/ppermute | solution.py:20
  55.3 1.8 %collective-permute-start.4 = (bf16[1024,512]{1,0:T(8,128)(2,1)S(1)}, bf16[1024,512]{1,0:T(8,128)(2,1)S(1)}, u32[]{:S(2)}, u32[]{:S(2)}) collective-permute-start(bf16[1024,512]{1,0:T(8,128)(2,1)S(1)} %broadcast_select_fusion), channel_id=1, source_target_pairs={{0,1},{2,3},{5,4},{7,6},{10,11},{8,9},{15,14},{13,12},{16,17},{18,... | collective-permute-start | bytes 3145736 | tf_op jit(solution)/shard_map/ppermute | solution.py:423
  57.1 0.9 collective-permute-done.13
  57.9 1.2 %add.139 = bf16[256,1024]{1,0:T(8,128)(2,1)S(1)} add(bf16[256,1024]{1,0:T(8,128)(2,1)} %collective-permute-done.12, bf16[256,1024]{1,0:T(8,128)(2,1)S(1)} %collective-permute-done.13) | non-fusion elementwise | flops 262144 | bytes 1572864 | tf_op jit(solution)/shard_map/add | solution.py:533
  59.7 8.4 %collective-permute-done.17 = bf16[256,1024]{1,0:T(8,128)(2,1)S(1)} collective-permute-done((bf16[256,1024]{1,0:T(8,128)(2,1)S(1)}, bf16[256,1024]{1,0:T(8,128)(2,1)S(1)}, u32[]{:S(2)}, u32[]{:S(2)}) %collective-permute-start.17) | collective-permute-done | bytes 524320 | tf_op jit(solution)/shard_map/ppermute | solution.py:20
  70.9 1.1 %collective-permute-start.19 = (bf16[64,1024]{1,0:T(8,128)(2,1)S(1)}, bf16[64,1024]{1,0:T(8,128)(2,1)S(1)}, u32[]{:S(2)}, u32[]{:S(2)}) collective-permute-start(bf16[64,1024]{1,0:T(8,128)(2,1)S(1)} %dynamic-slice_convert_fusion), channel_id=1, source_target_pairs={{0,2},{1,3},{2,0},{3,1},{4,6},{5,7},{6,4},{7,5},{8,10},{9,11},{10,... | collective-permute-start | bytes 393224 | tf_op jit(solution)/shard_map/ppermute | solution.py:20
  72.0 3.8 %collective-permute-done.15 = bf16[64,1024]{1,0:T(8,128)(2,1)S(1)} collective-permute-done((bf16[64,1024]{1,0:T(8,128)(2,1)S(1)}, bf16[64,1024]{1,0:T(8,128)(2,1)S(1)}, u32[]{:S(2)}, u32[]{:S(2)}) %collective-permute-start.15) | collective-permute-done | bytes 131104 | tf_op jit(solution)/shard_map/ppermute | solution.py:20
  75.8 2.3 %collective-permute-done.19 = bf16[64,1024]{1,0:T(8,128)(2,1)S(1)} collective-permute-done((bf16[64,1024]{1,0:T(8,128)(2,1)S(1)}, bf16[64,1024]{1,0:T(8,128)(2,1)S(1)}, u32[]{:S(2)}, u32[]{:S(2)}) %collective-permute-start.19) | collective-permute-done | bytes 131104 | tf_op jit(solution)/shard_map/ppermute | solution.py:20
  78.3 1.5 %logit_part.1 = (f32[256,512]{1,0:T(8,128)S(1)}, f32[1,256]{1,0:T(1,128)S(1)}, f32[1,256]{1,0:T(1,128)S(1)}, bf16[72,512]{1,0:T(8,128)(2,1)S(1)}, bf16[72,512]{1...) custom-call(s32[5]{0:T(128)S(1)} %stack.32.where_ref, bf16[1024,512]{1,0:T(8,128)(2,1)S(1)} %broadcast_select_fusion.1.un_ref, ...), custom_call_target="tpu_custom_call" | custom-call | tf_op jit(solution)/shard_map/logit_part/pallas_call | solution.py:333
  79.8 1.8 %collective-permute-start.20 = (bf16[72,512]{1,0:T(8,128)(2,1)S(1)}, bf16[72,512]{1,0:T(8,128)(2,1)S(1)}, u32[]{:S(2)}, u32[]{:S(2)}) collective-permute-start(bf16[72,512]{1,0:T(8,128)(2,1)S(1)} %get-tuple-element.47), channel_id=1, source_target_pairs={{0,4},{4,0},{8,12},{12,8},{1,5},{5,1},{9,13},{13,9},{2,6},{6,2},{1... | collective-permute-start | bytes 221192 | tf_op jit(solution)/shard_map/ppermute | solution.py:20
  81.7 2.5 %collective-permute-start.22 = (bf16[72,512]{1,0:T(8,128)(2,1)S(1)}, bf16[72,512]{1,0:T(8,128)(2,1)S(1)}, u32[]{:S(2)}, u32[]{:S(2)}) collective-permute-start(bf16[72,512]{1,0:T(8,128)(2,1)S(1)} %get-tuple-element.49), channel_id=1, source_target_pairs={{0,12},{4,8},{8,4},{12,0},{1,13},{5,9},{9,5},{13,1},{2,14},{6,10},... | collective-permute-start | bytes 221192 | tf_op jit(solution)/shard_map/ppermute | solution.py:20
  84.3 5.4 %collective-permute-done.21.rest_1_ = bf16[72,512]{1,0:T(8,128)(2,1)S(1)} collective-permute-done((bf16[72,512]{1,0:T(8,128)(2,1)S(1)}, bf16[72,512]{1,0:T(8,128)(2,1)S(1)}, u32[]{:S(2)}, u32[]{:S(2)}) %collective-permute-start.21) | collective-permute-done | bytes 73760 | tf_op jit(solution)/shard_map/ppermute | solution.py:20
  91.4 1.2 %collective-permute-start.25 = (f32[2,256]{1,0:T(2,128)S(1)}, f32[2,256]{1,0:T(2,128)S(1)}, u32[]{:S(2)}, u32[]{:S(2)}) collective-permute-start(f32[2,256]{1,0:T(2,128)S(1)} %final_part.1.refs_0_), channel_id=1, source_target_pairs={{0,3},{1,2},{2,1},{3,0},{4,7},{5,6},{6,5},{7,4},{8,11},{9,10},{10,... | collective-permute-start | bytes 6152 | tf_op jit(solution)/shard_map/ppermute | solution.py:20
  92.5 1.8 %collective-permute-done.24.refs_2_ = f32[2,256]{1,0:T(2,128)S(1)} collective-permute-done((f32[2,256]{1,0:T(2,128)S(1)}, f32[2,256]{1,0:T(2,128)S(1)}, u32[]{:S(2)}, u32[]{:S(2)}) %collective-permute-start.24) | collective-permute-done | bytes 2080 | tf_op jit(solution)/shard_map/ppermute | solution.py:20
  (79 shorter events, 9.1 us)
Async XLA Ops:
  5.4 10.3 %collective-permute-start = (bf16[32,1024]{1,0:T(8,128)(2,1)S(1)}, bf16[32,1024]{1,0:T(8,128)(2,1)S(1)}, u32[]{:S(2)}, u32[]{:S(2)}) collective-permute-start(bf16[32,1024]{1,0:T(8,128)(2,1)S(1)} %get-tuple-element.38.rest_0_), channel_id=1, source_target_pairs={{0,4},{4,0},{8,12},{12,8},{1,5},{5,1},{9,13},{13,9},{2,6},{6,2},{1... | collective-permute-start | bytes 196616 | tf_op jit(solution)/shard_map/ppermute | solution.py:20
  8.6 7.3 %collective-permute-start.1 = (bf16[32,1024]{1,0:T(8,128)(2,1)S(1)}, bf16[32,1024]{1,0:T(8,128)(2,1)S(1)}, u32[]{:S(2)}, u32[]{:S(2)}) collective-permute-start(bf16[32,1024]{1,0:T(8,128)(2,1)S(1)} %get-tuple-element.38.rest_0_), channel_id=1, source_target_pairs={{0,8},{4,12},{8,0},{12,4},{1,9},{5,13},{9,1},{13,5},{2,10},{6,14},... | collective-permute-start | bytes 196616 | tf_op jit(solution)/shard_map/ppermute | solution.py:20
  11.1 6.1 %collective-permute-start.2 = (bf16[32,1024]{1,0:T(8,128)(2,1)S(1)}, bf16[32,1024]{1,0:T(8,128)(2,1)S(1)}, u32[]{:S(2)}, u32[]{:S(2)}) collective-permute-start(bf16[32,1024]{1,0:T(8,128)(2,1)S(1)} %get-tuple-element.38.rest_0_), channel_id=1, source_target_pairs={{0,12},{4,8},{8,4},{12,0},{1,13},{5,9},{9,5},{13,1},{2,14},{6,10},... | collective-permute-start | bytes 196616 | tf_op jit(solution)/shard_map/ppermute | solution.py:20
  11.2 44.0 %collective-permute-start.3 = (bf16[1024,512]{1,0:T(8,128)(2,1)}, bf16[1024,512]{1,0:T(8,128)(2,1)}, u32[]{:S(2)}, u32[]{:S(2)}) collective-permute-start(bf16[1024,512]{1,0:T(8,128)(2,1)} %param.14), channel_id=1, source_target_pairs={{0,2},{5,7},{10,8},{15,13},{16,18},{21,23},{26,24},{31,29}} | collective-permute-start | bytes 3145736 | tf_op jit(solution)/shard_map/ppermute | solution.py:423
  18.8 13.2 %collective-permute-start.9 = (bf16[256,1024]{1,0:T(8,128)(2,1)S(1)}, bf16[256,1024]{1,0:T(8,128)(2,1)}, u32[]{:S(2)}, u32[]{:S(2)}) collective-permute-start(bf16[256,1024]{1,0:T(8,128)(2,1)S(1)} %carry_part.1.later_any), channel_id=1, source_target_pairs={{0,4},{4,0},{8,12},{12,8},{1,5},{5,1},{9,13},{13,9},{2,6},{6,2},{1... | collective-permute-start | bytes 1572872 | tf_op jit(solution)/shard_map/ppermute | solution.py:20
  18.9 21.7 %collective-permute-start.12 = (bf16[256,1024]{1,0:T(8,128)(2,1)S(1)}, bf16[256,1024]{1,0:T(8,128)(2,1)}, u32[]{:S(2)}, u32[]{:S(2)}) collective-permute-start(bf16[256,1024]{1,0:T(8,128)(2,1)S(1)} %carry_part.1.later_any), channel_id=1, source_target_pairs={{4,8},{8,4},{5,9},{9,5},{6,10},{10,6},{7,11},{11,7},{20,24},{24,20... | collective-permute-start | bytes 1572872 | tf_op jit(solution)/shard_map/ppermute | solution.py:529
  21.9 1.9 %copy-start.1 = (f32[1024]{0:T(1024)S(1)}, f32[1024]{0:T(1024)}, u32[]{:S(2)}) copy-start(f32[1024]{0:T(1024)} %param.13) | copy-start | bytes 12292
  22.0 5.3 %copy-start.3 = (s32[256]{0:T(256)S(1)}, s32[256]{0:T(256)}, u32[]{:S(2)}) copy-start(s32[256]{0:T(256)} %param.16) | copy-start | bytes 3076
  22.0 7.9 %copy-start.4 = (s32[256]{0:T(256)S(1)}, s32[256]{0:T(256)}, u32[]{:S(2)}) copy-start(s32[256]{0:T(256)} %param.15) | copy-start | bytes 3076
  22.0 9.7 %copy-start.2 = (s32[256]{0:T(256)S(1)}, s32[256]{0:T(256)}, u32[]{:S(2)}) copy-start(s32[256]{0:T(256)} %param.17) | copy-start | bytes 3076
  23.2 10.3 %collective-permute-start.7 = (bf16[128,1024]{1,0:T(8,128)(2,1)}, bf16[128,1024]{1,0:T(8,128)(2,1)S(1)}, u32[]{:S(2)}, u32[]{:S(2)}) collective-permute-start(bf16[128,1024]{1,0:T(8,128)(2,1)} %convolution_convert_fusion.3), channel_id=1, source_target_pairs={{0,1},{1,0},{2,3},{3,2},{4,5},{5,4},{6,7},{7,6},{8,9},{9,8},{10,11... | collective-permute-start | bytes 786440 | tf_op jit(solution)/shard_map/ppermute | solution.py:20
  23.9 4.7 %collective-permute-start.5 = (f32[1024]{0:T(1024)S(1)}, f32[1024]{0:T(1024)S(1)}, u32[]{:S(2)}, u32[]{:S(2)}) collective-permute-start(f32[1024]{0:T(1024)S(1)} %copy-done.1), channel_id=1, source_target_pairs={{0,2},{5,7},{10,8},{15,13},{16,18},{21,23},{26,24},{31,29}} | collective-permute-start | bytes 12296 | tf_op jit(solution)/shard_map/ppermute | solution.py:423
  28.6 3.4 %collective-permute-start.6 = (f32[1024]{0:T(1024)S(1)}, f32[1024]{0:T(1024)S(1)}, u32[]{:S(2)}, u32[]{:S(2)}) collective-permute-start(f32[1024]{0:T(1024)S(1)} %broadcast_select_fusion.2), channel_id=1, source_target_pairs={{0,1},{2,3},{5,4},{7,6},{10,11},{8,9},{15,14},{13,12},{16,17},{18,... | collective-permute-start | bytes 12296 | tf_op jit(solution)/shard_map/ppermute | solution.py:423
  33.4 3.6 %collective-permute-start.10 = (bf16[128,1024]{1,0:T(8,128)(2,1)S(1)}, bf16[128,1024]{1,0:T(8,128)(2,1)S(1)}, u32[]{:S(2)}, u32[]{:S(2)}) collective-permute-start(bf16[128,1024]{1,0:T(8,128)(2,1)S(1)} %convolution_convert_fusion.2), channel_id=1, source_target_pairs={{0,1},{1,0},{2,3},{3,2},{4,5},{5,4},{6,7},{7,6},{8,9},{9,8},{10,11... | collective-permute-start | bytes 786440 | tf_op jit(solution)/shard_map/ppermute | solution.py:20
  34.0 21.1 %copy-start = (bf16[1024,512]{1,0:T(8,128)(2,1)S(1)}, bf16[1024,512]{1,0:T(8,128)(2,1)}, u32[]{:S(2)}) copy-start(bf16[1024,512]{1,0:T(8,128)(2,1)} %param.14) | copy-start | bytes 3145732
  34.0 6.5 %collective-permute-start.8 = (bf16[64,1024]{1,0:T(8,128)(2,1)S(1)}, bf16[64,1024]{1,0:T(8,128)(2,1)S(1)}, u32[]{:S(2)}, u32[]{:S(2)}) collective-permute-start(bf16[64,1024]{1,0:T(8,128)(2,1)S(1)} %dynamic-slice_convert_fusion.3), channel_id=1, source_target_pairs={{0,2},{1,3},{2,0},{3,1},{4,6},{5,7},{6,4},{7,5},{8,10},{9,11},{10,... | collective-permute-start | bytes 393224 | tf_op jit(solution)/shard_map/ppermute | solution.py:20
  36.4 8.6 %collective-permute-start.16 = (bf16[256,1024]{1,0:T(8,128)(2,1)}, bf16[256,1024]{1,0:T(8,128)(2,1)S(1)}, u32[]{:S(2)}, u32[]{:S(2)}) collective-permute-start(bf16[256,1024]{1,0:T(8,128)(2,1)} %collective-permute-done.9), channel_id=1, source_target_pairs={{4,8},{8,4},{5,9},{9,5},{6,10},{10,6},{7,11},{11,7},{20,24},{24,20... | collective-permute-start | bytes 1572872 | tf_op jit(solution)/shard_map/ppermute | solution.py:530
  38.5 6.4 %collective-permute-start.11 = (bf16[64,1024]{1,0:T(8,128)(2,1)S(1)}, bf16[64,1024]{1,0:T(8,128)(2,1)S(1)}, u32[]{:S(2)}, u32[]{:S(2)}) collective-permute-start(bf16[64,1024]{1,0:T(8,128)(2,1)S(1)} %dynamic-slice_convert_fusion.2), channel_id=1, source_target_pairs={{0,2},{1,3},{2,0},{3,1},{4,6},{5,7},{6,4},{7,5},{8,10},{9,11},{10,... | collective-permute-start | bytes 393224 | tf_op jit(solution)/shard_map/ppermute | solution.py:20
  40.6 17.4 %collective-permute-start.13 = (bf16[256,1024]{1,0:T(8,128)(2,1)}, bf16[256,1024]{1,0:T(8,128)(2,1)S(1)}, u32[]{:S(2)}, u32[]{:S(2)}) collective-permute-start(bf16[256,1024]{1,0:T(8,128)(2,1)} %collective-permute-done.12), channel_id=1, source_target_pairs={{0,4},{4,0},{8,12},{12,8},{1,5},{5,1},{9,13},{13,9},{2,6},{6,2},{1... | collective-permute-start | bytes 1572872 | tf_op jit(solution)/shard_map/ppermute | solution.py:20
  45.0 23.1 %collective-permute-start.17 = (bf16[256,1024]{1,0:T(8,128)(2,1)S(1)}, bf16[256,1024]{1,0:T(8,128)(2,1)S(1)}, u32[]{:S(2)}, u32[]{:S(2)}) collective-permute-start(bf16[256,1024]{1,0:T(8,128)(2,1)S(1)} %collective-permute-done.16), channel_id=1, source_target_pairs={{0,4},{4,0},{8,12},{12,8},{1,5},{5,1},{9,13},{13,9},{2,6},{6,2},{1... | collective-permute-start | bytes 1572872 | tf_op jit(solution)/shard_map/ppermute | solution.py:20
  55.3 22.9 %collective-permute-start.4 = (bf16[1024,512]{1,0:T(8,128)(2,1)S(1)}, bf16[1024,512]{1,0:T(8,128)(2,1)S(1)}, u32[]{:S(2)}, u32[]{:S(2)}) collective-permute-start(bf16[1024,512]{1,0:T(8,128)(2,1)S(1)} %broadcast_select_fusion), channel_id=1, source_target_pairs={{0,1},{2,3},{5,4},{7,6},{10,11},{8,9},{15,14},{13,12},{16,17},{18,... | collective-permute-start | bytes 3145736 | tf_op jit(solution)/shard_map/ppermute | solution.py:423
  59.6 9.2 %collective-permute-start.14 = (bf16[128,1024]{1,0:T(8,128)(2,1)S(1)}, bf16[128,1024]{1,0:T(8,128)(2,1)S(1)}, u32[]{:S(2)}, u32[]{:S(2)}) collective-permute-start(bf16[128,1024]{1,0:T(8,128)(2,1)S(1)} %convolution_convert_fusion.1), channel_id=1, source_target_pairs={{0,1},{1,0},{2,3},{3,2},{4,5},{5,4},{6,7},{7,6},{8,9},{9,8},{10,11... | collective-permute-start | bytes 786440 | tf_op jit(solution)/shard_map/ppermute | solution.py:20
  68.8 1.6 %collective-permute-start.18 = (bf16[128,1024]{1,0:T(8,128)(2,1)S(1)}, bf16[128,1024]{1,0:T(8,128)(2,1)S(1)}, u32[]{:S(2)}, u32[]{:S(2)}) collective-permute-start(bf16[128,1024]{1,0:T(8,128)(2,1)S(1)} %convolution_convert_fusion), channel_id=1, source_target_pairs={{0,1},{1,0},{2,3},{3,2},{4,5},{5,4},{6,7},{7,6},{8,9},{9,8},{10,11... | collective-permute-start | bytes 786440 | tf_op jit(solution)/shard_map/ppermute | solution.py:20
  69.4 6.4 %collective-permute-start.15 = (bf16[64,1024]{1,0:T(8,128)(2,1)S(1)}, bf16[64,1024]{1,0:T(8,128)(2,1)S(1)}, u32[]{:S(2)}, u32[]{:S(2)}) collective-permute-start(bf16[64,1024]{1,0:T(8,128)(2,1)S(1)} %dynamic-slice_convert_fusion.1), channel_id=1, source_target_pairs={{0,2},{1,3},{2,0},{3,1},{4,6},{5,7},{6,4},{7,5},{8,10},{9,11},{10,... | collective-permute-start | bytes 393224 | tf_op jit(solution)/shard_map/ppermute | solution.py:20
  70.9 7.2 %collective-permute-start.19 = (bf16[64,1024]{1,0:T(8,128)(2,1)S(1)}, bf16[64,1024]{1,0:T(8,128)(2,1)S(1)}, u32[]{:S(2)}, u32[]{:S(2)}) collective-permute-start(bf16[64,1024]{1,0:T(8,128)(2,1)S(1)} %dynamic-slice_convert_fusion), channel_id=1, source_target_pairs={{0,2},{1,3},{2,0},{3,1},{4,6},{5,7},{6,4},{7,5},{8,10},{9,11},{10,... | collective-permute-start | bytes 393224 | tf_op jit(solution)/shard_map/ppermute | solution.py:20
  79.8 4.5 %collective-permute-start.20 = (bf16[72,512]{1,0:T(8,128)(2,1)S(1)}, bf16[72,512]{1,0:T(8,128)(2,1)S(1)}, u32[]{:S(2)}, u32[]{:S(2)}) collective-permute-start(bf16[72,512]{1,0:T(8,128)(2,1)S(1)} %get-tuple-element.47), channel_id=1, source_target_pairs={{0,4},{4,0},{8,12},{12,8},{1,5},{5,1},{9,13},{13,9},{2,6},{6,2},{1... | collective-permute-start | bytes 221192 | tf_op jit(solution)/shard_map/ppermute | solution.py:20
  81.6 8.2 %collective-permute-start.21 = (bf16[72,512]{1,0:T(8,128)(2,1)S(1)}, bf16[72,512]{1,0:T(8,128)(2,1)S(1)}, u32[]{:S(2)}, u32[]{:S(2)}) collective-permute-start(bf16[72,512]{1,0:T(8,128)(2,1)S(1)} %get-tuple-element.48), channel_id=1, source_target_pairs={{0,8},{4,12},{8,0},{12,4},{1,9},{5,13},{9,1},{13,5},{2,10},{6,14},... | collective-permute-start | bytes 221192 | tf_op jit(solution)/shard_map/ppermute | solution.py:20
  81.7 8.1 %collective-permute-start.22 = (bf16[72,512]{1,0:T(8,128)(2,1)S(1)}, bf16[72,512]{1,0:T(8,128)(2,1)S(1)}, u32[]{:S(2)}, u32[]{:S(2)}) collective-permute-start(bf16[72,512]{1,0:T(8,128)(2,1)S(1)} %get-tuple-element.49), channel_id=1, source_target_pairs={{0,12},{4,8},{8,4},{12,0},{1,13},{5,9},{9,5},{13,1},{2,14},{6,10},... | collective-permute-start | bytes 221192 | tf_op jit(solution)/shard_map/ppermute | solution.py:20
  90.6 1.9 %collective-permute-start.23 = (f32[2,256]{1,0:T(2,128)S(1)}, f32[2,256]{1,0:T(2,128)S(1)}, u32[]{:S(2)}, u32[]{:S(2)}) collective-permute-start(f32[2,256]{1,0:T(2,128)S(1)} %final_part.1.refs_0_), channel_id=1, source_target_pairs={{0,1},{1,0},{2,3},{3,2},{4,5},{5,4},{6,7},{7,6},{8,9},{9,8},{10,11... | collective-permute-start | bytes 6152 | tf_op jit(solution)/shard_map/ppermute | solution.py:20
  90.7 3.7 %collective-permute-start.24 = (f32[2,256]{1,0:T(2,128)S(1)}, f32[2,256]{1,0:T(2,128)S(1)}, u32[]{:S(2)}, u32[]{:S(2)}) collective-permute-start(f32[2,256]{1,0:T(2,128)S(1)} %final_part.1.refs_0_), channel_id=1, source_target_pairs={{0,2},{1,3},{2,0},{3,1},{4,6},{5,7},{6,4},{7,5},{8,10},{9,11},{10,... | collective-permute-start | bytes 6152 | tf_op jit(solution)/shard_map/ppermute | solution.py:20
  91.4 3.0 %collective-permute-start.25 = (f32[2,256]{1,0:T(2,128)S(1)}, f32[2,256]{1,0:T(2,128)S(1)}, u32[]{:S(2)}, u32[]{:S(2)}) collective-permute-start(f32[2,256]{1,0:T(2,128)S(1)} %final_part.1.refs_0_), channel_id=1, source_target_pairs={{0,3},{1,2},{2,1},{3,0},{4,7},{5,6},{6,5},{7,4},{8,11},{9,10},{10,... | collective-permute-start | bytes 6152 | tf_op jit(solution)/shard_map/ppermute | solution.py:20

commit v4 on v3

--- a/solution.py
+++ b/solution.py
@@ -36,83 +36,118 @@
     return pl.ds(pl.multiple_of(tile * LANES, LANES), LANES)
 
 
-def local_kernel(
-    steps, modes, x_any, filt_any, mode_any, nat_any, y_ref, gate_ref, start_ref, msg_ref,
-    filt_ref, mode_ref, held, nat_ref, xs, gs, sems, side_sems
+def behind(value):
+    sub = lax.broadcasted_iota(jnp.int32, value.shape, 0)
+    return jnp.where(sub == 0, 0.0, pltpu.roll(value, 1, 0))
+
+
+def spread_modes(mode_ref, cols, modes):
+    decay = [jnp.broadcast_to(mode_ref[0, m : m + 1, cols], (SUBS, LANES)) for m in range(modes)]
+    return decay, [jnp.exp(-d) for d in decay]
+
+
+def running(state, decay, steps):
+    sub = lax.broadcasted_iota(jnp.int32, state.shape, 0)
+    for reach in (1, 2, 4):
+        power = jnp.exp(-decay * float(steps * reach))
+        state = state + jnp.where(sub < reach, 0.0, power * pltpu.roll(state, reach, 0))
+    return state
+
+
+def end_kernel(
+    steps, modes, x_any, filt_any, mode_any, nat_any, prod_ref, gate_ref, msg_ref, filt_ref, mode_ref,
+    held, nat_ref, xs, sems, side_sems
 ):
     rows = steps * SUBS
     tiles = held.shape[0]
-    spread = rows // LANES
+    base = 2 * modes
 
     def fetch(tile):
-        return pltpu.make_async_copy(x_any.at[:, :, lane_slice(tile)], held.at[tile], sems.at[tile])
+        return pltpu.make_async_copy(x_any.at[1:3, :, lane_slice(tile)], held.at[tile], sems.at[tile])
 
     sides = [
         pltpu.make_async_copy(src, dst, side_sems.at[k])
-        for k, (src, dst) in enumerate(((filt_any, filt_ref), (mode_any, mode_ref), (nat_any, nat_ref)))
+        for k, (src, dst) in enumerate(
+            ((filt_any, filt_ref), (mode_any, mode_ref), (nat_any, nat_ref), (x_any.at[0], gate_ref))
+        )
     ]
     fetch(0).start()
-    for side in sides:
+    for side in sides[:3]:
         side.start()
 
     @pl.loop(1, tiles)
     def _(tile):
         fetch(tile).start()
 
-    for side in sides:
+    sides[3].start()
+    for side in sides[:3]:
         side.wait()
 
     @pl.loop(0, tiles)
     def _(tile):
         cols = lane_slice(tile)
         sub = lax.broadcasted_iota(jnp.int32, (SUBS, LANES), 0)
-        decay = [jnp.broadcast_to(mode_ref[0, m : m + 1, cols], (SUBS, LANES)) for m in range(modes)]
-        res = [jnp.broadcast_to(mode_ref[1, m : m + 1, cols], (SUBS, LANES)) for m in range(modes)]
-        fall = [jnp.exp(-d) for d in decay]
-        taps = [taps_of(filt_ref, i, cols) for i in range(3)]
-        ids = nat_ref[0:1, lane_slice(tile % spread)]
-        ids = jnp.where(tile < spread, ids // 256, jnp.where(tile < 2 * spread, ids % 256, 0)).astype(F32)
+        decay, fall = spread_modes(mode_ref, cols, modes)
+        taps = [taps_of(filt_ref, i, cols) for i in (1, 2)]
         fetch(tile).wait()
-        for i in range(3):
+        for i in range(2):
             xs[i] = held[tile, i].astype(F32)
 
         def at(i, t):
             return xs[i, pl.ds(t, SUBS, stride=steps), :]
 
-        def behind(value):
-            return jnp.where(sub == 0, 0.0, pltpu.roll(value, 1, 0))
-
-        back2 = [behind(at(i, steps - 2)) for i in range(3)]
-        back1 = [behind(at(i, steps - 1)) for i in range(3)]
+        back2 = [behind(at(i, steps - 2)) for i in range(2)]
+        back1 = [behind(at(i, steps - 1)) for i in range(2)]
         state = [jnp.zeros((SUBS, LANES), F32) for _ in range(modes)]
         for t in range(steps):
-            now = [at(i, t) for i in range(3)]
-            mixed = [mix(taps[i], now[i], back1[i], back2[i]) for i in range(3)]
+            now = [at(i, t) for i in range(2)]
+            mixed = [mix(taps[i], now[i], back1[i], back2[i]) for i in range(2)]
             back2, back1 = back1, now
-            gs[pl.ds(t, SUBS, stride=steps), :] = mixed[0]
-            prod = rounded(mixed[1] * mixed[2])
+            prod = rounded(mixed[0] * mixed[1])
             if t < 2:
                 prod = jnp.where(sub == 0, 0.0, prod)
+            prod_ref[t * SUBS : (t + 1) * SUBS, cols] = prod
+            state = [f * s + prod for f, s in zip(fall, state)]
+        ends = [running(state[m], decay[m], steps)[SUBS - 1 : SUBS, :] for m in range(modes)]
+        end = jnp.concatenate(ends, axis=0)
+        high = rounded(end)
+        edge = [xs[0, 0:2, :], xs[1, 0:2, :], xs[0, rows - 2 : rows, :], xs[1, rows - 2 : rows, :]]
+        msg_ref[0 : base + 8, cols] = jnp.concatenate([high, end - high] + edge, axis=0).astype(BF16)
+
+    sides[3].wait()
+    width = gate_ref.shape[1]
+    ids = nat_ref[...]
+    empty = jnp.zeros((1, width - 2 * rows), jnp.int32)
+    ids = jnp.concatenate([ids // 256, ids % 256, empty], axis=1).astype(F32)
+    head = gate_ref[0:16, :].astype(F32)
+    tail = gate_ref[rows - 16 : rows, :].astype(F32)
+    other = jnp.concatenate([tail[14:16, :], head[0:2, :], ids, jnp.zeros((3, width), F32)], axis=0)
+    msg_ref[base + 8 : base + 16, :] = other.astype(BF16)
+
+
+def local_kernel(steps, modes, filt_ref, mode_ref, prod_ref, x_ref, y_ref, gate_ref, start_ref, xs, gs):
+    @pl.loop(0, x_ref.shape[1] // LANES)
+    def _(tile):
+        cols = lane_slice(tile)
+        decay, fall = spread_modes(mode_ref, cols, modes)
+        res = [jnp.broadcast_to(mode_ref[1, m : m + 1, cols], (SUBS, LANES)) for m in range(modes)]
+        taps = taps_of(filt_ref, 0, cols)
+        xs[...] = x_ref[:, cols].astype(F32)
+        back2 = behind(xs[pl.ds(steps - 2, SUBS, stride=steps), :])
+        back1 = behind(xs[pl.ds(steps - 1, SUBS, stride=steps), :])
+        state = [jnp.zeros((SUBS, LANES), F32) for _ in range(modes)]
+        for t in range(steps):
+            now = xs[pl.ds(t, SUBS, stride=steps), :]
+            gs[pl.ds(t, SUBS, stride=steps), :] = mix(taps, now, back1, back2)
+            back2, back1 = back1, now
+            prod = prod_ref[t * SUBS : (t + 1) * SUBS, cols]
             state = [f * s + prod for f, s in zip(fall, state)]
             y_ref[t * SUBS : (t + 1) * SUBS, cols] = functools.reduce(
                 lambda p, q: p + q, [r * s for r, s in zip(res, state)]
             )
         gate_ref[:, cols] = gs[...].astype(BF16)
-        ends = []
         for m in range(modes):
-            total = state[m]
-            for reach in (1, 2, 4):
-                power = jnp.exp(-decay[m] * float(steps * reach))
-                total = total + jnp.where(sub < reach, 0.0, power * pltpu.roll(total, reach, 0))
-            start_ref[m * SUBS : (m + 1) * SUBS, cols] = behind(total)
-            ends.append(total[SUBS - 1 : SUBS, :])
-        end = jnp.concatenate(ends, axis=0)
-        high = rounded(end)
-        first = [xs[i, 0:2, :] for i in range(3)]
-        last = [xs[i, rows - 2 : rows, :] for i in range(3)]
-        edge = jnp.concatenate([first[1], first[2], last[1], last[2]], axis=0)
-        other = jnp.concatenate([last[0], first[0], ids, jnp.zeros((3, LANES), F32)], axis=0)
-        msg_ref[:, cols] = jnp.concatenate([high, end - high, edge, other], axis=0).astype(BF16)
+            start_ref[m * SUBS : (m + 1) * SUBS, cols] = behind(running(state[m], decay[m], steps))
 
 
 SMALL = pltpu.CompilerParams(vmem_limit_bytes=16 * 2**20)
@@ -122,36 +157,52 @@
     return pl.BlockSpec(memory_space=pltpu.VMEM)
 
 
-def local_part(streams, filt, modes_t, native):
+def end_part(streams, filt, modes_t, native):
     rows, width = streams.shape[1:]
     modes = modes_t.shape[1]
     steps = rows // SUBS
     tiles = width // LANES
     msg_rows = 2 * modes + 16
     return pl.pallas_call(
-        functools.partial(local_kernel, steps, modes),
+        functools.partial(end_kernel, steps, modes),
         in_specs=[pl.BlockSpec(memory_space=pltpu.HBM)] * 4,
-        out_specs=[in_vmem()] * 6,
+        out_specs=[in_vmem()] * 5,
         out_shape=[
             pltpu.VMEM((rows, width), F32),
             pltpu.VMEM((rows, width), BF16),
-            pltpu.VMEM((modes * SUBS, width), F32),
             pltpu.VMEM((msg_rows, width), BF16),
             pltpu.VMEM(filt.shape, F32),
             pltpu.VMEM(modes_t.shape, F32),
         ],
         scratch_shapes=[
-            pltpu.VMEM((tiles, 3, rows, LANES), BF16),
+            pltpu.VMEM((tiles, 2, rows, LANES), BF16),
             pltpu.VMEM((1, rows), jnp.int32),
-            pltpu.VMEM((3, rows, LANES), F32),
-            pltpu.VMEM((rows, LANES), F32),
+            pltpu.VMEM((2, rows, LANES), F32),
             pltpu.SemaphoreType.DMA((tiles,)),
-            pltpu.SemaphoreType.DMA((3,)),
+            pltpu.SemaphoreType.DMA((4,)),
         ],
         compiler_params=SMALL,
-        cost_estimate=pl.CostEstimate(flops=rows * width * 64, bytes_accessed=rows * width * 12, transcendentals=0),
+        name="end_part",
+    )(*[pltpu.with_memory_space_constraint(v, pltpu.HBM) for v in (streams, filt, modes_t, native[None, :])])
+
+
+def local_part(filt, modes_t, prod, gate_stream):
+    rows, width = prod.shape
+    modes = modes_t.shape[1]
+    return pl.pallas_call(
+        functools.partial(local_kernel, rows // SUBS, modes),
+        in_specs=[in_vmem()] * 4,
+        out_specs=[in_vmem()] * 3,
+        out_shape=[
+            pltpu.VMEM((rows, width), F32),
+            pltpu.VMEM((rows, width), BF16),
+            pltpu.VMEM((modes * SUBS, width), F32),
+        ],
+        input_output_aliases={2: 0, 3: 1},
+        scratch_shapes=[pltpu.VMEM((rows, LANES), F32), pltpu.VMEM((rows, LANES), F32)],
+        compiler_params=SMALL,
         name="local_part",
-    )(*[pltpu.with_memory_space_constraint(v, pltpu.HBM) for v in (streams, filt, modes_t, native[None, :])])
+    )(*[pltpu.with_memory_space_constraint(v, pltpu.VMEM) for v in (filt, modes_t, prod, gate_stream)])
 
 
 def carry_kernel(steps, modes, stacked, count, where_ref, filt_ref, mode_ref, y_ref, gate_ref, start_ref, *rest):
@@ -423,7 +474,7 @@
     return lax.ppermute(value, ("ctx", "mp"), pairs)
 
 
-def feature_rows(unembed, norm_gain, rows_wanted, z, m, first_move):
+def feature_rows(unembed, norm_gain, rows_wanted, z, m):
     shards = lax.axis_size("mp")
     held = unembed.shape[0]
     if held % rows_wanted != 0:
@@ -434,16 +485,15 @@
     ratio = held // rows_wanted
     place = m ^ (z // ratio)
     result = []
-    for value, moved in ((unembed, first_move), (norm_gain, None)):
+    for value in (unembed, norm_gain):
         value = lax.dynamic_slice_in_dim(value, (z % ratio) * rows_wanted, rows_wanted, 0)
         bit, holders, known = shards // 2, [0], place == 0
         while bit:
-            if moved is None:
-                moved = hand_on(value, owner, bit, holders)
+            moved = hand_on(value, owner, bit, holders)
             value = jnp.where(known, value, moved)
             holders = holders + [h ^ bit for h in holders]
             known = sum((place == h).astype(jnp.int32) for h in holders) > 0
-            bit, moved = bit // 2, None
+            bit //= 2
         result.append(value)
     return tuple(result)
 
@@ -464,7 +514,7 @@
         keep, send = split_half(gated if value is None else value, upper)
         if value is None:
             sent = jnp.dot(send, weight, preferred_element_type=F32).astype(BF16)
-            keep = jnp.dot(keep, weight, preferred_element_type=F32)
+            keep = lax.optimization_barrier(jnp.dot(keep, weight, preferred_element_type=F32))
         else:
             sent = send.astype(BF16)
         got = swap(sent, "mp", bit)
@@ -489,20 +539,16 @@
     quick = count == 4
     modes_t = jnp.swapaxes(mode_params, 1, 2)
     me = z.astype(jnp.int32)[None]
-    y, gate, start, msg, filt, modes_t = local_part(streams, short_filter, modes_t, native)
+    prod, gate_stream, msg, filt, modes_t = end_part(streams, short_filter, modes_t, native)
+    y, gate, start = local_part(filt, modes_t, prod, gate_stream)
     nat_at = 2 * mode_params.shape[2] + 12
     if quick:
         msgs = [msg]
         for k in range(1, count):
             msgs.append(swap(msg, "ctx", k))
-        width_out = out_weight.shape[1]
-        moved = None
-        if unembed.shape[0] == width_out and shards > 1:
-            moved = hand_on(unembed, owners(width_out, width_out), shards // 2, [0])
         gated = carry_part(me, filt, modes_t, y, gate, start, msgs, False)
         nat_rows = msgs
     else:
-        moved = None
         every = lax.all_gather(msg, "ctx")
         gated = carry_part(me, filt, modes_t, y, gate, start, [every], True)
         nat_rows = every
@@ -516,7 +562,7 @@
     nat_rows = nat_rows.astype(jnp.int32)
     nat_all = (nat_rows[:, :rows] * 256 + nat_rows[:, rows:]).reshape(-1)
 
-    un, gains = feature_rows(unembed, norm_gain, out_weight.shape[1], z, m, moved)
+    un, gains = feature_rows(unembed, norm_gain, out_weight.shape[1], z, m)
     piece = row_piece(m)
     share = rows // shards
     block, inner = mut_pos // rows, mut_pos % rows

time: 95.4 us -> 100 us (1.048)
  waiting for transfers between devices: 27.6 us -> 35.1 us
  starting transfers between devices: 44.4 us -> 38.1 us
  Pallas kernels: 10.9 us -> 12.8 us
  other arithmetic: 1.94 us -> 3.18 us
    ppermute x20, waiting for transfers between devices: 26.4 us -> 33.8 us  [swap(): return lax.ppermute(value, axis, [(i, i ^ bit) for i in range(count)])]
    ppermute x20, starting transfers between devices: 31.1 us -> 26 us  [swap(): return lax.ppermute(value, axis, [(i, i ^ bit) for i in range(count)])]
    pallas_call x1 -> x2, Pallas kernels: 4.8 us -> 6.71 us  [the longest x1 3.51 us: local_part(): pl.pallas_call(functools.partial(local_kernel, rows // SUBS, modes), in_s...]
    add x4 -> x8, other arithmetic: 0.11 us -> 1.38 us  [project(): value = keep + got.astype(F32)]
    ppermute x4, starting transfers between devices: 11.1 us -> 9.94 us  [hand_on(): return lax.ppermute(value, ('ctx', 'mp'), pairs)]
  transfers between devices with their start and end apart: 26 -> 26, of which waited for: 12 -> 8; matrix products, arithmetic and copies ran while one was open for 11% -> 13% of each run, Pallas kernels for 3% -> 7%
where the time goes in v4:
time: 100 us
  starting transfers between devices  38.1 us (38%)
  waiting for transfers between devices  35.1 us (35%)
  Pallas kernels  12.8 us (13%)
  matrix products  6.97 us (7%)
  other arithmetic  3.18 us (3%)
  local copies, waits for them, and re-layouts  2.74 us (3%)
  between operations  1.25 us (1%)
    ppermute x20, waiting for transfers between devices, swap(): return lax.ppermute(value, axis, [(i, i ^ bit) for i in range(count)])  33.8 us
    ppermute x20, starting transfers between devices, swap(): return lax.ppermute(value, axis, [(i, i ^ bit) for i in range(count)])  26 us
    ppermute x4, starting transfers between devices, hand_on(): return lax.ppermute(value, ('ctx', 'mp'), pairs)  9.94 us
    dot_general x4, matrix products, project(): jnp.dot(keep, weight, preferred_element_type=F32)  3.54 us
    pallas_call x1, Pallas kernels, local_part(): pl.pallas_call(functools.partial(local_kernel, rows // SUBS, modes), in_s...  3.51 us
    dot_general x4, matrix products, project(): sent = jnp.dot(send, weight, preferred_element_type=F32).astype(BF16)  3.43 us
    pallas_call x1, Pallas kernels, end_part(): pl.pallas_call(functools.partial(end_kernel, steps, modes), in_specs=[pl....  3.2 us
  transfers between devices with their start and end apart: 26, of which 8 were waited for; matrix products, arithmetic and copies ran while one was open for 13% of the time, Pallas kernels for 7%

profile of v4, /device:TPU:0, one launch (start us, length us, event | category | flops | bytes accessed | tf_op | source)
XLA Modules:
  0.0 100.0 jit_solution(362522146172619003)
XLA Ops:
  0.6 3.2 %end_part.1 = (f32[256,1024]{1,0:T(8,128)S(1)}, bf16[256,1024]{1,0:T(8,128)(2,1)S(1)}, bf16[32,1024]{1,0:T(8,128)(2,1)S(1)}, f32[3,3,1024]{2,1,0:T(4,128)S(1)}, f32[2,8,1024]{2,1,0:T(8,128)S(1)}) custom-call(bf16[3,256,1024]{2,1,0:T(8,128)(2,1)} %x_any.1, f32[3,3,1024]{2,1,0:T(4,128)} %filt_any.1, f32[2,8,1024]{2,1,0:T(8,128)} %bitcast.31, s32[1,256]{1,0:T(1,128)} %bitcast.35), custom_call_target="tpu_custom_call" | custom-call | tf_op jit(solution)/shard_map/end_part/pallas_call | solution.py:166
  3.8 3.1 %collective-permute-start = (bf16[32,1024]{1,0:T(8,128)(2,1)S(1)}, bf16[32,1024]{1,0:T(8,128)(2,1)S(1)}, u32[]{:S(2)}, u32[]{:S(2)}) collective-permute-start(bf16[32,1024]{1,0:T(8,128)(2,1)S(1)} %get-tuple-element.42.rest_0_), channel_id=1, source_target_pairs={{0,4},{4,0},{8,12},{12,8},{1,5},{5,1},{9,13},{13,9},{2,6},{6,2},{1... | collective-permute-start | bytes 196616 | tf_op jit(solution)/shard_map/ppermute | solution.py:20
  7.0 2.6 %collective-permute-start.1 = (bf16[32,1024]{1,0:T(8,128)(2,1)S(1)}, bf16[32,1024]{1,0:T(8,128)(2,1)S(1)}, u32[]{:S(2)}, u32[]{:S(2)}) collective-permute-start(bf16[32,1024]{1,0:T(8,128)(2,1)S(1)} %get-tuple-element.42.rest_0_), channel_id=1, source_target_pairs={{0,8},{4,12},{8,0},{12,4},{1,9},{5,13},{9,1},{13,5},{2,10},{6,14},... | collective-permute-start | bytes 196616 | tf_op jit(solution)/shard_map/ppermute | solution.py:20
  9.5 4.6 %collective-permute-start.3 = (bf16[1024,512]{1,0:T(8,128)(2,1)}, bf16[1024,512]{1,0:T(8,128)(2,1)}, u32[]{:S(2)}, u32[]{:S(2)}) collective-permute-start(bf16[1024,512]{1,0:T(8,128)(2,1)} %param.14), channel_id=1, source_target_pairs={{0,2},{5,7},{10,8},{15,13},{16,18},{21,23},{26,24},{31,29}} | collective-permute-start | bytes 3145736 | tf_op jit(solution)/shard_map/ppermute | solution.py:474
  14.1 3.5 %local_part.1 = (f32[256,1024]{1,0:T(8,128)S(1)}, bf16[256,1024]{1,0:T(8,128)(2,1)S(1)}, f32[64,1024]{1,0:T(8,128)S(1)}) custom-call(f32[3,3,1024]{2,1,0:T(4,128)S(1)} %get-tuple-element.29.filt_ref, f32[2,8,1024]{2,1,0:T(8,128)S(1)} %get-tuple-element.30.mode_ref, ...), custom_call_target="tpu_custom_call", output_to_operand_aliasing={{0}: (2, {}), {1}: (3, {})} | custom-call | tf_op jit(solution)/shard_map/local_part/pallas_call | solution.py:192
  17.7 1.5 %carry_part.1.later_any = bf16[256,1024]{1,0:T(8,128)(2,1)S(1)} custom-call(s32[1]{0:T(128)} %bitcast.where_ref, f32[3,3,1024]{2,1,0:T(4,128)S(1)} %get-tuple-element.29.filt_ref, f32[2,8,1024]{2,1,0:T(8,128)S(1)} %get-tuple-element.30.mode_ref, f32[256,1024]{1,0:T(8,128)S(1)} %get-tuple-element.33.y_ref, bf16[256,1024]{1,0:T(8,128)(2,1)S(1)} %get-tuple-element.34.gate_ref, ...), custom_call_target="tpu_custom_call" | custom-call | flops 8388608 | bytes 2097152 | tf_op jit(solution)/shard_map/carry_part/pallas_call | solution.py:297
  19.4 1.5 %collective-permute-start.12 = (bf16[256,1024]{1,0:T(8,128)(2,1)S(1)}, bf16[256,1024]{1,0:T(8,128)(2,1)}, u32[]{:S(2)}, u32[]{:S(2)}) collective-permute-start(bf16[256,1024]{1,0:T(8,128)(2,1)S(1)} %carry_part.1.later_any), channel_id=1, source_target_pairs={{4,8},{8,4},{5,9},{9,5},{6,10},{10,6},{7,11},{11,7},{20,24},{24,20... | collective-permute-start | bytes 1572872 | tf_op jit(solution)/shard_map/ppermute | solution.py:575
  20.8 1.6 %bring.1 = bf16[1024,1024]{1,0:T(8,128)(2,1)S(1)} custom-call(bf16[256,1024]{1,0:T(8,128)(2,1)S(1)} %carry_part.1.later_any, bf16[1024,1024]{1,0:T(8,128)(2,1)} %src_any.1), custom_call_target="tpu_custom_call" | custom-call | tf_op jit(solution)/shard_map/bring/pallas_call | solution.py:316
  22.4 1.1 %convolution_convert_fusion.3 = bf16[128,1024]{1,0:T(8,128)(2,1)} fusion(bf16[1024,1024]{1,0:T(8,128)(2,1)S(1)} %bring.1, bf16[256,1024]{1,0:T(8,128)(2,1)S(1)} %carry_part.1.later_any, s32[]{:T(128)S(6)} %select_n.168), kind=kOutput, calls=%fused_computation.5 | convolution fusion | flops 268566528 | bytes 2621444 | tf_op jit(solution)/shard_map/dot_general | solution.py:516
  23.6 1.3 %fusion.10 = f32[128,1024]{1,0:T(8,128)} fusion(bf16[1024,1024]{1,0:T(8,128)(2,1)S(1)} %bring.1, bf16[256,1024]{1,0:T(8,128)(2,1)S(1)} %carry_part.1.later_any, s32[]{:T(128)S(6)} %select_n.167), kind=kOutput, calls=%fused_computation.30 | convolution fusion | flops 268435456 | bytes 2883588 | tf_op jit(solution)/shard_map/dot_general | solution.py:517
  25.6 1.3 %collective-permute-start.5 = (f32[1024]{0:T(1024)S(1)}, f32[1024]{0:T(1024)S(1)}, u32[]{:S(2)}, u32[]{:S(2)}) collective-permute-start(f32[1024]{0:T(1024)S(1)} %copy-done.1), channel_id=1, source_target_pairs={{0,2},{5,7},{10,8},{15,13},{16,18},{21,23},{26,24},{31,29}} | collective-permute-start | bytes 12296 | tf_op jit(solution)/shard_map/ppermute | solution.py:474
  27.0 1.2 %collective-permute-done.5 = f32[1024]{0:T(1024)S(1)} collective-permute-done((f32[1024]{0:T(1024)S(1)}, f32[1024]{0:T(1024)S(1)}, u32[]{:S(2)}, u32[]{:S(2)}) %collective-permute-start.5) | collective-permute-done | bytes 4128 | tf_op jit(solution)/shard_map/ppermute | solution.py:474
  28.2 1.3 %collective-permute-start.6 = (f32[1024]{0:T(1024)S(1)}, f32[1024]{0:T(1024)S(1)}, u32[]{:S(2)}, u32[]{:S(2)}) collective-permute-start(f32[1024]{0:T(1024)S(1)} %broadcast_select_fusion.2), channel_id=1, source_target_pairs={{0,1},{2,3},{5,4},{7,6},{10,11},{8,9},{15,14},{13,12},{16,17},{18,... | collective-permute-start | bytes 12296 | tf_op jit(solution)/shard_map/ppermute | solution.py:474
  29.6 1.4 %gather_fusion.1 = s32[256]{0:T(256)S(1)} fusion(s32[1024]{0:T(1024)S(1)} %bitcast.30, s32[1024]{0:T(1024)S(1)} %pad_clamp_fusion), kind=kCustom, calls=%fused_computation.1 | custom fusion | bytes 3072 | tf_op jit(solution)/shard_map/gather | solution.py:570
  31.6 1.1 %convert_add_fusion.3 = f32[128,1024]{1,0:T(8,128)S(1)} fusion(f32[128,1024]{1,0:T(8,128)} %fusion.10, bf16[128,1024]{1,0:T(8,128)(2,1)S(1)} %collective-permute-done.7), kind=kLoop, calls=%fused_computation.11 | loop fusion | flops 262144 | bytes 1310720 | tf_op jit(solution)/shard_map/add | solution.py:521
  32.8 2.3 %collective-permute-start.8 = (bf16[64,1024]{1,0:T(8,128)(2,1)S(1)}, bf16[64,1024]{1,0:T(8,128)(2,1)S(1)}, u32[]{:S(2)}, u32[]{:S(2)}) collective-permute-start(bf16[64,1024]{1,0:T(8,128)(2,1)S(1)} %dynamic-slice_convert_fusion.3), channel_id=1, source_target_pairs={{0,2},{1,3},{2,0},{3,1},{4,6},{5,7},{6,4},{7,5},{8,10},{9,11},{10,... | collective-permute-start | bytes 393224 | tf_op jit(solution)/shard_map/ppermute | solution.py:20
  35.1 1.4 %convolution_convert_fusion.2 = bf16[128,1024]{1,0:T(8,128)(2,1)S(1)} fusion(bf16[1024,1024]{1,0:T(8,128)(2,1)S(1)} %bring.1, bf16[256,1024]{1,0:T(8,128)(2,1)} %collective-permute-done.9, s32[]{:T(128)S(6)} %select_n.168), kind=kOutput, calls=%fused_computation.4 | convolution fusion | flops 268566528 | bytes 2621444 | tf_op jit(solution)/shard_map/dot_general | solution.py:516
  36.6 1.4 %fusion.7 = f32[128,1024]{1,0:T(8,128)S(1)} fusion(bf16[1024,1024]{1,0:T(8,128)(2,1)S(1)} %bring.1, bf16[256,1024]{1,0:T(8,128)(2,1)} %collective-permute-done.9, s32[]{:T(128)S(6)} %select_n.167), kind=kOutput, calls=%fused_computation.25 | convolution fusion | flops 268435456 | bytes 2883588 | tf_op jit(solution)/shard_map/dot_general | solution.py:517
  39.1 8.3 %collective-permute-start.13 = (bf16[256,1024]{1,0:T(8,128)(2,1)}, bf16[256,1024]{1,0:T(8,128)(2,1)S(1)}, u32[]{:S(2)}, u32[]{:S(2)}) collective-permute-start(bf16[256,1024]{1,0:T(8,128)(2,1)} %collective-permute-done.12), channel_id=1, source_target_pairs={{0,4},{4,0},{8,12},{12,8},{1,5},{5,1},{9,13},{13,9},{2,6},{6,2},{1... | collective-permute-start | bytes 1572872 | tf_op jit(solution)/shard_map/ppermute | solution.py:20
  47.6 2.7 %collective-permute-start.4 = (bf16[1024,512]{1,0:T(8,128)(2,1)S(1)}, bf16[1024,512]{1,0:T(8,128)(2,1)S(1)}, u32[]{:S(2)}, u32[]{:S(2)}) collective-permute-start(bf16[1024,512]{1,0:T(8,128)(2,1)S(1)} %broadcast_select_fusion), channel_id=1, source_target_pairs={{0,1},{2,3},{5,4},{7,6},{10,11},{8,9},{15,14},{13,12},{16,17},{18,... | collective-permute-start | bytes 3145736 | tf_op jit(solution)/shard_map/ppermute | solution.py:474
  50.3 9.2 %collective-permute-done.13 = bf16[256,1024]{1,0:T(8,128)(2,1)S(1)} collective-permute-done((bf16[256,1024]{1,0:T(8,128)(2,1)}, bf16[256,1024]{1,0:T(8,128)(2,1)S(1)}, u32[]{:S(2)}, u32[]{:S(2)}) %collective-permute-start.13) | collective-permute-done | bytes 524320 | tf_op jit(solution)/shard_map/ppermute | solution.py:20
  59.5 1.2 %add.139 = bf16[256,1024]{1,0:T(8,128)(2,1)S(1)} add(bf16[256,1024]{1,0:T(8,128)(2,1)} %collective-permute-done.12, bf16[256,1024]{1,0:T(8,128)(2,1)S(1)} %collective-permute-done.13) | non-fusion elementwise | flops 262144 | bytes 1572864 | tf_op jit(solution)/shard_map/add | solution.py:579
  61.3 1.8 %collective-permute-start.17 = (bf16[256,1024]{1,0:T(8,128)(2,1)S(1)}, bf16[256,1024]{1,0:T(8,128)(2,1)S(1)}, u32[]{:S(2)}, u32[]{:S(2)}) collective-permute-start(bf16[256,1024]{1,0:T(8,128)(2,1)S(1)} %collective-permute-done.16), channel_id=1, source_target_pairs={{0,4},{4,0},{8,12},{12,8},{1,5},{5,1},{9,13},{13,9},{2,6},{6,2},{1... | collective-permute-start | bytes 1572872 | tf_op jit(solution)/shard_map/ppermute | solution.py:20
  64.2 11.5 %collective-permute-done.17 = bf16[256,1024]{1,0:T(8,128)(2,1)S(1)} collective-permute-done((bf16[256,1024]{1,0:T(8,128)(2,1)S(1)}, bf16[256,1024]{1,0:T(8,128)(2,1)S(1)}, u32[]{:S(2)}, u32[]{:S(2)}) %collective-permute-start.17) | collective-permute-done | bytes 524320 | tf_op jit(solution)/shard_map/ppermute | solution.py:20
  76.8 1.1 %collective-permute-done.18 = bf16[128,1024]{1,0:T(8,128)(2,1)S(1)} collective-permute-done((bf16[128,1024]{1,0:T(8,128)(2,1)S(1)}, bf16[128,1024]{1,0:T(8,128)(2,1)S(1)}, u32[]{:S(2)}, u32[]{:S(2)}) %collective-permute-start.18) | collective-permute-done | bytes 262176 | tf_op jit(solution)/shard_map/ppermute | solution.py:20
  78.5 5.1 %collective-permute-done.19 = bf16[64,1024]{1,0:T(8,128)(2,1)S(1)} collective-permute-done((bf16[64,1024]{1,0:T(8,128)(2,1)S(1)}, bf16[64,1024]{1,0:T(8,128)(2,1)S(1)}, u32[]{:S(2)}, u32[]{:S(2)}) %collective-permute-start.19) | collective-permute-done | bytes 131104 | tf_op jit(solution)/shard_map/ppermute | solution.py:20
  83.7 1.5 %logit_part.1 = (f32[256,512]{1,0:T(8,128)S(1)}, f32[1,256]{1,0:T(1,128)S(1)}, f32[1,256]{1,0:T(1,128)S(1)}, bf16[72,512]{1,0:T(8,128)(2,1)S(1)}, bf16[72,512]{1...) custom-call(s32[5]{0:T(128)S(1)} %stack.32.where_ref, bf16[1024,512]{1,0:T(8,128)(2,1)S(1)} %broadcast_select_fusion.1.un_ref, ...), custom_call_target="tpu_custom_call" | custom-call | tf_op jit(solution)/shard_map/logit_part/pallas_call | solution.py:384
  85.2 1.8 %collective-permute-start.20 = (bf16[72,512]{1,0:T(8,128)(2,1)S(1)}, bf16[72,512]{1,0:T(8,128)(2,1)S(1)}, u32[]{:S(2)}, u32[]{:S(2)}) collective-permute-start(bf16[72,512]{1,0:T(8,128)(2,1)S(1)} %get-tuple-element.51), channel_id=1, source_target_pairs={{0,4},{4,0},{8,12},{12,8},{1,5},{5,1},{9,13},{13,9},{2,6},{6,2},{1... | collective-permute-start | bytes 221192 | tf_op jit(solution)/shard_map/ppermute | solution.py:20
  87.1 2.6 %collective-permute-start.22 = (bf16[72,512]{1,0:T(8,128)(2,1)S(1)}, bf16[72,512]{1,0:T(8,128)(2,1)S(1)}, u32[]{:S(2)}, u32[]{:S(2)}) collective-permute-start(bf16[72,512]{1,0:T(8,128)(2,1)S(1)} %get-tuple-element.53), channel_id=1, source_target_pairs={{0,12},{4,8},{8,4},{12,0},{1,13},{5,9},{9,5},{13,1},{2,14},{6,10},... | collective-permute-start | bytes 221192 | tf_op jit(solution)/shard_map/ppermute | solution.py:20
  89.8 5.1 %collective-permute-done.21.rest_1_ = bf16[72,512]{1,0:T(8,128)(2,1)S(1)} collective-permute-done((bf16[72,512]{1,0:T(8,128)(2,1)S(1)}, bf16[72,512]{1,0:T(8,128)(2,1)S(1)}, u32[]{:S(2)}, u32[]{:S(2)}) %collective-permute-start.21) | collective-permute-done | bytes 73760 | tf_op jit(solution)/shard_map/ppermute | solution.py:20
  96.3 1.3 %collective-permute-start.25 = (f32[2,256]{1,0:T(2,128)S(1)}, f32[2,256]{1,0:T(2,128)S(1)}, u32[]{:S(2)}, u32[]{:S(2)}) collective-permute-start(f32[2,256]{1,0:T(2,128)S(1)} %final_part.1.refs_0_), channel_id=1, source_target_pairs={{0,3},{1,2},{2,1},{3,0},{4,7},{5,6},{6,5},{7,4},{8,11},{9,10},{10,... | collective-permute-start | bytes 6152 | tf_op jit(solution)/shard_map/ppermute | solution.py:20
  97.6 1.8 %collective-permute-done.24.refs_2_ = f32[2,256]{1,0:T(2,128)S(1)} collective-permute-done((f32[2,256]{1,0:T(2,128)S(1)}, f32[2,256]{1,0:T(2,128)S(1)}, u32[]{:S(2)}, u32[]{:S(2)}) %collective-permute-start.24) | collective-permute-done | bytes 2080 | tf_op jit(solution)/shard_map/ppermute | solution.py:20
  (84 shorter events, 8.3 us)
Async XLA Ops:
  3.8 13.8 %collective-permute-start = (bf16[32,1024]{1,0:T(8,128)(2,1)S(1)}, bf16[32,1024]{1,0:T(8,128)(2,1)S(1)}, u32[]{:S(2)}, u32[]{:S(2)}) collective-permute-start(bf16[32,1024]{1,0:T(8,128)(2,1)S(1)} %get-tuple-element.42.rest_0_), channel_id=1, source_target_pairs={{0,4},{4,0},{8,12},{12,8},{1,5},{5,1},{9,13},{13,9},{2,6},{6,2},{1... | collective-permute-start | bytes 196616 | tf_op jit(solution)/shard_map/ppermute | solution.py:20
  7.0 10.7 %collective-permute-start.1 = (bf16[32,1024]{1,0:T(8,128)(2,1)S(1)}, bf16[32,1024]{1,0:T(8,128)(2,1)S(1)}, u32[]{:S(2)}, u32[]{:S(2)}) collective-permute-start(bf16[32,1024]{1,0:T(8,128)(2,1)S(1)} %get-tuple-element.42.rest_0_), channel_id=1, source_target_pairs={{0,8},{4,12},{8,0},{12,4},{1,9},{5,13},{9,1},{13,5},{2,10},{6,14},... | collective-permute-start | bytes 196616 | tf_op jit(solution)/shard_map/ppermute | solution.py:20
  9.5 8.1 %collective-permute-start.2 = (bf16[32,1024]{1,0:T(8,128)(2,1)S(1)}, bf16[32,1024]{1,0:T(8,128)(2,1)S(1)}, u32[]{:S(2)}, u32[]{:S(2)}) collective-permute-start(bf16[32,1024]{1,0:T(8,128)(2,1)S(1)} %get-tuple-element.42.rest_0_), channel_id=1, source_target_pairs={{0,12},{4,8},{8,4},{12,0},{1,13},{5,9},{9,5},{13,1},{2,14},{6,10},... | collective-permute-start | bytes 196616 | tf_op jit(solution)/shard_map/ppermute | solution.py:20
  9.5 37.9 %collective-permute-start.3 = (bf16[1024,512]{1,0:T(8,128)(2,1)}, bf16[1024,512]{1,0:T(8,128)(2,1)}, u32[]{:S(2)}, u32[]{:S(2)}) collective-permute-start(bf16[1024,512]{1,0:T(8,128)(2,1)} %param.14), channel_id=1, source_target_pairs={{0,2},{5,7},{10,8},{15,13},{16,18},{21,23},{26,24},{31,29}} | collective-permute-start | bytes 3145736 | tf_op jit(solution)/shard_map/ppermute | solution.py:474
  19.3 15.8 %collective-permute-start.9 = (bf16[256,1024]{1,0:T(8,128)(2,1)S(1)}, bf16[256,1024]{1,0:T(8,128)(2,1)}, u32[]{:S(2)}, u32[]{:S(2)}) collective-permute-start(bf16[256,1024]{1,0:T(8,128)(2,1)S(1)} %carry_part.1.later_any), channel_id=1, source_target_pairs={{0,4},{4,0},{8,12},{12,8},{1,5},{5,1},{9,13},{13,9},{2,6},{6,2},{1... | collective-permute-start | bytes 1572872 | tf_op jit(solution)/shard_map/ppermute | solution.py:20
  19.4 19.7 %collective-permute-start.12 = (bf16[256,1024]{1,0:T(8,128)(2,1)S(1)}, bf16[256,1024]{1,0:T(8,128)(2,1)}, u32[]{:S(2)}, u32[]{:S(2)}) collective-permute-start(bf16[256,1024]{1,0:T(8,128)(2,1)S(1)} %carry_part.1.later_any), channel_id=1, source_target_pairs={{4,8},{8,4},{5,9},{9,5},{6,10},{10,6},{7,11},{11,7},{20,24},{24,20... | collective-permute-start | bytes 1572872 | tf_op jit(solution)/shard_map/ppermute | solution.py:575
  23.6 2.0 %copy-start.1 = (f32[1024]{0:T(1024)S(1)}, f32[1024]{0:T(1024)}, u32[]{:S(2)}) copy-start(f32[1024]{0:T(1024)} %param.13) | copy-start | bytes 12292
  23.6 3.3 %copy-start.3 = (s32[256]{0:T(256)S(1)}, s32[256]{0:T(256)}, u32[]{:S(2)}) copy-start(s32[256]{0:T(256)} %param.16) | copy-start | bytes 3076
  23.6 5.9 %copy-start.4 = (s32[256]{0:T(256)S(1)}, s32[256]{0:T(256)}, u32[]{:S(2)}) copy-start(s32[256]{0:T(256)} %param.15) | copy-start | bytes 3076
  23.6 8.0 %collective-permute-start.7 = (bf16[128,1024]{1,0:T(8,128)(2,1)}, bf16[128,1024]{1,0:T(8,128)(2,1)S(1)}, u32[]{:S(2)}, u32[]{:S(2)}) collective-permute-start(bf16[128,1024]{1,0:T(8,128)(2,1)} %convolution_convert_fusion.3), channel_id=1, source_target_pairs={{0,1},{1,0},{2,3},{3,2},{4,5},{5,4},{6,7},{7,6},{8,9},{9,8},{10,11... | collective-permute-start | bytes 786440 | tf_op jit(solution)/shard_map/ppermute | solution.py:20
  23.6 7.7 %copy-start.2 = (s32[256]{0:T(256)S(1)}, s32[256]{0:T(256)}, u32[]{:S(2)}) copy-start(s32[256]{0:T(256)} %param.17) | copy-start | bytes 3076
  25.6 2.6 %collective-permute-start.5 = (f32[1024]{0:T(1024)S(1)}, f32[1024]{0:T(1024)S(1)}, u32[]{:S(2)}, u32[]{:S(2)}) collective-permute-start(f32[1024]{0:T(1024)S(1)} %copy-done.1), channel_id=1, source_target_pairs={{0,2},{5,7},{10,8},{15,13},{16,18},{21,23},{26,24},{31,29}} | collective-permute-start | bytes 12296 | tf_op jit(solution)/shard_map/ppermute | solution.py:474
  28.2 3.4 %collective-permute-start.6 = (f32[1024]{0:T(1024)S(1)}, f32[1024]{0:T(1024)S(1)}, u32[]{:S(2)}, u32[]{:S(2)}) collective-permute-start(f32[1024]{0:T(1024)S(1)} %broadcast_select_fusion.2), channel_id=1, source_target_pairs={{0,1},{2,3},{5,4},{7,6},{10,11},{8,9},{15,14},{13,12},{16,17},{18,... | collective-permute-start | bytes 12296 | tf_op jit(solution)/shard_map/ppermute | solution.py:474
  32.8 5.5 %collective-permute-start.8 = (bf16[64,1024]{1,0:T(8,128)(2,1)S(1)}, bf16[64,1024]{1,0:T(8,128)(2,1)S(1)}, u32[]{:S(2)}, u32[]{:S(2)}) collective-permute-start(bf16[64,1024]{1,0:T(8,128)(2,1)S(1)} %dynamic-slice_convert_fusion.3), channel_id=1, source_target_pairs={{0,2},{1,3},{2,0},{3,1},{4,6},{5,7},{6,4},{7,5},{8,10},{9,11},{10,... | collective-permute-start | bytes 393224 | tf_op jit(solution)/shard_map/ppermute | solution.py:20
  36.5 1.6 %collective-permute-start.10 = (bf16[128,1024]{1,0:T(8,128)(2,1)S(1)}, bf16[128,1024]{1,0:T(8,128)(2,1)S(1)}, u32[]{:S(2)}, u32[]{:S(2)}) collective-permute-start(bf16[128,1024]{1,0:T(8,128)(2,1)S(1)} %convolution_convert_fusion.2), channel_id=1, source_target_pairs={{0,1},{1,0},{2,3},{3,2},{4,5},{5,4},{6,7},{7,6},{8,9},{9,8},{10,11... | collective-permute-start | bytes 786440 | tf_op jit(solution)/shard_map/ppermute | solution.py:20
  38.0 9.4 %copy-start = (bf16[1024,512]{1,0:T(8,128)(2,1)S(1)}, bf16[1024,512]{1,0:T(8,128)(2,1)}, u32[]{:S(2)}) copy-start(bf16[1024,512]{1,0:T(8,128)(2,1)} %param.14) | copy-start | bytes 3145732
  38.2 9.2 %collective-permute-start.11 = (bf16[64,1024]{1,0:T(8,128)(2,1)S(1)}, bf16[64,1024]{1,0:T(8,128)(2,1)S(1)}, u32[]{:S(2)}, u32[]{:S(2)}) collective-permute-start(bf16[64,1024]{1,0:T(8,128)(2,1)S(1)} %dynamic-slice_convert_fusion.2), channel_id=1, source_target_pairs={{0,2},{1,3},{2,0},{3,1},{4,6},{5,7},{6,4},{7,5},{8,10},{9,11},{10,... | collective-permute-start | bytes 393224 | tf_op jit(solution)/shard_map/ppermute | solution.py:20
  38.3 23.0 %collective-permute-start.16 = (bf16[256,1024]{1,0:T(8,128)(2,1)}, bf16[256,1024]{1,0:T(8,128)(2,1)S(1)}, u32[]{:S(2)}, u32[]{:S(2)}) collective-permute-start(bf16[256,1024]{1,0:T(8,128)(2,1)} %collective-permute-done.9), channel_id=1, source_target_pairs={{4,8},{8,4},{5,9},{9,5},{6,10},{10,6},{7,11},{11,7},{20,24},{24,20... | collective-permute-start | bytes 1572872 | tf_op jit(solution)/shard_map/ppermute | solution.py:576
  39.1 20.5 %collective-permute-start.13 = (bf16[256,1024]{1,0:T(8,128)(2,1)}, bf16[256,1024]{1,0:T(8,128)(2,1)S(1)}, u32[]{:S(2)}, u32[]{:S(2)}) collective-permute-start(bf16[256,1024]{1,0:T(8,128)(2,1)} %collective-permute-done.12), channel_id=1, source_target_pairs={{0,4},{4,0},{8,12},{12,8},{1,5},{5,1},{9,13},{13,9},{2,6},{6,2},{1... | collective-permute-start | bytes 1572872 | tf_op jit(solution)/shard_map/ppermute | solution.py:20
  47.6 36.0 %collective-permute-start.4 = (bf16[1024,512]{1,0:T(8,128)(2,1)S(1)}, bf16[1024,512]{1,0:T(8,128)(2,1)S(1)}, u32[]{:S(2)}, u32[]{:S(2)}) collective-permute-start(bf16[1024,512]{1,0:T(8,128)(2,1)S(1)} %broadcast_select_fusion), channel_id=1, source_target_pairs={{0,1},{2,3},{5,4},{7,6},{10,11},{8,9},{15,14},{13,12},{16,17},{18,... | collective-permute-start | bytes 3145736 | tf_op jit(solution)/shard_map/ppermute | solution.py:474
  61.2 2.3 %collective-permute-start.14 = (bf16[128,1024]{1,0:T(8,128)(2,1)S(1)}, bf16[128,1024]{1,0:T(8,128)(2,1)S(1)}, u32[]{:S(2)}, u32[]{:S(2)}) collective-permute-start(bf16[128,1024]{1,0:T(8,128)(2,1)S(1)} %convolution_convert_fusion.1), channel_id=1, source_target_pairs={{0,1},{1,0},{2,3},{3,2},{4,5},{5,4},{6,7},{7,6},{8,9},{9,8},{10,11... | collective-permute-start | bytes 786440 | tf_op jit(solution)/shard_map/ppermute | solution.py:20
  61.3 14.3 %collective-permute-start.17 = (bf16[256,1024]{1,0:T(8,128)(2,1)S(1)}, bf16[256,1024]{1,0:T(8,128)(2,1)S(1)}, u32[]{:S(2)}, u32[]{:S(2)}) collective-permute-start(bf16[256,1024]{1,0:T(8,128)(2,1)S(1)} %collective-permute-done.16), channel_id=1, source_target_pairs={{0,4},{4,0},{8,12},{12,8},{1,5},{5,1},{9,13},{13,9},{2,6},{6,2},{1... | collective-permute-start | bytes 1572872 | tf_op jit(solution)/shard_map/ppermute | solution.py:20
  63.7 14.8 %collective-permute-start.15 = (bf16[64,1024]{1,0:T(8,128)(2,1)S(1)}, bf16[64,1024]{1,0:T(8,128)(2,1)S(1)}, u32[]{:S(2)}, u32[]{:S(2)}) collective-permute-start(bf16[64,1024]{1,0:T(8,128)(2,1)S(1)} %dynamic-slice_convert_fusion.1), channel_id=1, source_target_pairs={{0,2},{1,3},{2,0},{3,1},{4,6},{5,7},{6,4},{7,5},{8,10},{9,11},{10,... | collective-permute-start | bytes 393224 | tf_op jit(solution)/shard_map/ppermute | solution.py:20
  76.3 1.6 %collective-permute-start.18 = (bf16[128,1024]{1,0:T(8,128)(2,1)S(1)}, bf16[128,1024]{1,0:T(8,128)(2,1)S(1)}, u32[]{:S(2)}, u32[]{:S(2)}) collective-permute-start(bf16[128,1024]{1,0:T(8,128)(2,1)S(1)} %convolution_convert_fusion), channel_id=1, source_target_pairs={{0,1},{1,0},{2,3},{3,2},{4,5},{5,4},{6,7},{7,6},{8,9},{9,8},{10,11... | collective-permute-start | bytes 786440 | tf_op jit(solution)/shard_map/ppermute | solution.py:20
  78.0 5.6 %collective-permute-start.19 = (bf16[64,1024]{1,0:T(8,128)(2,1)S(1)}, bf16[64,1024]{1,0:T(8,128)(2,1)S(1)}, u32[]{:S(2)}, u32[]{:S(2)}) collective-permute-start(bf16[64,1024]{1,0:T(8,128)(2,1)S(1)} %dynamic-slice_convert_fusion), channel_id=1, source_target_pairs={{0,2},{1,3},{2,0},{3,1},{4,6},{5,7},{6,4},{7,5},{8,10},{9,11},{10,... | collective-permute-start | bytes 393224 | tf_op jit(solution)/shard_map/ppermute | solution.py:20
  85.2 4.5 %collective-permute-start.20 = (bf16[72,512]{1,0:T(8,128)(2,1)S(1)}, bf16[72,512]{1,0:T(8,128)(2,1)S(1)}, u32[]{:S(2)}, u32[]{:S(2)}) collective-permute-start(bf16[72,512]{1,0:T(8,128)(2,1)S(1)} %get-tuple-element.51), channel_id=1, source_target_pairs={{0,4},{4,0},{8,12},{12,8},{1,5},{5,1},{9,13},{13,9},{2,6},{6,2},{1... | collective-permute-start | bytes 221192 | tf_op jit(solution)/shard_map/ppermute | solution.py:20
  87.0 7.8 %collective-permute-start.21 = (bf16[72,512]{1,0:T(8,128)(2,1)S(1)}, bf16[72,512]{1,0:T(8,128)(2,1)S(1)}, u32[]{:S(2)}, u32[]{:S(2)}) collective-permute-start(bf16[72,512]{1,0:T(8,128)(2,1)S(1)} %get-tuple-element.52), channel_id=1, source_target_pairs={{0,8},{4,12},{8,0},{12,4},{1,9},{5,13},{9,1},{13,5},{2,10},{6,14},... | collective-permute-start | bytes 221192 | tf_op jit(solution)/shard_map/ppermute | solution.py:20
  87.1 7.8 %collective-permute-start.22 = (bf16[72,512]{1,0:T(8,128)(2,1)S(1)}, bf16[72,512]{1,0:T(8,128)(2,1)S(1)}, u32[]{:S(2)}, u32[]{:S(2)}) collective-permute-start(bf16[72,512]{1,0:T(8,128)(2,1)S(1)} %get-tuple-element.53), channel_id=1, source_target_pairs={{0,12},{4,8},{8,4},{12,0},{1,13},{5,9},{9,5},{13,1},{2,14},{6,10},... | collective-permute-start | bytes 221192 | tf_op jit(solution)/shard_map/ppermute | solution.py:20
  95.7 1.9 %collective-permute-start.23 = (f32[2,256]{1,0:T(2,128)S(1)}, f32[2,256]{1,0:T(2,128)S(1)}, u32[]{:S(2)}, u32[]{:S(2)}) collective-permute-start(f32[2,256]{1,0:T(2,128)S(1)} %final_part.1.refs_0_), channel_id=1, source_target_pairs={{0,1},{1,0},{2,3},{3,2},{4,5},{5,4},{6,7},{7,6},{8,9},{9,8},{10,11... | collective-permute-start | bytes 6152 | tf_op jit(solution)/shard_map/ppermute | solution.py:20
  95.8 3.7 %collective-permute-start.24 = (f32[2,256]{1,0:T(2,128)S(1)}, f32[2,256]{1,0:T(2,128)S(1)}, u32[]{:S(2)}, u32[]{:S(2)}) collective-permute-start(f32[2,256]{1,0:T(2,128)S(1)} %final_part.1.refs_0_), channel_id=1, source_target_pairs={{0,2},{1,3},{2,0},{3,1},{4,6},{5,7},{6,4},{7,5},{8,10},{9,11},{10,... | collective-permute-start | bytes 6152 | tf_op jit(solution)/shard_map/ppermute | solution.py:20
  96.3 3.1 %collective-permute-start.25 = (f32[2,256]{1,0:T(2,128)S(1)}, f32[2,256]{1,0:T(2,128)S(1)}, u32[]{:S(2)}, u32[]{:S(2)}) collective-permute-start(f32[2,256]{1,0:T(2,128)S(1)} %final_part.1.refs_0_), channel_id=1, source_target_pairs={{0,3},{1,2},{2,1},{3,0},{4,7},{5,6},{6,5},{7,4},{8,11},{9,10},{10,... | collective-permute-start | bytes 6152 | tf_op jit(solution)/shard_map/ppermute | solution.py:20

commit v5 on v4

--- a/solution.py
+++ b/solution.py
@@ -343,7 +343,7 @@
     return jnp.concatenate([both, jnp.zeros((2, width - row.shape[1]), F32)], axis=1)
 
 
-def logit_kernel(share, peers, where_ref, un_ref, gain_ref, row_ref, id_ref, nat_ref, *rest):
+def logit_kernel(share, peers, where_ref, un_ref, row_ref, id_ref, nat_ref, *rest):
     slots = where_ref.shape[0] - 1
     slot_refs, rest = rest[:slots], rest[slots:]
     part_ref, square_ref, score_ref = rest[:3]
@@ -354,7 +354,7 @@
     total = values.shape[0]
     square = as_row(jnp.sum(values * values, axis=1, keepdims=True), total)
     square_ref[...] = square
-    part = jnp.dot((values * gain_ref[...]).astype(BF16), un_ref[...], preferred_element_type=F32)
+    part = jnp.dot(values.astype(BF16), un_ref[...], preferred_element_type=F32)
     part_ref[...] = part
     muts = row_ref.shape[0]
     vocab = part.shape[1]
@@ -375,7 +375,7 @@
             msg_refs[k - 1][share : share + 8, :] = extra
 
 
-def logit_part(where, slots, un, gains, mut_row, mut_id, mut_nat, peers):
+def logit_part(where, slots, un, mut_row, mut_id, mut_nat, peers):
     share, wide = slots[0].shape
     total = share * len(slots)
     vocab = un.shape[1]
@@ -383,7 +383,7 @@
     whole = pl.BlockSpec(memory_space=pltpu.VMEM)
     return pl.pallas_call(
         functools.partial(logit_kernel, share, peers),
-        in_specs=[pl.BlockSpec(memory_space=pltpu.SMEM)] + [whole] * (5 + len(slots)),
+        in_specs=[pl.BlockSpec(memory_space=pltpu.SMEM)] + [whole] * (4 + len(slots)),
         out_specs=[whole] * (3 + peers),
         out_shape=[
             jax.ShapeDtypeStruct((total, vocab), F32),
@@ -394,7 +394,7 @@
         scratch_shapes=[pltpu.VMEM((total, wide), F32)],
         compiler_params=SMALL,
         name="logit_part",
-    )(where, un, gains, mut_row, mut_id, mut_nat, *slots)
+    )(where, un, mut_row, mut_id, mut_nat, *slots)
 
 
 def final_kernel(feats, where_ref, log_ref, square_ref, score_ref, nat_ref, row_ref, *rest):
@@ -464,38 +464,44 @@
     )(*pieces)
 
 
-def owners(rows_held, rows_wanted):
-    return [i * rows_wanted // rows_held for i in range(lax.axis_size("ctx"))]
-
-
-def hand_on(value, owner, bit, holders):
+def choose_kernel(place_ref, *refs):
+    sources, (out_ref, sem) = refs[:-2], refs[-2:]
+    for k, source in enumerate(sources):
+
+        @pl.when(place_ref[0] == k)
+        def _():
+            copy = pltpu.make_async_copy(source, out_ref, sem)
+            copy.start()
+            copy.wait()
+
+
+def choose(place, sources):
+    return pl.pallas_call(
+        choose_kernel,
+        in_specs=[pl.BlockSpec(memory_space=pltpu.SMEM)] + [pl.BlockSpec(memory_space=pltpu.HBM)] * len(sources),
+        out_specs=in_vmem(),
+        out_shape=pltpu.VMEM(sources[0].shape, sources[0].dtype),
+        scratch_shapes=[pltpu.SemaphoreType.DMA],
+        compiler_params=SMALL,
+        name="choose",
+    )(place, *[pltpu.with_memory_space_constraint(v, pltpu.HBM) for v in sources])
+
+
+def feature_rows(unembed, norm_gain, rows_wanted, z, m):
     count, shards = lax.axis_size("ctx"), lax.axis_size("mp")
-    pairs = [(i * shards + (owner[i] ^ h), i * shards + (owner[i] ^ h ^ bit)) for i in range(count) for h in holders]
-    return lax.ppermute(value, ("ctx", "mp"), pairs)
-
-
-def feature_rows(unembed, norm_gain, rows_wanted, z, m):
-    shards = lax.axis_size("mp")
     held = unembed.shape[0]
+    scaled = (unembed.astype(F32) * norm_gain[:, None]).astype(BF16)
     if held % rows_wanted != 0:
-        unembed = lax.all_gather(unembed, "mp", axis=0, tiled=True)
-        norm_gain = lax.all_gather(norm_gain, "mp", axis=0, tiled=True)
-        return tuple(lax.dynamic_slice_in_dim(v, z * rows_wanted, rows_wanted, 0) for v in (unembed, norm_gain))
-    owner = owners(held, rows_wanted)
+        every = lax.all_gather(scaled, "mp", axis=0, tiled=True)
+        return lax.dynamic_slice_in_dim(every, z * rows_wanted, rows_wanted, 0)
     ratio = held // rows_wanted
-    place = m ^ (z // ratio)
-    result = []
-    for value in (unembed, norm_gain):
-        value = lax.dynamic_slice_in_dim(value, (z % ratio) * rows_wanted, rows_wanted, 0)
-        bit, holders, known = shards // 2, [0], place == 0
-        while bit:
-            moved = hand_on(value, owner, bit, holders)
-            value = jnp.where(known, value, moved)
-            holders = holders + [h ^ bit for h in holders]
-            known = sum((place == h).astype(jnp.int32) for h in holders) > 0
-            bit //= 2
-        result.append(value)
-    return tuple(result)
+    piece = lax.dynamic_slice_in_dim(scaled, (z % ratio) * rows_wanted, rows_wanted, 0)
+    copies = [piece]
+    for k in range(1, shards):
+        owner = [i // ratio for i in range(count)]
+        pairs = [(i * shards + owner[i], i * shards + (owner[i] ^ k)) for i in range(count)]
+        copies.append(lax.ppermute(piece, ("ctx", "mp"), pairs))
+    return choose((m ^ (z // ratio)).astype(jnp.int32)[None], copies)
 
 
 def split_half(value, upper):
@@ -555,19 +561,20 @@
     gated, nat_rows, native, mut_pos, mut_ids, z, m, norm_gain = lax.optimization_barrier(
         (gated, nat_rows, native, mut_pos, mut_ids, z, lax.axis_index("mp"), norm_gain)
     )
+    un = feature_rows(unembed, norm_gain, out_weight.shape[1], z, m)
+    piece = row_piece(m)
+    share = rows // shards
     if quick:
         nat_rows = jnp.stack([nat_rows[k][nat_at, : 2 * rows] for k in range(count)])[z ^ jnp.arange(count)]
     else:
         nat_rows = nat_rows[:, nat_at, : 2 * rows]
     nat_rows = nat_rows.astype(jnp.int32)
     nat_all = (nat_rows[:, :rows] * 256 + nat_rows[:, rows:]).reshape(-1)
-
-    un, gains = feature_rows(unembed, norm_gain, out_weight.shape[1], z, m)
-    piece = row_piece(m)
-    share = rows // shards
     block, inner = mut_pos // rows, mut_pos % rows
     mut_row = jnp.where(inner // share == piece, block * share + inner % share, -1)[:, None]
     mut_nat = nat_all[mut_pos][:, None]
+    mut_col = mut_ids[:, None]
+    own_nat = lax.dynamic_slice_in_dim(native, piece * share, share, 0)[:, None]
 
     if quick:
         middle = [(1, 2), (2, 1)]
@@ -592,7 +599,7 @@
     for part in blocks:
         slots.append(project(part, out_weight, m))
     peers = count - 1 if quick else 0
-    part, squares, scores, *msgs = logit_part(where, slots, un, gains[None, :], mut_row, mut_ids[:, None], mut_nat, peers)
+    part, squares, scores, *msgs = logit_part(where, slots, un, mut_row, mut_col, mut_nat, peers)
     if quick:
         for k in range(1, count):
             msgs[k - 1] = swap(msgs[k - 1], "ctx", k)
@@ -601,7 +608,6 @@
         squares = lax.psum(squares, "ctx")
         scores = lax.psum(scores, "ctx")
 
-    own_nat = lax.dynamic_slice_in_dim(native, piece * share, share, 0)[:, None]
     spot = jnp.stack([z, piece]).astype(jnp.int32)
     feats = norm_gain.shape[0] * shards
     span = max(rows, mut_pos.shape[0])

time: 100 us -> 105 us (1.050)
  starting transfers between devices: 38.1 us -> 32.5 us
  waiting for transfers between devices: 35.1 us -> 39.9 us
  other arithmetic: 3.18 us -> 5.59 us
  local copies, waits for them, and re-layouts: 2.74 us -> 4.96 us
  Pallas kernels: 12.8 us -> 14 us
    ppermute x20, starting transfers between devices: 26 us -> 19.8 us  [swap(): return lax.ppermute(value, axis, [(i, i ^ bit) for i in range(count)])]
    ppermute x20, waiting for transfers between devices: 33.8 us -> 39.8 us  [swap(): return lax.ppermute(value, axis, [(i, i ^ bit) for i in range(count)])]
    convert_element_type x0 -> x1, other arithmetic: none -> 2.49 us  [feature_rows(): scaled = (unembed.astype(F32) * norm_gain[:, None]).astype(BF16)]
    unnamed x11 -> x13, local copies, waits for them, and re-layouts: 0.03 us -> 1.59 us
    pallas_call x0 -> x1, Pallas kernels: none -> 1.24 us  [choose(): pl.pallas_call(choose_kernel, in_specs=[pl.BlockSpec(memory_space=pltpu.S...]
    ppermute x4 -> x3, waiting for transfers between devices: 1.24 us -> 0.01 us  [feature_rows(): copies.append(lax.ppermute(piece, ('ctx', 'mp'), pairs))]
    ppermute x4 -> x3, starting transfers between devices: 9.94 us -> 10.6 us  [feature_rows(): copies.append(lax.ppermute(piece, ('ctx', 'mp'), pairs))]
  transfers between devices with their start and end apart: 26 -> 25, of which waited for: 8 -> 12; matrix products, arithmetic and copies ran while one was open for 13% -> 12% of each run, Pallas kernels for 7% -> 6%
where the time goes in v5:
time: 105 us; the launch traced here: 104 us
  waiting for transfers between devices  39.9 us (38%)
  starting transfers between devices  32.5 us (31%)
  Pallas kernels  14 us (13%)
  matrix products  6.16 us (6%)
  other arithmetic  5.59 us (5%)
  local copies, waits for them, and re-layouts  4.96 us (5%)
  between operations  1.14 us (1%)
    ppermute x20, waiting for transfers between devices, swap(): return lax.ppermute(value, axis, [(i, i ^ bit) for i in range(count)])  39.8 us
    ppermute x20, starting transfers between devices, swap(): return lax.ppermute(value, axis, [(i, i ^ bit) for i in range(count)])  19.8 us
    ppermute x3, starting transfers between devices, feature_rows(): copies.append(lax.ppermute(piece, ('ctx', 'mp'), pairs))  10.6 us
    pallas_call x1, Pallas kernels, local_part(): pl.pallas_call(functools.partial(local_kernel, rows // SUBS, modes), in_s...  3.51 us
    dot_general x4, matrix products, project(): sent = jnp.dot(send, weight, preferred_element_type=F32).astype(BF16)  3.44 us
    pallas_call x1, Pallas kernels, end_part(): pl.pallas_call(functools.partial(end_kernel, steps, modes), in_specs=[pl....  3.2 us
    dot_general x4, matrix products, project(): jnp.dot(keep, weight, preferred_element_type=F32)  2.72 us
    convert_element_type x1, other arithmetic, feature_rows(): scaled = (unembed.astype(F32) * norm_gain[:, None]).astype(BF16)  2.49 us
  transfers between devices with their start and end apart: 25, of which 12 were waited for; matrix products, arithmetic and copies ran while one was open for 12% of the time, Pallas kernels for 6%

profile of v5, /device:TPU:0, one launch (start us, length us, event | category | flops | bytes accessed | tf_op | source)
XLA Modules:
  0.0 104.2 jit_solution(18166820005862336793)
XLA Ops:
  0.6 3.2 %end_part.1 = (f32[256,1024]{1,0:T(8,128)S(1)}, bf16[256,1024]{1,0:T(8,128)(2,1)S(1)}, bf16[32,1024]{1,0:T(8,128)(2,1)S(1)}, f32[3,3,1024]{2,1,0:T(4,128)S(1)}, f32[2,8,1024]{2,1,0:T(8,128)S(1)}) custom-call(bf16[3,256,1024]{2,1,0:T(8,128)(2,1)} %x_any.1, f32[3,3,1024]{2,1,0:T(4,128)} %filt_any.1, f32[2,8,1024]{2,1,0:T(8,128)} %bitcast.30, s32[1,256]{1,0:T(1,128)} %bitcast.34), custom_call_target="tpu_custom_call" | custom-call | tf_op jit(solution)/shard_map/end_part/pallas_call | solution.py:166
  3.8 3.1 %collective-permute-start = (bf16[32,1024]{1,0:T(8,128)(2,1)S(1)}, bf16[32,1024]{1,0:T(8,128)(2,1)S(1)}, u32[]{:S(2)}, u32[]{:S(2)}) collective-permute-start(bf16[32,1024]{1,0:T(8,128)(2,1)S(1)} %get-tuple-element.42.rest_0_), channel_id=1, source_target_pairs={{0,4},{4,0},{8,12},{12,8},{1,5},{5,1},{9,13},{13,9},{2,6},{6,2},{1... | collective-permute-start | bytes 196616 | tf_op jit(solution)/shard_map/ppermute | solution.py:20
  7.0 2.6 %collective-permute-start.1 = (bf16[32,1024]{1,0:T(8,128)(2,1)S(1)}, bf16[32,1024]{1,0:T(8,128)(2,1)S(1)}, u32[]{:S(2)}, u32[]{:S(2)}) collective-permute-start(bf16[32,1024]{1,0:T(8,128)(2,1)S(1)} %get-tuple-element.42.rest_0_), channel_id=1, source_target_pairs={{0,8},{4,12},{8,0},{12,4},{1,9},{5,13},{9,1},{13,5},{2,10},{6,14},... | collective-permute-start | bytes 196616 | tf_op jit(solution)/shard_map/ppermute | solution.py:20
  9.5 3.5 %local_part.1 = (f32[256,1024]{1,0:T(8,128)S(1)}, bf16[256,1024]{1,0:T(8,128)(2,1)S(1)}, f32[64,1024]{1,0:T(8,128)S(1)}) custom-call(f32[3,3,1024]{2,1,0:T(4,128)S(1)} %get-tuple-element.29.filt_ref, f32[2,8,1024]{2,1,0:T(8,128)S(1)} %get-tuple-element.30.mode_ref, ...), custom_call_target="tpu_custom_call", output_to_operand_aliasing={{0}: (2, {}), {1}: (3, {})} | custom-call | tf_op jit(solution)/shard_map/local_part/pallas_call | solution.py:192
  14.2 1.4 %collective-permute-done.2.rest_3_ = bf16[32,1024]{1,0:T(8,128)(2,1)S(1)} collective-permute-done((bf16[32,1024]{1,0:T(8,128)(2,1)S(1)}, bf16[32,1024]{1,0:T(8,128)(2,1)S(1)}, u32[]{:S(2)}, u32[]{:S(2)}) %collective-permute-start.2) | collective-permute-done | bytes 65568 | tf_op jit(solution)/shard_map/ppermute | solution.py:20
  15.6 1.5 %carry_part.1.later_any = bf16[256,1024]{1,0:T(8,128)(2,1)S(1)} custom-call(s32[1]{0:T(128)} %bitcast.where_ref, f32[3,3,1024]{2,1,0:T(4,128)S(1)} %get-tuple-element.29.filt_ref, f32[2,8,1024]{2,1,0:T(8,128)S(1)} %get-tuple-element.30.mode_ref, f32[256,1024]{1,0:T(8,128)S(1)} %get-tuple-element.33.y_ref, bf16[256,1024]{1,0:T(8,128)(2,1)S(1)} %get-tuple-element.34.gate_ref, ...), custom_call_target="tpu_custom_call" | custom-call | flops 8388608 | bytes 2097152 | tf_op jit(solution)/shard_map/carry_part/pallas_call | solution.py:297
  17.2 2.5 %multiply_convert_fusion.refs_0_ = bf16[1024,512]{1,0:T(8,128)(2,1)} fusion(bf16[1024,512]{1,0:T(8,128)(2,1)} %param.14, f32[1024]{0:T(1024)S(1)} %copy-done.3), kind=kLoop, calls=%fused_computation.2 | loop fusion | flops 1572864 | bytes 2101248 | tf_op jit(solution)/shard_map/convert_element_type | solution.py:493
  19.7 2.3 %collective-permute-start.3 = (bf16[1024,512]{1,0:T(8,128)(2,1)}, bf16[1024,512]{1,0:T(8,128)(2,1)}, u32[]{:S(2)}, u32[]{:S(2)}) collective-permute-start(bf16[1024,512]{1,0:T(8,128)(2,1)} %multiply_convert_fusion.refs_0_), channel_id=1, source_target_pairs={{0,1},{5,4},{10,11},{15,14},{16,17},{21,20},{26,27},{31,30}} | collective-permute-start | bytes 3145736 | tf_op jit(solution)/shard_map/ppermute | solution.py:503
  21.9 3.8 %collective-permute-start.4 = (bf16[1024,512]{1,0:T(8,128)(2,1)}, bf16[1024,512]{1,0:T(8,128)(2,1)}, u32[]{:S(2)}, u32[]{:S(2)}) collective-permute-start(bf16[1024,512]{1,0:T(8,128)(2,1)} %multiply_convert_fusion.refs_0_), channel_id=1, source_target_pairs={{0,2},{5,7},{10,8},{15,13},{16,18},{21,23},{26,24},{31,29}} | collective-permute-start | bytes 3145736 | tf_op jit(solution)/shard_map/ppermute | solution.py:503
  25.7 1.5 %collective-permute-start.11 = (bf16[256,1024]{1,0:T(8,128)(2,1)S(1)}, bf16[256,1024]{1,0:T(8,128)(2,1)}, u32[]{:S(2)}, u32[]{:S(2)}) collective-permute-start(bf16[256,1024]{1,0:T(8,128)(2,1)S(1)} %carry_part.1.later_any), channel_id=1, source_target_pairs={{4,8},{8,4},{5,9},{9,5},{6,10},{10,6},{7,11},{11,7},{20,24},{24,20... | collective-permute-start | bytes 1572872 | tf_op jit(solution)/shard_map/ppermute | solution.py:582
  27.8 1.6 %bring.1 = bf16[1024,1024]{1,0:T(8,128)(2,1)S(1)} custom-call(bf16[256,1024]{1,0:T(8,128)(2,1)S(1)} %carry_part.1.later_any, bf16[1024,1024]{1,0:T(8,128)(2,1)} %src_any.1), custom_call_target="tpu_custom_call" | custom-call | tf_op jit(solution)/shard_map/bring/pallas_call | solution.py:316
  29.9 1.1 %convolution_convert_fusion.3 = bf16[128,1024]{1,0:T(8,128)(2,1)} fusion(bf16[1024,1024]{1,0:T(8,128)(2,1)S(1)} %bring.1, bf16[256,1024]{1,0:T(8,128)(2,1)S(1)} %carry_part.1.later_any, s32[]{:T(128)S(6)} %select_n.129), kind=kOutput, calls=%fused_computation.6 | convolution fusion | flops 268566528 | bytes 2621444 | tf_op jit(solution)/shard_map/dot_general | solution.py:522
  31.1 1.7 %collective-permute-done.6 = bf16[128,1024]{1,0:T(8,128)(2,1)S(1)} collective-permute-done((bf16[128,1024]{1,0:T(8,128)(2,1)}, bf16[128,1024]{1,0:T(8,128)(2,1)S(1)}, u32[]{:S(2)}, u32[]{:S(2)}) %collective-permute-start.6) | collective-permute-done | bytes 262176 | tf_op jit(solution)/shard_map/ppermute | solution.py:20
  33.8 3.6 %collective-permute-done.8 = bf16[256,1024]{1,0:T(8,128)(2,1)} collective-permute-done((bf16[256,1024]{1,0:T(8,128)(2,1)S(1)}, bf16[256,1024]{1,0:T(8,128)(2,1)}, u32[]{:S(2)}, u32[]{:S(2)}) %collective-permute-start.8) | collective-permute-done | bytes 524320 | tf_op jit(solution)/shard_map/ppermute | solution.py:20
  37.4 1.4 %convolution_convert_fusion.2 = bf16[128,1024]{1,0:T(8,128)(2,1)S(1)} fusion(bf16[1024,1024]{1,0:T(8,128)(2,1)S(1)} %bring.1, bf16[256,1024]{1,0:T(8,128)(2,1)} %collective-permute-done.8, s32[]{:T(128)S(6)} %select_n.129), kind=kOutput, calls=%fused_computation.5 | convolution fusion | flops 268566528 | bytes 2621444 | tf_op jit(solution)/shard_map/dot_general | solution.py:522
  38.9 1.4 %fusion.7 = f32[128,1024]{1,0:T(8,128)S(1)} fusion(bf16[1024,1024]{1,0:T(8,128)(2,1)S(1)} %bring.1, bf16[256,1024]{1,0:T(8,128)(2,1)} %collective-permute-done.8, s32[]{:T(128)S(6)} %select_n.128), kind=kOutput, calls=%fused_computation.24 | convolution fusion | flops 268435456 | bytes 2883588 | tf_op jit(solution)/shard_map/dot_general | solution.py:523
  41.4 4.6 %collective-permute-start.5 = (bf16[1024,512]{1,0:T(8,128)(2,1)}, bf16[1024,512]{1,0:T(8,128)(2,1)}, u32[]{:S(2)}, u32[]{:S(2)}) collective-permute-start(bf16[1024,512]{1,0:T(8,128)(2,1)} %multiply_convert_fusion.refs_0_), channel_id=1, source_target_pairs={{0,3},{5,6},{10,9},{15,12},{16,19},{21,22},{26,25},{31,28}} | collective-permute-start | bytes 3145736 | tf_op jit(solution)/shard_map/ppermute | solution.py:503
  47.1 1.4 %gather_fusion.1 = s32[256]{0:T(256)S(1)} fusion(s32[1024]{0:T(1024)S(1)} %bitcast.29, s32[1024]{0:T(1024)S(1)} %pad_clamp_fusion), kind=kCustom, calls=%fused_computation.1 | custom fusion | bytes 3072 | tf_op jit(solution)/shard_map/gather | solution.py:575
  50.6 10.0 %collective-permute-done.12 = bf16[256,1024]{1,0:T(8,128)(2,1)} collective-permute-done((bf16[256,1024]{1,0:T(8,128)(2,1)}, bf16[256,1024]{1,0:T(8,128)(2,1)}, u32[]{:S(2)}, u32[]{:S(2)}) %collective-permute-start.12) | collective-permute-done | bytes 524320 | tf_op jit(solution)/shard_map/ppermute | solution.py:20
  60.5 1.4 %add.132 = bf16[256,1024]{1,0:T(8,128)(2,1)S(1)} add(bf16[256,1024]{1,0:T(8,128)(2,1)} %collective-permute-done.11, bf16[256,1024]{1,0:T(8,128)(2,1)} %collective-permute-done.12) | non-fusion elementwise | flops 262144 | bytes 1572864 | tf_op jit(solution)/shard_map/add | solution.py:586
  62.5 4.3 %collective-permute-start.16 = (bf16[256,1024]{1,0:T(8,128)(2,1)S(1)}, bf16[256,1024]{1,0:T(8,128)(2,1)S(1)}, u32[]{:S(2)}, u32[]{:S(2)}) collective-permute-start(bf16[256,1024]{1,0:T(8,128)(2,1)S(1)} %collective-permute-done.15), channel_id=1, source_target_pairs={{0,4},{4,0},{8,12},{12,8},{1,5},{5,1},{9,13},{13,9},{2,6},{6,2},{1... | collective-permute-start | bytes 1572872 | tf_op jit(solution)/shard_map/ppermute | solution.py:20
  67.3 1.2 %choose.1.un_ref = bf16[1024,512]{1,0:T(8,128)(2,1)S(1)} custom-call(s32[1]{0:T(128)} %bitcast.8.place_ref, bf16[1024,512]{1,0:T(8,128)(2,1)} %multiply_convert_fusion.refs_0_, bf16[1024,512]{1,0:T(8,128)(2,1)} %collective-permute-done.3.refs_1_, bf16[1024,512]{1,0:T(8,128)(2,1)} %collective-permute-done.4.refs_2_, ...), custom_call_target="tpu_custom_call" | custom-call | tf_op jit(solution)/shard_map/choose/pallas_call | solution.py:479
  69.4 8.7 %collective-permute-done.16 = bf16[256,1024]{1,0:T(8,128)(2,1)S(1)} collective-permute-done((bf16[256,1024]{1,0:T(8,128)(2,1)S(1)}, bf16[256,1024]{1,0:T(8,128)(2,1)S(1)}, u32[]{:S(2)}, u32[]{:S(2)}) %collective-permute-start.16) | collective-permute-done | bytes 524320 | tf_op jit(solution)/shard_map/ppermute | solution.py:20
  80.5 2.0 %collective-permute-start.18 = (bf16[64,1024]{1,0:T(8,128)(2,1)S(1)}, bf16[64,1024]{1,0:T(8,128)(2,1)S(1)}, u32[]{:S(2)}, u32[]{:S(2)}) collective-permute-start(bf16[64,1024]{1,0:T(8,128)(2,1)S(1)} %dynamic-slice_convert_fusion), channel_id=1, source_target_pairs={{0,2},{1,3},{2,0},{3,1},{4,6},{5,7},{6,4},{7,5},{8,10},{9,11},{10,... | collective-permute-start | bytes 393224 | tf_op jit(solution)/shard_map/ppermute | solution.py:20
  82.5 3.8 %collective-permute-done.18 = bf16[64,1024]{1,0:T(8,128)(2,1)S(1)} collective-permute-done((bf16[64,1024]{1,0:T(8,128)(2,1)S(1)}, bf16[64,1024]{1,0:T(8,128)(2,1)S(1)}, u32[]{:S(2)}, u32[]{:S(2)}) %collective-permute-start.18) | collective-permute-done | bytes 131104 | tf_op jit(solution)/shard_map/ppermute | solution.py:20
  86.3 1.5 %logit_part.1 = (f32[256,512]{1,0:T(8,128)S(1)}, f32[1,256]{1,0:T(1,128)S(1)}, f32[1,256]{1,0:T(1,128)S(1)}, bf16[72,512]{1,0:T(8,128)(2,1)S(1)}, bf16[72,512]{1...) custom-call(s32[5]{0:T(128)S(1)} %stack.32.where_ref, bf16[1024,512]{1,0:T(8,128)(2,1)S(1)} %choose.1.un_ref, ...), custom_call_target="tpu_custom_call" | custom-call | tf_op jit(solution)/shard_map/logit_part/pallas_call | solution.py:384
  87.8 1.8 %collective-permute-start.19 = (bf16[72,512]{1,0:T(8,128)(2,1)S(1)}, bf16[72,512]{1,0:T(8,128)(2,1)S(1)}, u32[]{:S(2)}, u32[]{:S(2)}) collective-permute-start(bf16[72,512]{1,0:T(8,128)(2,1)S(1)} %get-tuple-element.51), channel_id=1, source_target_pairs={{0,4},{4,0},{8,12},{12,8},{1,5},{5,1},{9,13},{13,9},{2,6},{6,2},{1... | collective-permute-start | bytes 221192 | tf_op jit(solution)/shard_map/ppermute | solution.py:20
  89.6 1.7 %collective-permute-start.20 = (bf16[72,512]{1,0:T(8,128)(2,1)S(1)}, bf16[72,512]{1,0:T(8,128)(2,1)S(1)}, u32[]{:S(2)}, u32[]{:S(2)}) collective-permute-start(bf16[72,512]{1,0:T(8,128)(2,1)S(1)} %get-tuple-element.52), channel_id=1, source_target_pairs={{0,8},{4,12},{8,0},{12,4},{1,9},{5,13},{9,1},{13,5},{2,10},{6,14},... | collective-permute-start | bytes 221192 | tf_op jit(solution)/shard_map/ppermute | solution.py:20
  91.3 1.2 %collective-permute-start.21 = (bf16[72,512]{1,0:T(8,128)(2,1)S(1)}, bf16[72,512]{1,0:T(8,128)(2,1)S(1)}, u32[]{:S(2)}, u32[]{:S(2)}) collective-permute-start(bf16[72,512]{1,0:T(8,128)(2,1)S(1)} %get-tuple-element.53), channel_id=1, source_target_pairs={{0,12},{4,8},{8,4},{12,0},{1,13},{5,9},{9,5},{13,1},{2,14},{6,10},... | collective-permute-start | bytes 221192 | tf_op jit(solution)/shard_map/ppermute | solution.py:20
  92.6 5.5 %collective-permute-done.20.rest_1_ = bf16[72,512]{1,0:T(8,128)(2,1)S(1)} collective-permute-done((bf16[72,512]{1,0:T(8,128)(2,1)S(1)}, bf16[72,512]{1,0:T(8,128)(2,1)S(1)}, u32[]{:S(2)}, u32[]{:S(2)}) %collective-permute-start.20) | collective-permute-done | bytes 73760 | tf_op jit(solution)/shard_map/ppermute | solution.py:20
  99.1 1.6 %collective-permute-start.23 = (f32[2,256]{1,0:T(2,128)S(1)}, f32[2,256]{1,0:T(2,128)S(1)}, u32[]{:S(2)}, u32[]{:S(2)}) collective-permute-start(f32[2,256]{1,0:T(2,128)S(1)} %final_part.1.refs_0_), channel_id=1, source_target_pairs={{0,2},{1,3},{2,0},{3,1},{4,6},{5,7},{6,4},{7,5},{8,10},{9,11},{10,... | collective-permute-start | bytes 6152 | tf_op jit(solution)/shard_map/ppermute | solution.py:20
  101.0 1.8 %collective-permute-done.23.refs_2_ = f32[2,256]{1,0:T(2,128)S(1)} collective-permute-done((f32[2,256]{1,0:T(2,128)S(1)}, f32[2,256]{1,0:T(2,128)S(1)}, u32[]{:S(2)}, u32[]{:S(2)}) %collective-permute-start.23) | collective-permute-done | bytes 2080 | tf_op jit(solution)/shard_map/ppermute | solution.py:20
  (82 shorter events, 14.4 us)
Async XLA Ops:
  3.8 9.2 %collective-permute-start = (bf16[32,1024]{1,0:T(8,128)(2,1)S(1)}, bf16[32,1024]{1,0:T(8,128)(2,1)S(1)}, u32[]{:S(2)}, u32[]{:S(2)}) collective-permute-start(bf16[32,1024]{1,0:T(8,128)(2,1)S(1)} %get-tuple-element.42.rest_0_), channel_id=1, source_target_pairs={{0,4},{4,0},{8,12},{12,8},{1,5},{5,1},{9,13},{13,9},{2,6},{6,2},{1... | collective-permute-start | bytes 196616 | tf_op jit(solution)/shard_map/ppermute | solution.py:20
  7.0 7.3 %collective-permute-start.1 = (bf16[32,1024]{1,0:T(8,128)(2,1)S(1)}, bf16[32,1024]{1,0:T(8,128)(2,1)S(1)}, u32[]{:S(2)}, u32[]{:S(2)}) collective-permute-start(bf16[32,1024]{1,0:T(8,128)(2,1)S(1)} %get-tuple-element.42.rest_0_), channel_id=1, source_target_pairs={{0,8},{4,12},{8,0},{12,4},{1,9},{5,13},{9,1},{13,5},{2,10},{6,14},... | collective-permute-start | bytes 196616 | tf_op jit(solution)/shard_map/ppermute | solution.py:20
  9.5 6.1 %collective-permute-start.2 = (bf16[32,1024]{1,0:T(8,128)(2,1)S(1)}, bf16[32,1024]{1,0:T(8,128)(2,1)S(1)}, u32[]{:S(2)}, u32[]{:S(2)}) collective-permute-start(bf16[32,1024]{1,0:T(8,128)(2,1)S(1)} %get-tuple-element.42.rest_0_), channel_id=1, source_target_pairs={{0,12},{4,8},{8,4},{12,0},{1,13},{5,9},{9,5},{13,1},{2,14},{6,10},... | collective-permute-start | bytes 196616 | tf_op jit(solution)/shard_map/ppermute | solution.py:20
  9.5 7.6 %copy-start.3 = (f32[1024]{0:T(1024)S(1)}, f32[1024]{0:T(1024)}, u32[]{:S(2)}) copy-start(f32[1024]{0:T(1024)} %param.13) | copy-start | bytes 12292
  19.7 47.6 %collective-permute-start.3 = (bf16[1024,512]{1,0:T(8,128)(2,1)}, bf16[1024,512]{1,0:T(8,128)(2,1)}, u32[]{:S(2)}, u32[]{:S(2)}) collective-permute-start(bf16[1024,512]{1,0:T(8,128)(2,1)} %multiply_convert_fusion.refs_0_), channel_id=1, source_target_pairs={{0,1},{5,4},{10,11},{15,14},{16,17},{21,20},{26,27},{31,30}} | collective-permute-start | bytes 3145736 | tf_op jit(solution)/shard_map/ppermute | solution.py:503
  21.9 45.4 %collective-permute-start.4 = (bf16[1024,512]{1,0:T(8,128)(2,1)}, bf16[1024,512]{1,0:T(8,128)(2,1)}, u32[]{:S(2)}, u32[]{:S(2)}) collective-permute-start(bf16[1024,512]{1,0:T(8,128)(2,1)} %multiply_convert_fusion.refs_0_), channel_id=1, source_target_pairs={{0,2},{5,7},{10,8},{15,13},{16,18},{21,23},{26,24},{31,29}} | collective-permute-start | bytes 3145736 | tf_op jit(solution)/shard_map/ppermute | solution.py:503
  25.7 11.7 %collective-permute-start.8 = (bf16[256,1024]{1,0:T(8,128)(2,1)S(1)}, bf16[256,1024]{1,0:T(8,128)(2,1)}, u32[]{:S(2)}, u32[]{:S(2)}) collective-permute-start(bf16[256,1024]{1,0:T(8,128)(2,1)S(1)} %carry_part.1.later_any), channel_id=1, source_target_pairs={{0,4},{4,0},{8,12},{12,8},{1,5},{5,1},{9,13},{13,9},{2,6},{6,2},{1... | collective-permute-start | bytes 1572872 | tf_op jit(solution)/shard_map/ppermute | solution.py:20
  25.7 20.3 %collective-permute-start.11 = (bf16[256,1024]{1,0:T(8,128)(2,1)S(1)}, bf16[256,1024]{1,0:T(8,128)(2,1)}, u32[]{:S(2)}, u32[]{:S(2)}) collective-permute-start(bf16[256,1024]{1,0:T(8,128)(2,1)S(1)} %carry_part.1.later_any), channel_id=1, source_target_pairs={{4,8},{8,4},{5,9},{9,5},{6,10},{10,6},{7,11},{11,7},{20,24},{24,20... | collective-permute-start | bytes 1572872 | tf_op jit(solution)/shard_map/ppermute | solution.py:582
  29.4 1.6 %copy-start.5 = (s32[256]{0:T(256)S(1)}, s32[256]{0:T(256)}, u32[]{:S(2)}) copy-start(s32[256]{0:T(256)} %param.16) | copy-start | bytes 3076
  31.1 1.7 %collective-permute-start.6 = (bf16[128,1024]{1,0:T(8,128)(2,1)}, bf16[128,1024]{1,0:T(8,128)(2,1)S(1)}, u32[]{:S(2)}, u32[]{:S(2)}) collective-permute-start(bf16[128,1024]{1,0:T(8,128)(2,1)} %convolution_convert_fusion.3), channel_id=1, source_target_pairs={{0,1},{1,0},{2,3},{3,2},{4,5},{5,4},{6,7},{7,6},{8,9},{9,8},{10,11... | collective-permute-start | bytes 786440 | tf_op jit(solution)/shard_map/ppermute | solution.py:20
  32.9 0.8 copy-start
  33.7 7.7 %collective-permute-start.7 = (bf16[64,1024]{1,0:T(8,128)(2,1)S(1)}, bf16[64,1024]{1,0:T(8,128)(2,1)S(1)}, u32[]{:S(2)}, u32[]{:S(2)}) collective-permute-start(bf16[64,1024]{1,0:T(8,128)(2,1)S(1)} %dynamic-slice_convert_fusion.3), channel_id=1, source_target_pairs={{0,2},{1,3},{2,0},{3,1},{4,6},{5,7},{6,4},{7,5},{8,10},{9,11},{10,... | collective-permute-start | bytes 393224 | tf_op jit(solution)/shard_map/ppermute | solution.py:20
  38.8 8.1 %copy-start.4 = (s32[256]{0:T(256)S(1)}, s32[256]{0:T(256)}, u32[]{:S(2)}) copy-start(s32[256]{0:T(256)} %param.17) | copy-start | bytes 3076
  38.8 1.6 %collective-permute-start.9 = (bf16[128,1024]{1,0:T(8,128)(2,1)S(1)}, bf16[128,1024]{1,0:T(8,128)(2,1)S(1)}, u32[]{:S(2)}, u32[]{:S(2)}) collective-permute-start(bf16[128,1024]{1,0:T(8,128)(2,1)S(1)} %convolution_convert_fusion.2), channel_id=1, source_target_pairs={{0,1},{1,0},{2,3},{3,2},{4,5},{5,4},{6,7},{7,6},{8,9},{9,8},{10,11... | collective-permute-start | bytes 786440 | tf_op jit(solution)/shard_map/ppermute | solution.py:20
  40.3 9.2 %copy-start.1 = (f32[128,1024]{1,0:T(8,128)S(1)}, f32[128,1024]{1,0:T(8,128)}, u32[]{:S(2)}) copy-start(f32[128,1024]{1,0:T(8,128)} %copy-done) | copy-start | bytes 1572868
  40.5 0.8 copy-start.2
  41.3 7.5 %collective-permute-start.10 = (bf16[64,1024]{1,0:T(8,128)(2,1)S(1)}, bf16[64,1024]{1,0:T(8,128)(2,1)}, u32[]{:S(2)}, u32[]{:S(2)}) collective-permute-start(bf16[64,1024]{1,0:T(8,128)(2,1)S(1)} %dynamic-slice_convert_fusion.2), channel_id=1, source_target_pairs={{0,2},{1,3},{2,0},{3,1},{4,6},{5,7},{6,4},{7,5},{8,10},{9,11},{10,... | collective-permute-start | bytes 393224 | tf_op jit(solution)/shard_map/ppermute | solution.py:20
  41.4 25.9 %collective-permute-start.5 = (bf16[1024,512]{1,0:T(8,128)(2,1)}, bf16[1024,512]{1,0:T(8,128)(2,1)}, u32[]{:S(2)}, u32[]{:S(2)}) collective-permute-start(bf16[1024,512]{1,0:T(8,128)(2,1)} %multiply_convert_fusion.refs_0_), channel_id=1, source_target_pairs={{0,3},{5,6},{10,9},{15,12},{16,19},{21,22},{26,25},{31,28}} | collective-permute-start | bytes 3145736 | tf_op jit(solution)/shard_map/ppermute | solution.py:503
  46.0 14.5 %collective-permute-start.12 = (bf16[256,1024]{1,0:T(8,128)(2,1)}, bf16[256,1024]{1,0:T(8,128)(2,1)}, u32[]{:S(2)}, u32[]{:S(2)}) collective-permute-start(bf16[256,1024]{1,0:T(8,128)(2,1)} %collective-permute-done.11), channel_id=1, source_target_pairs={{0,4},{4,0},{8,12},{12,8},{1,5},{5,1},{9,13},{13,9},{2,6},{6,2},{1... | collective-permute-start | bytes 1572872 | tf_op jit(solution)/shard_map/ppermute | solution.py:20
  48.8 13.7 %collective-permute-start.15 = (bf16[256,1024]{1,0:T(8,128)(2,1)}, bf16[256,1024]{1,0:T(8,128)(2,1)S(1)}, u32[]{:S(2)}, u32[]{:S(2)}) collective-permute-start(bf16[256,1024]{1,0:T(8,128)(2,1)} %collective-permute-done.8), channel_id=1, source_target_pairs={{4,8},{8,4},{5,9},{9,5},{6,10},{10,6},{7,11},{11,7},{20,24},{24,20... | collective-permute-start | bytes 1572872 | tf_op jit(solution)/shard_map/ppermute | solution.py:583
  62.4 6.2 %collective-permute-start.13 = (bf16[128,1024]{1,0:T(8,128)(2,1)S(1)}, bf16[128,1024]{1,0:T(8,128)(2,1)S(1)}, u32[]{:S(2)}, u32[]{:S(2)}) collective-permute-start(bf16[128,1024]{1,0:T(8,128)(2,1)S(1)} %convolution_convert_fusion.1), channel_id=1, source_target_pairs={{0,1},{1,0},{2,3},{3,2},{4,5},{5,4},{6,7},{7,6},{8,9},{9,8},{10,11... | collective-permute-start | bytes 786440 | tf_op jit(solution)/shard_map/ppermute | solution.py:20
  62.5 15.7 %collective-permute-start.16 = (bf16[256,1024]{1,0:T(8,128)(2,1)S(1)}, bf16[256,1024]{1,0:T(8,128)(2,1)S(1)}, u32[]{:S(2)}, u32[]{:S(2)}) collective-permute-start(bf16[256,1024]{1,0:T(8,128)(2,1)S(1)} %collective-permute-done.15), channel_id=1, source_target_pairs={{0,4},{4,0},{8,12},{12,8},{1,5},{5,1},{9,13},{13,9},{2,6},{6,2},{1... | collective-permute-start | bytes 1572872 | tf_op jit(solution)/shard_map/ppermute | solution.py:20
  68.7 13.8 %collective-permute-start.14 = (bf16[64,1024]{1,0:T(8,128)(2,1)S(1)}, bf16[64,1024]{1,0:T(8,128)(2,1)S(1)}, u32[]{:S(2)}, u32[]{:S(2)}) collective-permute-start(bf16[64,1024]{1,0:T(8,128)(2,1)S(1)} %dynamic-slice_convert_fusion.1), channel_id=1, source_target_pairs={{0,2},{1,3},{2,0},{3,1},{4,6},{5,7},{6,4},{7,5},{8,10},{9,11},{10,... | collective-permute-start | bytes 393224 | tf_op jit(solution)/shard_map/ppermute | solution.py:20
  78.8 1.6 %collective-permute-start.17 = (bf16[128,1024]{1,0:T(8,128)(2,1)S(1)}, bf16[128,1024]{1,0:T(8,128)(2,1)S(1)}, u32[]{:S(2)}, u32[]{:S(2)}) collective-permute-start(bf16[128,1024]{1,0:T(8,128)(2,1)S(1)} %convolution_convert_fusion), channel_id=1, source_target_pairs={{0,1},{1,0},{2,3},{3,2},{4,5},{5,4},{6,7},{7,6},{8,9},{9,8},{10,11... | collective-permute-start | bytes 786440 | tf_op jit(solution)/shard_map/ppermute | solution.py:20
  80.5 5.8 %collective-permute-start.18 = (bf16[64,1024]{1,0:T(8,128)(2,1)S(1)}, bf16[64,1024]{1,0:T(8,128)(2,1)S(1)}, u32[]{:S(2)}, u32[]{:S(2)}) collective-permute-start(bf16[64,1024]{1,0:T(8,128)(2,1)S(1)} %dynamic-slice_convert_fusion), channel_id=1, source_target_pairs={{0,2},{1,3},{2,0},{3,1},{4,6},{5,7},{6,4},{7,5},{8,10},{9,11},{10,... | collective-permute-start | bytes 393224 | tf_op jit(solution)/shard_map/ppermute | solution.py:20
  87.8 4.8 %collective-permute-start.19 = (bf16[72,512]{1,0:T(8,128)(2,1)S(1)}, bf16[72,512]{1,0:T(8,128)(2,1)S(1)}, u32[]{:S(2)}, u32[]{:S(2)}) collective-permute-start(bf16[72,512]{1,0:T(8,128)(2,1)S(1)} %get-tuple-element.51), channel_id=1, source_target_pairs={{0,4},{4,0},{8,12},{12,8},{1,5},{5,1},{9,13},{13,9},{2,6},{6,2},{1... | collective-permute-start | bytes 221192 | tf_op jit(solution)/shard_map/ppermute | solution.py:20
  89.6 8.5 %collective-permute-start.20 = (bf16[72,512]{1,0:T(8,128)(2,1)S(1)}, bf16[72,512]{1,0:T(8,128)(2,1)S(1)}, u32[]{:S(2)}, u32[]{:S(2)}) collective-permute-start(bf16[72,512]{1,0:T(8,128)(2,1)S(1)} %get-tuple-element.52), channel_id=1, source_target_pairs={{0,8},{4,12},{8,0},{12,4},{1,9},{5,13},{9,1},{13,5},{2,10},{6,14},... | collective-permute-start | bytes 221192 | tf_op jit(solution)/shard_map/ppermute | solution.py:20
  91.3 6.8 %collective-permute-start.21 = (bf16[72,512]{1,0:T(8,128)(2,1)S(1)}, bf16[72,512]{1,0:T(8,128)(2,1)S(1)}, u32[]{:S(2)}, u32[]{:S(2)}) collective-permute-start(bf16[72,512]{1,0:T(8,128)(2,1)S(1)} %get-tuple-element.53), channel_id=1, source_target_pairs={{0,12},{4,8},{8,4},{12,0},{1,13},{5,9},{9,5},{13,1},{2,14},{6,10},... | collective-permute-start | bytes 221192 | tf_op jit(solution)/shard_map/ppermute | solution.py:20
  99.0 1.9 %collective-permute-start.22 = (f32[2,256]{1,0:T(2,128)S(1)}, f32[2,256]{1,0:T(2,128)S(1)}, u32[]{:S(2)}, u32[]{:S(2)}) collective-permute-start(f32[2,256]{1,0:T(2,128)S(1)} %final_part.1.refs_0_), channel_id=1, source_target_pairs={{0,1},{1,0},{2,3},{3,2},{4,5},{5,4},{6,7},{7,6},{8,9},{9,8},{10,11... | collective-permute-start | bytes 6152 | tf_op jit(solution)/shard_map/ppermute | solution.py:20
  99.1 3.7 %collective-permute-start.23 = (f32[2,256]{1,0:T(2,128)S(1)}, f32[2,256]{1,0:T(2,128)S(1)}, u32[]{:S(2)}, u32[]{:S(2)}) collective-permute-start(f32[2,256]{1,0:T(2,128)S(1)} %final_part.1.refs_0_), channel_id=1, source_target_pairs={{0,2},{1,3},{2,0},{3,1},{4,6},{5,7},{6,4},{7,5},{8,10},{9,11},{10,... | collective-permute-start | bytes 6152 | tf_op jit(solution)/shard_map/ppermute | solution.py:20
  100.7 3.0 %collective-permute-start.24 = (f32[2,256]{1,0:T(2,128)S(1)}, f32[2,256]{1,0:T(2,128)S(1)}, u32[]{:S(2)}, u32[]{:S(2)}) collective-permute-start(f32[2,256]{1,0:T(2,128)S(1)} %final_part.1.refs_0_), channel_id=1, source_target_pairs={{0,3},{1,2},{2,1},{3,0},{4,7},{5,6},{6,5},{7,4},{8,11},{9,10},{10,... | collective-permute-start | bytes 6152 | tf_op jit(solution)/shard_map/ppermute | solution.py:20

commit v6 on v5

--- a/solution.py
+++ b/solution.py
@@ -343,13 +343,16 @@
     return jnp.concatenate([both, jnp.zeros((2, width - row.shape[1]), F32)], axis=1)
 
 
-def logit_kernel(share, peers, where_ref, un_ref, row_ref, id_ref, nat_ref, *rest):
+def logit_kernel(share, given, peers, where_ref, un_ref, row_ref, id_ref, nat_ref, *rest):
     slots = where_ref.shape[0] - 1
-    slot_refs, rest = rest[:slots], rest[slots:]
+    slot_refs, rest = rest[:given], rest[given:]
     part_ref, square_ref, score_ref = rest[:3]
     msg_refs, acc = rest[3 : 3 + peers], rest[-1]
-    for k in range(slots):
-        acc[pl.ds(pl.multiple_of(where_ref[k] * share, share), share), :] = slot_refs[k][...]
+    at = 0
+    for slot_ref in slot_refs:
+        for k in range(slot_ref.shape[0] // share):
+            acc[pl.ds(pl.multiple_of(where_ref[at] * share, share), share), :] = slot_ref[k * share : (k + 1) * share, :]
+            at += 1
     values = acc[...]
     total = values.shape[0]
     square = as_row(jnp.sum(values * values, axis=1, keepdims=True), total)
@@ -375,14 +378,14 @@
             msg_refs[k - 1][share : share + 8, :] = extra
 
 
-def logit_part(where, slots, un, mut_row, mut_id, mut_nat, peers):
-    share, wide = slots[0].shape
-    total = share * len(slots)
+def logit_part(share, where, slots, un, mut_row, mut_id, mut_nat, peers):
+    wide = slots[0].shape[1]
+    total = share * (where.shape[0] - 1)
     vocab = un.shape[1]
     muts = mut_row.shape[0]
     whole = pl.BlockSpec(memory_space=pltpu.VMEM)
     return pl.pallas_call(
-        functools.partial(logit_kernel, share, peers),
+        functools.partial(logit_kernel, share, len(slots), peers),
         in_specs=[pl.BlockSpec(memory_space=pltpu.SMEM)] + [whole] * (4 + len(slots)),
         out_specs=[whole] * (3 + peers),
         out_shape=[
@@ -504,29 +507,52 @@
     return choose((m ^ (z // ratio)).astype(jnp.int32)[None], copies)
 
 
-def split_half(value, upper):
-    half = value.shape[0] // 2
-    keep = lax.dynamic_slice_in_dim(value, upper * half, half, 0)
-    send = lax.dynamic_slice_in_dim(value, (1 - upper) * half, half, 0)
-    return keep, send
-
-
-def project(gated, weight, m):
-    shards = lax.axis_size("mp")
-    bit = 1
-    value = None
+def half_kernel(groups, which_ref, weight_ref, *refs):
+    out_ref = refs[-1]
+    half = refs[0].shape[0] // 2
+    rows = pl.ds(pl.multiple_of(which_ref[0] * half, half), half)
+    parts, at = [], 0
+    for size in groups:
+        parts.append(functools.reduce(lambda p, q: p + q, [ref[rows, :] for ref in refs[at : at + size]]))
+        at += size
+    block = parts[0] if len(parts) == 1 else jnp.concatenate(parts, axis=0)
+    out_ref[...] = jnp.dot(block, weight_ref[...], preferred_element_type=F32).astype(out_ref.dtype)
+
+
+def half_part(which, weight, blocks, dtype):
+    rows = len(blocks) * (blocks[0][0].shape[0] // 2)
+    flat = [part for block in blocks for part in block]
+    return pl.pallas_call(
+        functools.partial(half_kernel, tuple(len(block) for block in blocks)),
+        in_specs=[pl.BlockSpec(memory_space=pltpu.SMEM)] + [in_vmem()] * (1 + len(flat)),
+        out_specs=in_vmem(),
+        out_shape=jax.ShapeDtypeStruct((rows, weight.shape[1]), dtype),
+        compiler_params=SMALL,
+        name="half_part",
+    )(which.astype(jnp.int32)[None], weight, *flat)
+
+
+def project(blocks, weight, m):
+    shards, count = lax.axis_size("mp"), len(blocks)
+    if shards == 1:
+        whole = [functools.reduce(lambda p, q: p + q, block) for block in blocks]
+        return jnp.dot(jnp.concatenate(whole, axis=0), weight, preferred_element_type=F32)
+    bit, value = 1, None
     while bit < shards:
         upper = (m // bit) % 2
-        keep, send = split_half(gated if value is None else value, upper)
         if value is None:
-            sent = jnp.dot(send, weight, preferred_element_type=F32).astype(BF16)
-            keep = lax.optimization_barrier(jnp.dot(keep, weight, preferred_element_type=F32))
+            send = half_part(1 - upper, weight, blocks, BF16)
+            keep = half_part(upper, weight, blocks, F32)
         else:
-            sent = send.astype(BF16)
-        got = swap(sent, "mp", bit)
+            half = value.shape[0] // count // 2
+            pieces = value.reshape(count, 2, half, value.shape[1])
+            keep = lax.dynamic_index_in_dim(pieces, upper, 1, False).reshape(count * half, value.shape[1])
+            send = lax.dynamic_index_in_dim(pieces, 1 - upper, 1, False).reshape(count * half, value.shape[1])
+            send = send.astype(BF16)
+        got = swap(send, "mp", bit)
         value = keep + got.astype(F32)
         bit *= 2
-    return jnp.dot(gated, weight, preferred_element_type=F32) if value is None else value
+    return value
 
 
 def row_piece(m):
@@ -583,23 +609,21 @@
         mid_b = lax.ppermute(beside, "ctx", middle)
         far_a = swap(mid_a, "ctx", 1)
         far_b = swap(mid_b, "ctx", 1)
-        third = mid_a + far_a
-        fourth = mid_b + far_b
-        blocks = [gated, beside, third, fourth]
+        groups = [[[gated], [beside]], [[mid_a, far_a]], [[mid_b, far_b]]]
         low = z < 2
         where = [z, z ^ 1, jnp.where(low, 2, 1), jnp.where(low, 3, 0)]
     else:
         every = lax.all_gather(gated, "ctx")
-        blocks = [every[b] for b in range(count)]
+        groups = [[[every[b]]] for b in range(count)]
         where = list(range(count))
     where = jnp.stack([jnp.asarray(w, jnp.int32) for w in where + [z]])
     if quick:
         out_weight = bring(gated, out_weight)
     slots = []
-    for part in blocks:
-        slots.append(project(part, out_weight, m))
+    for blocks in groups:
+        slots.append(project(blocks, out_weight, m))
     peers = count - 1 if quick else 0
-    part, squares, scores, *msgs = logit_part(where, slots, un, mut_row, mut_col, mut_nat, peers)
+    part, squares, scores, *msgs = logit_part(share, where, slots, un, mut_row, mut_col, mut_nat, peers)
     if quick:
         for k in range(1, count):
             msgs[k - 1] = swap(msgs[k - 1], "ctx", k)

time: 105 us -> 104 us (level)
  waiting for transfers between devices: 39.9 us -> 22.8 us
  starting transfers between devices: 32.5 us -> 49.3 us
  Pallas kernels: 14 us -> 22.5 us
  matrix products: 6.16 us -> 0 us
  local copies, waits for them, and re-layouts: 4.96 us -> 3.4 us
  other arithmetic: 5.59 us -> 4.1 us
    ppermute x20 -> x18, starting transfers between devices: 19.8 us -> 38.1 us  [swap(): return lax.ppermute(value, axis, [(i, i ^ bit) for i in range(count)])]
    ppermute x20 -> x18, waiting for transfers between devices: 39.8 us -> 22.8 us  [swap(): return lax.ppermute(value, axis, [(i, i ^ bit) for i in range(count)])]
    pallas_call x1 -> x7, Pallas kernels: 1.49 us -> 9.97 us  [the longest x6 8.49 us: half_part(): pl.pallas_call(functools.partial(half_kernel, tuple((len(block) for block...]
    dot_general x8 -> x0, matrix products: 6.16 us -> none  [the longest x4 3.44 us: project(): sent = jnp.dot(send, weight, preferred_element_type=F32).astype(BF16)]
    ppermute x3, starting transfers between devices: 10.6 us -> 8.27 us  [feature_rows(): copies.append(lax.ppermute(piece, ('ctx', 'mp'), pairs))]
    add x2 -> x0, other arithmetic: 1.58 us -> none  [the longest x1 1.39 us: body(): third = mid_a + far_a]
    unnamed x13 -> x11, local copies, waits for them, and re-layouts: 1.59 us -> 0.03 us
  transfers between devices with their start and end apart: 25 -> 23, of which waited for: 12 -> 8; matrix products, arithmetic and copies ran while one was open for 12% -> 7% of each run, Pallas kernels for 6% -> 14%
where the time goes in v6:
time: 104 us; the launch traced here: 103 us
  starting transfers between devices  49.3 us (47%)
  waiting for transfers between devices  22.8 us (22%)
  Pallas kernels  22.5 us (22%)
  other arithmetic  4.1 us (4%)
  local copies, waits for them, and re-layouts  3.4 us (3%)
    ppermute x18, starting transfers between devices, swap(): return lax.ppermute(value, axis, [(i, i ^ bit) for i in range(count)])  38.1 us
    ppermute x18, waiting for transfers between devices, swap(): return lax.ppermute(value, axis, [(i, i ^ bit) for i in range(count)])  22.8 us
    pallas_call x6, Pallas kernels, half_part(): pl.pallas_call(functools.partial(half_kernel, tuple((len(block) for block...  8.49 us
    ppermute x3, starting transfers between devices, feature_rows(): copies.append(lax.ppermute(piece, ('ctx', 'mp'), pairs))  8.27 us
    pallas_call x1, Pallas kernels, local_part(): pl.pallas_call(functools.partial(local_kernel, rows // SUBS, modes), in_s...  3.51 us
    pallas_call x1, Pallas kernels, end_part(): pl.pallas_call(functools.partial(end_kernel, steps, modes), in_specs=[pl....  3.2 us
    convert_element_type x1, other arithmetic, feature_rows(): scaled = (unembed.astype(F32) * norm_gain[:, None]).astype(BF16)  2.49 us
  transfers between devices with their start and end apart: 23, of which 8 were waited for; matrix products, arithmetic and copies ran while one was open for 7% of the time, Pallas kernels for 14%

profile of v6, /device:TPU:0, one launch (start us, length us, event | category | flops | bytes accessed | tf_op | source)
XLA Modules:
  0.0 103.1 jit_solution(3174908536778438168)
XLA Ops:
  0.6 3.2 %end_part.1 = (f32[256,1024]{1,0:T(8,128)S(1)}, bf16[256,1024]{1,0:T(8,128)(2,1)S(1)}, bf16[32,1024]{1,0:T(8,128)(2,1)S(1)}, f32[3,3,1024]{2,1,0:T(4,128)S(1)}, f32[2,8,1024]{2,1,0:T(8,128)S(1)}) custom-call(bf16[3,256,1024]{2,1,0:T(8,128)(2,1)} %x_any.1, f32[3,3,1024]{2,1,0:T(4,128)} %filt_any.1, f32[2,8,1024]{2,1,0:T(8,128)} %bitcast.49, s32[1,256]{1,0:T(1,128)} %bitcast.53), custom_call_target="tpu_custom_call" | custom-call | tf_op jit(solution)/shard_map/end_part/pallas_call | solution.py:166
  3.8 3.1 %collective-permute-start = (bf16[32,1024]{1,0:T(8,128)(2,1)S(1)}, bf16[32,1024]{1,0:T(8,128)(2,1)S(1)}, u32[]{:S(2)}, u32[]{:S(2)}) collective-permute-start(bf16[32,1024]{1,0:T(8,128)(2,1)S(1)} %get-tuple-element.42.rest_0_), channel_id=1, source_target_pairs={{0,4},{4,0},{8,12},{12,8},{1,5},{5,1},{9,13},{13,9},{2,6},{6,2},{1... | collective-permute-start | bytes 196616 | tf_op jit(solution)/shard_map/ppermute | solution.py:20
  7.0 2.6 %collective-permute-start.1 = (bf16[32,1024]{1,0:T(8,128)(2,1)S(1)}, bf16[32,1024]{1,0:T(8,128)(2,1)S(1)}, u32[]{:S(2)}, u32[]{:S(2)}) collective-permute-start(bf16[32,1024]{1,0:T(8,128)(2,1)S(1)} %get-tuple-element.42.rest_0_), channel_id=1, source_target_pairs={{0,8},{4,12},{8,0},{12,4},{1,9},{5,13},{9,1},{13,5},{2,10},{6,14},... | collective-permute-start | bytes 196616 | tf_op jit(solution)/shard_map/ppermute | solution.py:20
  9.5 3.5 %local_part.1 = (f32[256,1024]{1,0:T(8,128)S(1)}, bf16[256,1024]{1,0:T(8,128)(2,1)S(1)}, f32[64,1024]{1,0:T(8,128)S(1)}) custom-call(f32[3,3,1024]{2,1,0:T(4,128)S(1)} %get-tuple-element.29.filt_ref, f32[2,8,1024]{2,1,0:T(8,128)S(1)} %get-tuple-element.30.mode_ref, ...), custom_call_target="tpu_custom_call", output_to_operand_aliasing={{0}: (2, {}), {1}: (3, {})} | custom-call | tf_op jit(solution)/shard_map/local_part/pallas_call | solution.py:192
  14.2 1.4 %collective-permute-done.2.rest_3_ = bf16[32,1024]{1,0:T(8,128)(2,1)S(1)} collective-permute-done((bf16[32,1024]{1,0:T(8,128)(2,1)S(1)}, bf16[32,1024]{1,0:T(8,128)(2,1)S(1)}, u32[]{:S(2)}, u32[]{:S(2)}) %collective-permute-start.2) | collective-permute-done | bytes 65568 | tf_op jit(solution)/shard_map/ppermute | solution.py:20
  15.6 1.5 %carry_part.1.later_any.refs_0_ = bf16[256,1024]{1,0:T(8,128)(2,1)S(1)} custom-call(s32[1]{0:T(128)} %bitcast.where_ref, f32[3,3,1024]{2,1,0:T(4,128)S(1)} %get-tuple-element.29.filt_ref, f32[2,8,1024]{2,1,0:T(8,128)S(1)} %get-tuple-element.30.mode_ref, f32[256,1024]{1,0:T(8,128)S(1)} %get-tuple-element.33.y_ref, ...), custom_call_target="tpu_custom_call" | custom-call | flops 8388608 | bytes 2097152 | tf_op jit(solution)/shard_map/carry_part/pallas_call | solution.py:297
  17.2 1.5 %collective-permute-start.9 = (bf16[256,1024]{1,0:T(8,128)(2,1)S(1)}, bf16[256,1024]{1,0:T(8,128)(2,1)}, u32[]{:S(2)}, u32[]{:S(2)}) collective-permute-start(bf16[256,1024]{1,0:T(8,128)(2,1)S(1)} %carry_part.1.later_any.refs_0_), channel_id=1, source_target_pairs={{4,8},{8,4},{5,9},{9,5},{6,10},{10,6},{7,11},{11,7},{20,24},{24,20... | collective-permute-start | bytes 1572872 | tf_op jit(solution)/shard_map/ppermute | solution.py:608
  18.6 2.7 %collective-permute-start.6 = (bf16[256,1024]{1,0:T(8,128)(2,1)S(1)}, bf16[256,1024]{1,0:T(8,128)(2,1)S(1)}, u32[]{:S(2)}, u32[]{:S(2)}) collective-permute-start(bf16[256,1024]{1,0:T(8,128)(2,1)S(1)} %carry_part.1.later_any.refs_0_), channel_id=1, source_target_pairs={{0,4},{4,0},{8,12},{12,8},{1,5},{5,1},{9,13},{13,9},{2,6},{6,2},{1... | collective-permute-start | bytes 1572872 | tf_op jit(solution)/shard_map/ppermute | solution.py:20
  21.3 10.8 %collective-permute-start.10 = (bf16[256,1024]{1,0:T(8,128)(2,1)}, bf16[256,1024]{1,0:T(8,128)(2,1)}, u32[]{:S(2)}, u32[]{:S(2)}) collective-permute-start(bf16[256,1024]{1,0:T(8,128)(2,1)} %collective-permute-done.9.refs_0_), channel_id=1, source_target_pairs={{0,4},{4,0},{8,12},{12,8},{1,5},{5,1},{9,13},{13,9},{2,6},{6,2},{1... | collective-permute-start | bytes 1572872 | tf_op jit(solution)/shard_map/ppermute | solution.py:20
  32.1 2.5 %multiply_convert_fusion.refs_0_ = bf16[1024,512]{1,0:T(8,128)(2,1)} fusion(bf16[1024,512]{1,0:T(8,128)(2,1)} %param.14, f32[1024]{0:T(1024)S(1)} %copy-done.1), kind=kLoop, calls=%fused_computation.2 | loop fusion | flops 1572864 | bytes 2101248 | tf_op jit(solution)/shard_map/convert_element_type | solution.py:496
  34.6 2.3 %collective-permute-start.3 = (bf16[1024,512]{1,0:T(8,128)(2,1)}, bf16[1024,512]{1,0:T(8,128)(2,1)}, u32[]{:S(2)}, u32[]{:S(2)}) collective-permute-start(bf16[1024,512]{1,0:T(8,128)(2,1)} %multiply_convert_fusion.refs_0_), channel_id=1, source_target_pairs={{0,1},{5,4},{10,11},{15,14},{16,17},{21,20},{26,27},{31,30}} | collective-permute-start | bytes 3145736 | tf_op jit(solution)/shard_map/ppermute | solution.py:506
  36.9 3.8 %collective-permute-start.4 = (bf16[1024,512]{1,0:T(8,128)(2,1)}, bf16[1024,512]{1,0:T(8,128)(2,1)}, u32[]{:S(2)}, u32[]{:S(2)}) collective-permute-start(bf16[1024,512]{1,0:T(8,128)(2,1)} %multiply_convert_fusion.refs_0_), channel_id=1, source_target_pairs={{0,2},{5,7},{10,8},{15,13},{16,18},{21,23},{26,24},{31,29}} | collective-permute-start | bytes 3145736 | tf_op jit(solution)/shard_map/ppermute | solution.py:506
  40.6 2.3 %collective-permute-start.5 = (bf16[1024,512]{1,0:T(8,128)(2,1)}, bf16[1024,512]{1,0:T(8,128)(2,1)}, u32[]{:S(2)}, u32[]{:S(2)}) collective-permute-start(bf16[1024,512]{1,0:T(8,128)(2,1)} %multiply_convert_fusion.refs_0_), channel_id=1, source_target_pairs={{0,3},{5,6},{10,9},{15,12},{16,19},{21,22},{26,25},{31,28}} | collective-permute-start | bytes 3145736 | tf_op jit(solution)/shard_map/ppermute | solution.py:506
  42.9 1.6 %bring.1.weight_ref = bf16[1024,1024]{1,0:T(8,128)(2,1)S(1)} custom-call(bf16[256,1024]{1,0:T(8,128)(2,1)S(1)} %carry_part.1.later_any.refs_0_, bf16[1024,1024]{1,0:T(8,128)(2,1)} %src_any.1), custom_call_target="tpu_custom_call" | custom-call | tf_op jit(solution)/shard_map/bring/pallas_call | solution.py:316
  45.2 1.5 %half_part.7 = bf16[256,1024]{1,0:T(8,128)(2,1)} custom-call(s32[1]{0:T(128)} %bitcast.14.which_ref, bf16[1024,1024]{1,0:T(8,128)(2,1)S(1)} %bring.1.weight_ref, bf16[256,1024]{1,0:T(8,128)(2,1)S(1)} %carry_part.1.later_any.refs_0_, bf16[256,1024]{1,0:T(8,128)(2,1)S(1)} %collective-permute-done.6.refs_1_), custom_call_target="tpu_custom_call" | custom-call | tf_op jit(solution)/shard_map/half_part/pallas_call | solution.py:525
  46.7 1.5 %collective-permute-start.13 = (bf16[256,1024]{1,0:T(8,128)(2,1)S(1)}, bf16[256,1024]{1,0:T(8,128)(2,1)}, u32[]{:S(2)}, u32[]{:S(2)}) collective-permute-start(bf16[256,1024]{1,0:T(8,128)(2,1)S(1)} %collective-permute-done.6.refs_1_), channel_id=1, source_target_pairs={{4,8},{8,4},{5,9},{9,5},{6,10},{10,6},{7,11},{11,7},{20,24},{24,20... | collective-permute-start | bytes 1572872 | tf_op jit(solution)/shard_map/ppermute | solution.py:609
  51.7 1.6 %half_part.9 = bf16[128,1024]{1,0:T(8,128)(2,1)S(1)} custom-call(s32[1]{0:T(128)} %bitcast.14.which_ref, bf16[1024,1024]{1,0:T(8,128)(2,1)S(1)} %bring.1.weight_ref, bf16[256,1024]{1,0:T(8,128)(2,1)} %collective-permute-done.9.refs_0_, bf16[256,1024]{1,0:T(8,128)(2,1)} %collective-permute-done.10.refs_1_), custom_call_target="tpu_custom_call" | custom-call | tf_op jit(solution)/shard_map/half_part/pallas_call | solution.py:525
  53.9 8.3 %collective-permute-start.14 = (bf16[256,1024]{1,0:T(8,128)(2,1)}, bf16[256,1024]{1,0:T(8,128)(2,1)S(1)}, u32[]{:S(2)}, u32[]{:S(2)}) collective-permute-start(bf16[256,1024]{1,0:T(8,128)(2,1)} %collective-permute-done.13.refs_0_), channel_id=1, source_target_pairs={{0,4},{4,0},{8,12},{12,8},{1,5},{5,1},{9,13},{13,9},{2,6},{6,2},{1... | collective-permute-start | bytes 1572872 | tf_op jit(solution)/shard_map/ppermute | solution.py:20
  63.4 1.6 %half_part.8 = f32[128,1024]{1,0:T(8,128)S(1)} custom-call(s32[1]{0:T(128)} %bitcast.13.which_ref, bf16[1024,1024]{1,0:T(8,128)(2,1)S(1)} %bring.1.weight_ref, bf16[256,1024]{1,0:T(8,128)(2,1)} %collective-permute-done.9.refs_0_, bf16[256,1024]{1,0:T(8,128)(2,1)} %collective-permute-done.10.refs_1_), custom_call_target="tpu_custom_call" | custom-call | tf_op jit(solution)/shard_map/half_part/pallas_call | solution.py:525
  65.2 1.5 %collective-permute-start.8 = (bf16[128,1024]{1,0:T(8,128)(2,1)S(1)}, bf16[128,1024]{1,0:T(8,128)(2,1)S(1)}, u32[]{:S(2)}, u32[]{:S(2)}) collective-permute-start(bf16[128,1024]{1,0:T(8,128)(2,1)S(1)} %bitcast.48), channel_id=1, source_target_pairs={{0,2},{1,3},{2,0},{3,1},{4,6},{5,7},{6,4},{7,5},{8,10},{9,11},{10,... | collective-permute-start | bytes 786440 | tf_op jit(solution)/shard_map/ppermute | solution.py:20
  68.0 7.0 %collective-permute-done.14.refs_1_ = bf16[256,1024]{1,0:T(8,128)(2,1)S(1)} collective-permute-done((bf16[256,1024]{1,0:T(8,128)(2,1)}, bf16[256,1024]{1,0:T(8,128)(2,1)S(1)}, u32[]{:S(2)}, u32[]{:S(2)}) %collective-permute-start.14) | collective-permute-done | bytes 524320 | tf_op jit(solution)/shard_map/ppermute | solution.py:20
  75.0 1.5 %half_part.11 = bf16[128,1024]{1,0:T(8,128)(2,1)S(1)} custom-call(s32[1]{0:T(128)} %bitcast.14.which_ref, bf16[1024,1024]{1,0:T(8,128)(2,1)S(1)} %bring.1.weight_ref, bf16[256,1024]{1,0:T(8,128)(2,1)} %collective-permute-done.13.refs_0_, bf16[256,1024]{1,0:T(8,128)(2,1)S(1)} %collective-permute-done.14.refs_1_), custom_call_target="tpu_custom_call" | custom-call | tf_op jit(solution)/shard_map/half_part/pallas_call | solution.py:525
  76.6 1.5 %collective-permute-start.12 = (bf16[64,1024]{1,0:T(8,128)(2,1)S(1)}, bf16[64,1024]{1,0:T(8,128)(2,1)S(1)}, u32[]{:S(2)}, u32[]{:S(2)}) collective-permute-start(bf16[64,1024]{1,0:T(8,128)(2,1)S(1)} %fusion), channel_id=1, source_target_pairs={{0,2},{1,3},{2,0},{3,1},{4,6},{5,7},{6,4},{7,5},{8,10},{9,11},{10,... | collective-permute-start | bytes 393224 | tf_op jit(solution)/shard_map/ppermute | solution.py:20
  78.2 1.5 %half_part.10 = f32[128,1024]{1,0:T(8,128)S(1)} custom-call(s32[1]{0:T(128)} %bitcast.13.which_ref, bf16[1024,1024]{1,0:T(8,128)(2,1)S(1)} %bring.1.weight_ref, bf16[256,1024]{1,0:T(8,128)(2,1)} %collective-permute-done.13.refs_0_, bf16[256,1024]{1,0:T(8,128)(2,1)S(1)} %collective-permute-done.14.refs_1_), custom_call_target="tpu_custom_call" | custom-call | tf_op jit(solution)/shard_map/half_part/pallas_call | solution.py:525
  80.5 2.1 %collective-permute-done.12 = bf16[64,1024]{1,0:T(8,128)(2,1)S(1)} collective-permute-done((bf16[64,1024]{1,0:T(8,128)(2,1)S(1)}, bf16[64,1024]{1,0:T(8,128)(2,1)S(1)}, u32[]{:S(2)}, u32[]{:S(2)}) %collective-permute-start.12) | collective-permute-done | bytes 131104 | tf_op jit(solution)/shard_map/ppermute | solution.py:20
  82.6 2.9 %collective-permute-done.16 = bf16[64,1024]{1,0:T(8,128)(2,1)S(1)} collective-permute-done((bf16[64,1024]{1,0:T(8,128)(2,1)S(1)}, bf16[64,1024]{1,0:T(8,128)(2,1)S(1)}, u32[]{:S(2)}, u32[]{:S(2)}) %collective-permute-start.16) | collective-permute-done | bytes 131104 | tf_op jit(solution)/shard_map/ppermute | solution.py:20
  85.5 1.5 %logit_part.1 = (f32[256,512]{1,0:T(8,128)S(1)}, f32[1,256]{1,0:T(1,128)S(1)}, f32[1,256]{1,0:T(1,128)S(1)}, bf16[72,512]{1,0:T(8,128)(2,1)S(1)}, bf16[72,512]{1...) custom-call(s32[5]{0:T(128)S(1)} %stack.32.where_ref, bf16[1024,512]{1,0:T(8,128)(2,1)S(1)} %choose.1.un_ref, ...), custom_call_target="tpu_custom_call" | custom-call | tf_op jit(solution)/shard_map/logit_part/pallas_call | solution.py:387
  87.0 1.8 %collective-permute-start.17 = (bf16[72,512]{1,0:T(8,128)(2,1)S(1)}, bf16[72,512]{1,0:T(8,128)(2,1)S(1)}, u32[]{:S(2)}, u32[]{:S(2)}) collective-permute-start(bf16[72,512]{1,0:T(8,128)(2,1)S(1)} %get-tuple-element.51), channel_id=1, source_target_pairs={{0,4},{4,0},{8,12},{12,8},{1,5},{5,1},{9,13},{13,9},{2,6},{6,2},{1... | collective-permute-start | bytes 221192 | tf_op jit(solution)/shard_map/ppermute | solution.py:20
  88.8 1.4 %collective-permute-start.18 = (bf16[72,512]{1,0:T(8,128)(2,1)S(1)}, bf16[72,512]{1,0:T(8,128)(2,1)S(1)}, u32[]{:S(2)}, u32[]{:S(2)}) collective-permute-start(bf16[72,512]{1,0:T(8,128)(2,1)S(1)} %get-tuple-element.52), channel_id=1, source_target_pairs={{0,8},{4,12},{8,0},{12,4},{1,9},{5,13},{9,1},{13,5},{2,10},{6,14},... | collective-permute-start | bytes 221192 | tf_op jit(solution)/shard_map/ppermute | solution.py:20
  91.5 5.4 %collective-permute-done.18.rest_1_ = bf16[72,512]{1,0:T(8,128)(2,1)S(1)} collective-permute-done((bf16[72,512]{1,0:T(8,128)(2,1)S(1)}, bf16[72,512]{1,0:T(8,128)(2,1)S(1)}, u32[]{:S(2)}, u32[]{:S(2)}) %collective-permute-start.18) | collective-permute-done | bytes 73760 | tf_op jit(solution)/shard_map/ppermute | solution.py:20
  97.8 1.7 %collective-permute-start.21 = (f32[2,256]{1,0:T(2,128)S(1)}, f32[2,256]{1,0:T(2,128)S(1)}, u32[]{:S(2)}, u32[]{:S(2)}) collective-permute-start(f32[2,256]{1,0:T(2,128)S(1)} %final_part.1.refs_0_), channel_id=1, source_target_pairs={{0,2},{1,3},{2,0},{3,1},{4,6},{5,7},{6,4},{7,5},{8,10},{9,11},{10,... | collective-permute-start | bytes 6152 | tf_op jit(solution)/shard_map/ppermute | solution.py:20
  99.7 1.8 %collective-permute-done.21.refs_2_ = f32[2,256]{1,0:T(2,128)S(1)} collective-permute-done((f32[2,256]{1,0:T(2,128)S(1)}, f32[2,256]{1,0:T(2,128)S(1)}, u32[]{:S(2)}, u32[]{:S(2)}) %collective-permute-start.21) | collective-permute-done | bytes 2080 | tf_op jit(solution)/shard_map/ppermute | solution.py:20
  (70 shorter events, 13.4 us)
Async XLA Ops:
  3.8 9.2 %collective-permute-start = (bf16[32,1024]{1,0:T(8,128)(2,1)S(1)}, bf16[32,1024]{1,0:T(8,128)(2,1)S(1)}, u32[]{:S(2)}, u32[]{:S(2)}) collective-permute-start(bf16[32,1024]{1,0:T(8,128)(2,1)S(1)} %get-tuple-element.42.rest_0_), channel_id=1, source_target_pairs={{0,4},{4,0},{8,12},{12,8},{1,5},{5,1},{9,13},{13,9},{2,6},{6,2},{1... | collective-permute-start | bytes 196616 | tf_op jit(solution)/shard_map/ppermute | solution.py:20
  7.0 7.3 %collective-permute-start.1 = (bf16[32,1024]{1,0:T(8,128)(2,1)S(1)}, bf16[32,1024]{1,0:T(8,128)(2,1)S(1)}, u32[]{:S(2)}, u32[]{:S(2)}) collective-permute-start(bf16[32,1024]{1,0:T(8,128)(2,1)S(1)} %get-tuple-element.42.rest_0_), channel_id=1, source_target_pairs={{0,8},{4,12},{8,0},{12,4},{1,9},{5,13},{9,1},{13,5},{2,10},{6,14},... | collective-permute-start | bytes 196616 | tf_op jit(solution)/shard_map/ppermute | solution.py:20
  9.5 6.1 %collective-permute-start.2 = (bf16[32,1024]{1,0:T(8,128)(2,1)S(1)}, bf16[32,1024]{1,0:T(8,128)(2,1)S(1)}, u32[]{:S(2)}, u32[]{:S(2)}) collective-permute-start(bf16[32,1024]{1,0:T(8,128)(2,1)S(1)} %get-tuple-element.42.rest_0_), channel_id=1, source_target_pairs={{0,12},{4,8},{8,4},{12,0},{1,13},{5,9},{9,5},{13,1},{2,14},{6,10},... | collective-permute-start | bytes 196616 | tf_op jit(solution)/shard_map/ppermute | solution.py:20
  9.5 22.6 %copy-start.1 = (f32[1024]{0:T(1024)S(1)}, f32[1024]{0:T(1024)}, u32[]{:S(2)}) copy-start(f32[1024]{0:T(1024)} %param.13) | copy-start | bytes 12292
  17.2 4.1 %collective-permute-start.9 = (bf16[256,1024]{1,0:T(8,128)(2,1)S(1)}, bf16[256,1024]{1,0:T(8,128)(2,1)}, u32[]{:S(2)}, u32[]{:S(2)}) collective-permute-start(bf16[256,1024]{1,0:T(8,128)(2,1)S(1)} %carry_part.1.later_any.refs_0_), channel_id=1, source_target_pairs={{4,8},{8,4},{5,9},{9,5},{6,10},{10,6},{7,11},{11,7},{20,24},{24,20... | collective-permute-start | bytes 1572872 | tf_op jit(solution)/shard_map/ppermute | solution.py:608
  18.6 26.5 %collective-permute-start.6 = (bf16[256,1024]{1,0:T(8,128)(2,1)S(1)}, bf16[256,1024]{1,0:T(8,128)(2,1)S(1)}, u32[]{:S(2)}, u32[]{:S(2)}) collective-permute-start(bf16[256,1024]{1,0:T(8,128)(2,1)S(1)} %carry_part.1.later_any.refs_0_), channel_id=1, source_target_pairs={{0,4},{4,0},{8,12},{12,8},{1,5},{5,1},{9,13},{13,9},{2,6},{6,2},{1... | collective-permute-start | bytes 1572872 | tf_op jit(solution)/shard_map/ppermute | solution.py:20
  21.3 25.4 %collective-permute-start.10 = (bf16[256,1024]{1,0:T(8,128)(2,1)}, bf16[256,1024]{1,0:T(8,128)(2,1)}, u32[]{:S(2)}, u32[]{:S(2)}) collective-permute-start(bf16[256,1024]{1,0:T(8,128)(2,1)} %collective-permute-done.9.refs_0_), channel_id=1, source_target_pairs={{0,4},{4,0},{8,12},{12,8},{1,5},{5,1},{9,13},{13,9},{2,6},{6,2},{1... | collective-permute-start | bytes 1572872 | tf_op jit(solution)/shard_map/ppermute | solution.py:20
  34.6 30.6 %collective-permute-start.3 = (bf16[1024,512]{1,0:T(8,128)(2,1)}, bf16[1024,512]{1,0:T(8,128)(2,1)}, u32[]{:S(2)}, u32[]{:S(2)}) collective-permute-start(bf16[1024,512]{1,0:T(8,128)(2,1)} %multiply_convert_fusion.refs_0_), channel_id=1, source_target_pairs={{0,1},{5,4},{10,11},{15,14},{16,17},{21,20},{26,27},{31,30}} | collective-permute-start | bytes 3145736 | tf_op jit(solution)/shard_map/ppermute | solution.py:506
  36.9 29.8 %collective-permute-start.4 = (bf16[1024,512]{1,0:T(8,128)(2,1)}, bf16[1024,512]{1,0:T(8,128)(2,1)}, u32[]{:S(2)}, u32[]{:S(2)}) collective-permute-start(bf16[1024,512]{1,0:T(8,128)(2,1)} %multiply_convert_fusion.refs_0_), channel_id=1, source_target_pairs={{0,2},{5,7},{10,8},{15,13},{16,18},{21,23},{26,24},{31,29}} | collective-permute-start | bytes 3145736 | tf_op jit(solution)/shard_map/ppermute | solution.py:506
  40.6 26.1 %collective-permute-start.5 = (bf16[1024,512]{1,0:T(8,128)(2,1)}, bf16[1024,512]{1,0:T(8,128)(2,1)}, u32[]{:S(2)}, u32[]{:S(2)}) collective-permute-start(bf16[1024,512]{1,0:T(8,128)(2,1)} %multiply_convert_fusion.refs_0_), channel_id=1, source_target_pairs={{0,3},{5,6},{10,9},{15,12},{16,19},{21,22},{26,25},{31,28}} | collective-permute-start | bytes 3145736 | tf_op jit(solution)/shard_map/ppermute | solution.py:506
  44.5 3.7 %copy-start.3 = (s32[256]{0:T(256)S(1)}, s32[256]{0:T(256)}, u32[]{:S(2)}) copy-start(s32[256]{0:T(256)} %param.16) | copy-start | bytes 3076
  45.2 4.7 %copy-start.2 = (s32[256]{0:T(256)S(1)}, s32[256]{0:T(256)}, u32[]{:S(2)}) copy-start(s32[256]{0:T(256)} %param.17) | copy-start | bytes 3076
  45.2 4.9 %copy-start.4 = (s32[256]{0:T(256)S(1)}, s32[256]{0:T(256)}, u32[]{:S(2)}) copy-start(s32[256]{0:T(256)} %param.15) | copy-start | bytes 3076
  46.7 7.2 %collective-permute-start.7 = (bf16[256,1024]{1,0:T(8,128)(2,1)}, bf16[256,1024]{1,0:T(8,128)(2,1)}, u32[]{:S(2)}, u32[]{:S(2)}) collective-permute-start(bf16[256,1024]{1,0:T(8,128)(2,1)} %half_part.7), channel_id=1, source_target_pairs={{0,1},{1,0},{2,3},{3,2},{4,5},{5,4},{6,7},{7,6},{8,9},{9,8},{10,11... | collective-permute-start | bytes 1572872 | tf_op jit(solution)/shard_map/ppermute | solution.py:20
  46.7 6.6 %collective-permute-start.13 = (bf16[256,1024]{1,0:T(8,128)(2,1)S(1)}, bf16[256,1024]{1,0:T(8,128)(2,1)}, u32[]{:S(2)}, u32[]{:S(2)}) collective-permute-start(bf16[256,1024]{1,0:T(8,128)(2,1)S(1)} %collective-permute-done.6.refs_1_), channel_id=1, source_target_pairs={{4,8},{8,4},{5,9},{9,5},{6,10},{10,6},{7,11},{11,7},{20,24},{24,20... | collective-permute-start | bytes 1572872 | tf_op jit(solution)/shard_map/ppermute | solution.py:609
  53.3 14.6 %collective-permute-start.11 = (bf16[128,1024]{1,0:T(8,128)(2,1)S(1)}, bf16[128,1024]{1,0:T(8,128)(2,1)S(1)}, u32[]{:S(2)}, u32[]{:S(2)}) collective-permute-start(bf16[128,1024]{1,0:T(8,128)(2,1)S(1)} %half_part.9), channel_id=1, source_target_pairs={{0,1},{1,0},{2,3},{3,2},{4,5},{5,4},{6,7},{7,6},{8,9},{9,8},{10,11... | collective-permute-start | bytes 786440 | tf_op jit(solution)/shard_map/ppermute | solution.py:20
  53.9 21.1 %collective-permute-start.14 = (bf16[256,1024]{1,0:T(8,128)(2,1)}, bf16[256,1024]{1,0:T(8,128)(2,1)S(1)}, u32[]{:S(2)}, u32[]{:S(2)}) collective-permute-start(bf16[256,1024]{1,0:T(8,128)(2,1)} %collective-permute-done.13.refs_0_), channel_id=1, source_target_pairs={{0,4},{4,0},{8,12},{12,8},{1,5},{5,1},{9,13},{13,9},{2,6},{6,2},{1... | collective-permute-start | bytes 1572872 | tf_op jit(solution)/shard_map/ppermute | solution.py:20
  65.2 12.9 %collective-permute-start.8 = (bf16[128,1024]{1,0:T(8,128)(2,1)S(1)}, bf16[128,1024]{1,0:T(8,128)(2,1)S(1)}, u32[]{:S(2)}, u32[]{:S(2)}) collective-permute-start(bf16[128,1024]{1,0:T(8,128)(2,1)S(1)} %bitcast.48), channel_id=1, source_target_pairs={{0,2},{1,3},{2,0},{3,1},{4,6},{5,7},{6,4},{7,5},{8,10},{9,11},{10,... | collective-permute-start | bytes 786440 | tf_op jit(solution)/shard_map/ppermute | solution.py:20
  76.5 3.1 %collective-permute-start.15 = (bf16[128,1024]{1,0:T(8,128)(2,1)S(1)}, bf16[128,1024]{1,0:T(8,128)(2,1)S(1)}, u32[]{:S(2)}, u32[]{:S(2)}) collective-permute-start(bf16[128,1024]{1,0:T(8,128)(2,1)S(1)} %half_part.11), channel_id=1, source_target_pairs={{0,1},{1,0},{2,3},{3,2},{4,5},{5,4},{6,7},{7,6},{8,9},{9,8},{10,11... | collective-permute-start | bytes 786440 | tf_op jit(solution)/shard_map/ppermute | solution.py:20
  76.6 6.0 %collective-permute-start.12 = (bf16[64,1024]{1,0:T(8,128)(2,1)S(1)}, bf16[64,1024]{1,0:T(8,128)(2,1)S(1)}, u32[]{:S(2)}, u32[]{:S(2)}) collective-permute-start(bf16[64,1024]{1,0:T(8,128)(2,1)S(1)} %fusion), channel_id=1, source_target_pairs={{0,2},{1,3},{2,0},{3,1},{4,6},{5,7},{6,4},{7,5},{8,10},{9,11},{10,... | collective-permute-start | bytes 393224 | tf_op jit(solution)/shard_map/ppermute | solution.py:20
  79.8 17.2 %copy-start = (s32[64,1]{1,0:T(8,128)S(1)}, s32[64,1]{1,0:T(8,128)}, u32[]{:S(2)}) copy-start(s32[64,1]{1,0:T(8,128)} %copy.21.nat_ref) | copy-start | bytes 772
  79.8 5.7 %collective-permute-start.16 = (bf16[64,1024]{1,0:T(8,128)(2,1)S(1)}, bf16[64,1024]{1,0:T(8,128)(2,1)S(1)}, u32[]{:S(2)}, u32[]{:S(2)}) collective-permute-start(bf16[64,1024]{1,0:T(8,128)(2,1)S(1)} %fusion.1), channel_id=1, source_target_pairs={{0,2},{1,3},{2,0},{3,1},{4,6},{5,7},{6,4},{7,5},{8,10},{9,11},{10,... | collective-permute-start | bytes 393224 | tf_op jit(solution)/shard_map/ppermute | solution.py:20
  87.0 4.5 %collective-permute-start.17 = (bf16[72,512]{1,0:T(8,128)(2,1)S(1)}, bf16[72,512]{1,0:T(8,128)(2,1)S(1)}, u32[]{:S(2)}, u32[]{:S(2)}) collective-permute-start(bf16[72,512]{1,0:T(8,128)(2,1)S(1)} %get-tuple-element.51), channel_id=1, source_target_pairs={{0,4},{4,0},{8,12},{12,8},{1,5},{5,1},{9,13},{13,9},{2,6},{6,2},{1... | collective-permute-start | bytes 221192 | tf_op jit(solution)/shard_map/ppermute | solution.py:20
  88.8 8.1 %collective-permute-start.18 = (bf16[72,512]{1,0:T(8,128)(2,1)S(1)}, bf16[72,512]{1,0:T(8,128)(2,1)S(1)}, u32[]{:S(2)}, u32[]{:S(2)}) collective-permute-start(bf16[72,512]{1,0:T(8,128)(2,1)S(1)} %get-tuple-element.52), channel_id=1, source_target_pairs={{0,8},{4,12},{8,0},{12,4},{1,9},{5,13},{9,1},{13,5},{2,10},{6,14},... | collective-permute-start | bytes 221192 | tf_op jit(solution)/shard_map/ppermute | solution.py:20
  90.2 6.7 %collective-permute-start.19 = (bf16[72,512]{1,0:T(8,128)(2,1)S(1)}, bf16[72,512]{1,0:T(8,128)(2,1)S(1)}, u32[]{:S(2)}, u32[]{:S(2)}) collective-permute-start(bf16[72,512]{1,0:T(8,128)(2,1)S(1)} %get-tuple-element.53), channel_id=1, source_target_pairs={{0,12},{4,8},{8,4},{12,0},{1,13},{5,9},{9,5},{13,1},{2,14},{6,10},... | collective-permute-start | bytes 221192 | tf_op jit(solution)/shard_map/ppermute | solution.py:20
  97.8 1.9 %collective-permute-start.20 = (f32[2,256]{1,0:T(2,128)S(1)}, f32[2,256]{1,0:T(2,128)S(1)}, u32[]{:S(2)}, u32[]{:S(2)}) collective-permute-start(f32[2,256]{1,0:T(2,128)S(1)} %final_part.1.refs_0_), channel_id=1, source_target_pairs={{0,1},{1,0},{2,3},{3,2},{4,5},{5,4},{6,7},{7,6},{8,9},{9,8},{10,11... | collective-permute-start | bytes 6152 | tf_op jit(solution)/shard_map/ppermute | solution.py:20
  97.8 3.7 %collective-permute-start.21 = (f32[2,256]{1,0:T(2,128)S(1)}, f32[2,256]{1,0:T(2,128)S(1)}, u32[]{:S(2)}, u32[]{:S(2)}) collective-permute-start(f32[2,256]{1,0:T(2,128)S(1)} %final_part.1.refs_0_), channel_id=1, source_target_pairs={{0,2},{1,3},{2,0},{3,1},{4,6},{5,7},{6,4},{7,5},{8,10},{9,11},{10,... | collective-permute-start | bytes 6152 | tf_op jit(solution)/shard_map/ppermute | solution.py:20
  99.5 3.0 %collective-permute-start.22 = (f32[2,256]{1,0:T(2,128)S(1)}, f32[2,256]{1,0:T(2,128)S(1)}, u32[]{:S(2)}, u32[]{:S(2)}) collective-permute-start(f32[2,256]{1,0:T(2,128)S(1)} %final_part.1.refs_0_), channel_id=1, source_target_pairs={{0,3},{1,2},{2,1},{3,0},{4,7},{5,6},{6,5},{7,4},{8,11},{9,10},{10,... | collective-permute-start | bytes 6152 | tf_op jit(solution)/shard_map/ppermute | solution.py:20
